TPU v7x, 256 devices: a whole 4x4x8 slice. The times are simulated.
256 devices in a mesh: dp: 8 (over z), context: 32 (over y, x, core).
Axes of the slice: x: 4, y: 4, z: 8, core: 2. Of those that a mesh axis runs over, the one named last changes fastest.
Arguments:
- query_in: bfloat16 [8, 16384, 1024], P('dp', 'context'), may hold values from -6 to 6
- key_in: bfloat16 [8, 16384, 1024], P('dp', 'context'), may hold values from -6 to 6
- value_in: bfloat16 [8, 16384, 1024], P('dp', 'context'), may hold values from -6 to 6
- out_grad: bfloat16 [8, 16384, 2048], P('dp', 'context'), may hold values from -6 to 6
- out_weight: bfloat16 [1024, 2048], P('context'), may hold values from -0.1875 to 0.1875
Outputs:
- output: bfloat16 [8, 16384, 2048], P('dp', 'context')
- query_grad: bfloat16 [8, 16384, 1024], P('dp', 'context')
- key_grad: bfloat16 [8, 16384, 1024], P('dp', 'context')
- value_grad: bfloat16 [8, 16384, 1024], P('dp', 'context')
- weight_grad: float32 [1024, 2048], P('context')
All inputs are finite; a program needn't handle non-finite values.
Results may differ from a plain program's by a relative error of at most 0.025.
Values may be sent and summed in bfloat16 or wider, within the bound.
No kernel may reach another device: no remote copies, remote signals or barrier semaphores. Data moves between devices by JAX's collectives and lax.ppermute only.
A program may use at most 192 MiB of HBM per device.

v0:
```python
import math

import jax
import jax.numpy as jnp
from jax import lax
from jax.sharding import PartitionSpec as P

HEADS = 8
HEAD_DIM = 128


def prefix(value, axis, join, neutral, backward):
    count, mine = (lax.axis_size(axis), lax.axis_index(axis))
    pieces = lax.all_gather(value, axis)
    if backward:
        pieces = pieces[::-1]
        mine = count - 1 - mine
    so_far = jnp.full_like(value, 0) + jnp.asarray(neutral, value.dtype)

    def turn(position, so_far):
        longer = join(so_far, pieces[position])
        return jnp.where(position < mine, longer, so_far)

    return lax.fori_loop(0, count - 1, turn, so_far)


def add_state(earlier, later):
    return earlier + later


def on_device(query_in, key_in, value_in, out_grad, out_weight):
    tok_rows = query_in.shape[1]
    head_width = query_in.shape[2]
    contexts = lax.axis_size("context")
    groups = lax.axis_size("dp")
    att_scale = 1.0 / math.sqrt(HEAD_DIM * tok_rows * contexts)
    grad_scale = 1.0 / math.sqrt(tok_rows * contexts * groups)
    split_heads = (tok_rows, HEADS, HEAD_DIM)
    queries = query_in[0].reshape(split_heads)
    keys_here = key_in[0].reshape(split_heads)
    values_here = value_in[0].reshape(split_heads)
    grad_flat = out_grad[0]
    full_weight = lax.all_gather(out_weight, "context", axis=0, tiled=True)
    head_grad = lax.dot_general(
        grad_flat, full_weight, (((1,), (1,)), ((), ())), preferred_element_type=jnp.float32
    ).astype(jnp.bfloat16)
    grad_heads = head_grad.reshape(split_heads)
    kv_block = jnp.einsum(
        "shd,she->hde", keys_here, values_here, preferred_element_type=jnp.float32
    )
    qg_block = jnp.einsum("thd,the->hde", queries, grad_heads, preferred_element_type=jnp.float32)
    blank_state = jnp.zeros_like(kv_block)
    kv_prior = prefix(kv_block, "context", add_state, blank_state, False)
    qg_later = prefix(qg_block, "context", add_state, blank_state, True)
    kv_before = kv_prior.astype(jnp.bfloat16)
    qg_after = qg_later.astype(jnp.bfloat16)
    positions = lax.broadcasted_iota(jnp.int32, (tok_rows, tok_rows), 0)
    sources = lax.broadcasted_iota(jnp.int32, (tok_rows, tok_rows), 1)
    causal = (positions >= sources)[None]
    scores = (
        jnp.einsum("thd,shd->hts", queries, keys_here, preferred_element_type=jnp.float32)
        * att_scale
    )
    scores = jnp.where(causal, scores, 0.0).astype(jnp.bfloat16)
    attended = jnp.einsum(
        "hts,shd->thd", scores, values_here, preferred_element_type=jnp.float32
    ) + att_scale * jnp.einsum(
        "thd,hde->the", queries, kv_before, preferred_element_type=jnp.float32
    )
    attended = attended.astype(jnp.bfloat16).reshape(tok_rows, head_width)
    output = jnp.dot(attended, full_weight, preferred_element_type=jnp.float32).astype(jnp.bfloat16)
    back_scores = (
        jnp.einsum("the,she->hts", grad_heads, values_here, preferred_element_type=jnp.float32)
        * att_scale
    )
    back_scores = jnp.where(causal, back_scores, 0.0).astype(jnp.bfloat16)
    query_grad = jnp.einsum(
        "hts,shd->thd", back_scores, keys_here, preferred_element_type=jnp.float32
    ) + att_scale * jnp.einsum(
        "the,hde->thd", grad_heads, kv_before, preferred_element_type=jnp.float32
    )
    key_grad = jnp.einsum(
        "hts,thd->shd", back_scores, queries, preferred_element_type=jnp.float32
    ) + att_scale * jnp.einsum(
        "she,hde->shd", values_here, qg_after, preferred_element_type=jnp.float32
    )
    value_grad = jnp.einsum(
        "hts,the->she", scores, grad_heads, preferred_element_type=jnp.float32
    ) + att_scale * jnp.einsum(
        "shd,hde->she", keys_here, qg_after, preferred_element_type=jnp.float32
    )
    query_grad = query_grad.astype(jnp.bfloat16).reshape(tok_rows, head_width)
    key_grad = key_grad.astype(jnp.bfloat16).reshape(tok_rows, head_width)
    value_grad = value_grad.astype(jnp.bfloat16).reshape(tok_rows, head_width)
    group_part = lax.psum_scatter(
        (
            lax.dot_general(
                attended, grad_flat, (((0,), (0,)), ((), ())), preferred_element_type=jnp.float32
            )
            * grad_scale
        ).astype(jnp.bfloat16),
        "context",
        scatter_dimension=0,
        tiled=True,
    )
    weight_grad = lax.psum(group_part, "dp").astype(jnp.float32)
    return (output[None], query_grad[None], key_grad[None], value_grad[None], weight_grad)


def solution(mesh):
    placed = (
        P("dp", "context", None),
        P("dp", "context", None),
        P("dp", "context", None),
        P("dp", "context", None),
        P("context", None),
    )
    return jax.shard_map(
        on_device,
        mesh=mesh,
        in_specs=placed,
        out_specs=(
            P("dp", "context", None),
            P("dp", "context", None),
            P("dp", "context", None),
            P("dp", "context", None),
            P("context", None),
        ),
        check_vma=False,
    )
```

profile of v0, /device:TPU:1, one launch (start us, length us, event | category | flops | bytes accessed | tf_op | source)
XLA Modules:
  0.0 466.4 jit_solution(10558739906381796081)
XLA Ops:
  8.9 2.9 copy.58
  11.7 2.4 copy.35
  14.1 2.5 fusion.16
  17.6 2.5 copy.57
  20.0 5.0 %select_convert_fusion.1 = bf16[8,512,512]{2,1,0:T(8,128)(2,1)} fusion(pred[512,512]{1,0:T(8,128)(4,1)S(1)} %iota_compare_fusion, bf16[512,8,128]{2,1,0:T(8,128)(2,1)} %bitcast.83, bf16[512,8,128]{2,1,0:T(8,128)(2,1)} %bitcast.78), kind=kOutput, calls=%fused_computation.4 | convolution fusion | flops 543162368 | bytes 6553600 | tf_op jit(solution)/shard_map/thd,shd->hts/dot_general | solution.py:61
  25.0 73.5 %all-gather.8.cloned.1.call-done = f32[256,128,128]{2,1,0:T(8,128)} async-done(((f32[8,128,128]{2,1,0:T(8,128)}), f32[256,128,128]{2,1,0:T(8,128)}) %all-gather.8.cloned.1.call-update) | async-done | bytes 16777232 | tf_op jit(solution)/shard_map/all_gather | solution.py:14
  98.5 38.9 %while.28 = (s32[]{:T(128)}, f32[8,128,128]{2,1,0:T(8,128)S(1)}, s32[]{:T(128)}, f32[32,8,128,128]{3,2,1,0:T(8,128)}, s32[]{:T(128)}, /*index=5*/s32[]{:T(128)}) while((s32[]{:T(128)}, f32[8,128,128]{2,1,0:T(8,128)S(1)}, s32[]{:T(128)}, f32[32,8,128,128]{3,2,1,0:T(8,128)}, s32[]{:T(128)}, /*index=5*/s32[]{:T(128)}) %tuple.81), condition=%wide.region_1.2_spmd.clone, body=%wide.region_0.1_spmd.clone.sunk | while | flops 393220 | bytes 1572957 | solution.py:24
  137.5 1.8 fusion.21
  139.3 3.8 fusion.6
  144.2 4.3 multiply_convert_fusion
  148.6 3.2 all-gather.6.cloned.1.call-done
  151.7 5.5 %fusion.7 = bf16[512,1024]{1,0:T(8,128)(2,1)} fusion(bf16[1024,2048]{1,0:T(8,128)(2,1)} %all-gather.6.cloned.1.call-done, bf16[1,512,2048]{2,1,0:T(8,128)(2,1)S(1)} %copy-done), kind=kOutput, calls=%fused_computation.17 | convolution fusion | flops 2148007936 | bytes 7340032 | tf_op jit(solution)/shard_map/dot_general | solution.py:44
  158.9 83.8 %reduce-scatter.2.cloned.1.call-done = bf16[32,2048]{1,0:T(8,128)(2,1)} async-done(((bf16[1024,2048]{1,0:T(8,128)(2,1)}), bf16[32,2048]{1,0:T(8,128)(2,1)}) %reduce-scatter.2.cloned.1.call-update) | async-done | bytes 131088 | tf_op jit(solution)/shard_map/reduce_scatter | solution.py:95
  242.9 1.7 convolution_bitcast_fusion
  247.8 2.0 fusion.28
  253.4 6.2 %fusion = bf16[1,512,2048]{2,1,0:T(8,128)(2,1)} fusion(bf16[512,1024]{0,1:T(8,128)(2,1)} %bitcast.92, bf16[1024,2048]{1,0:T(8,128)(2,1)} %all-gather.6.cloned.1.call-done), kind=kOutput, calls=%fused_computation.6 | convolution fusion | flops 2148532224 | bytes 7340032 | tf_op jit(solution)/shard_map/dot_general | solution.py:71
  259.6 53.3 %all-reduce.2.cloned.1.call-done = bf16[32,2048]{1,0:T(8,128)(2,1)} async-done(((bf16[32,2048]{1,0:T(8,128)(2,1)}), bf16[32,2048]{1,0:T(8,128)(2,1)}) %all-reduce.2.cloned.1.call-update) | async-done | bytes 131088 | tf_op jit(solution)/shard_map/psum | solution.py:106
  314.5 82.2 %all-gather.10.cloned.1.call-done = f32[256,128,128]{2,1,0:T(8,128)} async-done(((f32[8,128,128]{2,1,0:T(8,128)}), f32[256,128,128]{2,1,0:T(8,128)}) %all-gather.10.cloned.1.call-update) | async-done | bytes 16777232 | tf_op jit(solution)/shard_map/all_gather | solution.py:14
  396.7 11.6 %rev.3 = f32[32,8,128,128]{3,2,1,0:T(8,128)} reverse(f32[32,8,128,128]{3,2,1,0:T(8,128)} %bitcast.73), dimensions={0} | reverse | bytes 33554432 | tf_op jit(solution)/shard_map/rev | solution.py:16
  408.4 38.8 %while.29 = (s32[]{:T(128)}, f32[8,128,128]{2,1,0:T(8,128)S(1)}, s32[]{:T(128)}, f32[32,8,128,128]{3,2,1,0:T(8,128)}, s32[]{:T(128)}, /*index=5*/s32[]{:T(128)}) while((s32[]{:T(128)}, f32[8,128,128]{2,1,0:T(8,128)S(1)}, s32[]{:T(128)}, f32[32,8,128,128]{3,2,1,0:T(8,128)}, s32[]{:T(128)}, /*index=5*/s32[]{:T(128)}) %tuple.68), condition=%wide.region_3.4_spmd.clone, body=%wide.region_2.3_spmd.clone.sunk | while | flops 393220 | bytes 1572957 | solution.py:24
  447.7 4.1 fusion.1
  451.8 2.4 copy.52
  454.2 3.5 add_convert_fusion
  457.6 2.3 copy.53
  (104 shorter events, 90.6 us)
Async XLA Ops:
  7.2 137.0 %copy-start = (bf16[1,512,2048]{2,1,0:T(8,128)(2,1)S(1)}, bf16[1,512,2048]{2,1,0:T(8,128)(2,1)}, u32[]{:S(2)}) copy-start(bf16[1,512,2048]{2,1,0:T(8,128)(2,1)} %param.12) | copy-start | bytes 6291460
  7.2 91.3 %all-gather.8.cloned.1.call-start = ((), (), s32[]{:S(2)}) async-start(), calls=%async_computation.4 | async-start | bytes 17301504 | tf_op jit(solution)/shard_map/all_gather | solution.py:14
  8.9 8.6 %copy-start.4 = (bf16[64,8,8,128]{3,2,1,0:T(8,128)(2,1)}, bf16[64,8,8,128]{3,2,1,0:T(8,128)(2,1)S(1)}, u32[]{:S(2)}) copy-start(bf16[64,8,8,128]{3,2,1,0:T(8,128)(2,1)S(1)} %copy.59) | copy-start | bytes 3145732
  16.6 135.1 %all-gather.6.cloned.1.call-start = ((), (), s32[]{:S(2)}) async-start(), calls=%async_computation.1 | async-start | bytes 4325376 | tf_op jit(solution)/shard_map/all_gather | solution.py:43
  17.4 225.3 %reduce-scatter.2.cloned.1.call-start = ((), (), s32[]{:S(2)}) async-start(), calls=%async_computation.2 | async-start | bytes 4325376 | tf_op jit(solution)/shard_map/reduce_scatter | solution.py:95
  137.5 1.8 copy-start.5
  143.1 1.1 copy-start.9
  148.5 164.4 %all-reduce.2.cloned.1.call-start = ((), (), s32[]{:S(2)}) async-start(), calls=%async_computation.3 | async-start | bytes 262144 | tf_op jit(solution)/shard_map/psum | solution.py:106
  157.3 88.4 %copy-start.6 = (bf16[64,8,8,128]{3,2,1,0:T(8,128)(2,1)S(1)}, bf16[64,8,8,128]{3,2,1,0:T(8,128)(2,1)}, u32[]{:S(2)}) copy-start(bf16[64,8,8,128]{3,2,1,0:T(8,128)(2,1)} %copy-done.4) | copy-start | bytes 3145732
  242.7 154.0 %all-gather.10.cloned.1.call-start = ((), (), s32[]{:S(2)}) async-start(), calls=%async_computation.5 | async-start | bytes 17301504 | tf_op jit(solution)/shard_map/all_gather | solution.py:14
  245.6 2.2 copy-start.2
  247.8 2.7 copy-start.3
  247.8 2.7 copy-start.8
  408.4 39.3 %copy-start.7 = (bf16[64,8,8,128]{3,2,1,0:T(8,128)(2,1)S(1)}, bf16[64,8,8,128]{3,2,1,0:T(8,128)(2,1)}, u32[]{:S(2)}) copy-start(bf16[64,8,8,128]{3,2,1,0:T(8,128)(2,1)} %copy.57) | copy-start | bytes 3145732
  451.8 8.1 %copy-start.1 = (bf16[1,512,2048]{2,1,0:T(8,128)(2,1)S(1)}, bf16[1,512,2048]{2,1,0:T(8,128)(2,1)}, u32[]{:S(2)}) copy-start(bf16[1,512,2048]{2,1,0:T(8,128)(2,1)} %param.12) | copy-start | bytes 6291460
Sparse Core Ops, SparseCore 0:
  16.8 81.7 all-gather.7
  101.1 50.6 all-gather.5
  155.7 86.9 reduce-scatter.1
  244.9 67.9 all-reduce.1
  315.3 81.3 all-gather.9
where the time goes:
time: 470 us; the launch traced here: 466 us
  waiting for transfers between devices  297 us (63%)
  other arithmetic  78 us (17%)
  matrix products  44.3 us (9%)
  local copies, waits for them, and re-layouts  31.5 us (7%)
  between operations  14 us (3%)
    all_gather x2, waiting for transfers between devices, prefix(): pieces = lax.all_gather(value, axis)  156 us
    reduce_scatter x1, waiting for transfers between devices, on_device(): lax.psum_scatter((lax.dot_general(attended, grad_flat, (((0,), (0,)), (()...  83.8 us
    select_n x62, other arithmetic, turn(): return jnp.where(position < mine, longer, so_far)  76.3 us
    psum x1, waiting for transfers between devices, on_device(): weight_grad = lax.psum(group_part, 'dp').astype(jnp.float32)  53.3 us
    unnamed x26, local copies, waits for them, and re-layouts  14.9 us
    rev x1, local copies, waits for them, and re-layouts, prefix(): pieces = pieces[::-1]  11.6 us
  transfers between devices with their start and end apart: 5, of which 5 were waited for; matrix products, arithmetic and copies ran while one was open for 17% of the time, Pallas kernels for 0%

commit v1 on v0

v1 whole, which is shorter than its diff:
```python
import math

import jax
import jax.numpy as jnp
from jax import lax
from jax.experimental import pallas as pl
from jax.experimental.pallas import tpu as pltpu
from jax.sharding import Mesh
from jax.sharding import PartitionSpec as P

HEADS = 8
HEAD_DIM = 128
BF16 = jnp.bfloat16
F32 = jnp.float32
CONTEXT = ("y", "x", "core")
PLANE = ("y", "x")
VMEM_BYTES = 56 * 1024 * 1024


def params():
    return pltpu.CompilerParams(vmem_limit_bytes=VMEM_BYTES)


def mul(a, b, a_dim, b_dim):
    return lax.dot_general(
        a, b, (((a_dim,), (b_dim,)), ((), ())), preferred_element_type=F32
    )


def kv_kernel(k_ref, v_ref, out_ref):
    out_ref[...] = mul(k_ref[...], v_ref[...], 0, 0).astype(BF16)


def kv_states(keys, values):
    toks, width = keys.shape
    return pl.pallas_call(
        kv_kernel,
        grid=(HEADS,),
        in_specs=[pl.BlockSpec((toks, HEAD_DIM), lambda h: (0, h))] * 2,
        out_specs=pl.BlockSpec((HEAD_DIM, HEAD_DIM), lambda h: (h, 0)),
        out_shape=jax.ShapeDtypeStruct((width, HEAD_DIM), BF16),
        compiler_params=params(),
        name="kv_states",
    )(keys, values)


def strict_prefix(pieces, backward):
    count = pieces.shape[0]

    def kernel(x_ref, out_ref):
        total = jnp.zeros(x_ref.shape[1:], F32)
        for step in range(count):
            at = count - 1 - step if backward else step
            out_ref[at] = total.astype(BF16)
            total = total + x_ref[at].astype(F32)

    return pl.pallas_call(
        kernel,
        out_shape=jax.ShapeDtypeStruct(pieces.shape, BF16),
        compiler_params=params(),
        name="strict_prefix",
    )(pieces)


def scan_states(states, backward):
    count = 32
    sent = states.reshape(count, states.shape[0] // count, HEAD_DIM)
    pieces = lax.all_to_all(sent, CONTEXT, 0, 0)
    prefixes = strict_prefix(pieces, backward)
    return lax.all_to_all(prefixes, CONTEXT, 0, 0).reshape(states.shape)


def causal_mask(rows):
    later = lax.broadcasted_iota(jnp.int32, (rows, rows), 0)
    earlier = lax.broadcasted_iota(jnp.int32, (rows, rows), 1)
    return later >= earlier


def attended_states(queries, keys, values, kv_before, att_scale):
    toks, width = queries.shape
    half = toks // 2

    def kernel(q_ref, k_ref, v_ref, s_ref, out_ref):
        mask = causal_mask(half)
        q0, q1 = q_ref[:half], q_ref[half:]
        k0, k1 = k_ref[:half], k_ref[half:]
        v0, v1 = v_ref[:half], v_ref[half:]
        state = s_ref[...]
        s00 = jnp.where(mask, mul(q0, k0, 1, 1) * att_scale, 0.0).astype(BF16)
        s10 = (mul(q1, k0, 1, 1) * att_scale).astype(BF16)
        s11 = jnp.where(mask, mul(q1, k1, 1, 1) * att_scale, 0.0).astype(BF16)
        out_ref[:half] = (mul(s00, v0, 1, 0) + att_scale * mul(q0, state, 1, 0)).astype(BF16)
        out_ref[half:] = (
            mul(s10, v0, 1, 0) + mul(s11, v1, 1, 0) + att_scale * mul(q1, state, 1, 0)
        ).astype(BF16)

    column = pl.BlockSpec((toks, HEAD_DIM), lambda h: (0, h))
    return pl.pallas_call(
        kernel,
        grid=(HEADS,),
        in_specs=[column] * 3 + [pl.BlockSpec((HEAD_DIM, HEAD_DIM), lambda h: (h, 0))],
        out_specs=column,
        out_shape=jax.ShapeDtypeStruct((toks, width), BF16),
        compiler_params=params(),
        name="attended",
    )(queries, keys, values, kv_before)


def pair_weight_grad(core, attended, attended_mate, grad, grad_mate, grad_scale):
    toks, width = attended.shape
    half = grad.shape[1] // 2
    rows = 256

    def kernel(core_ref, a_ref, am_ref, g_ref, gm_ref, out_ref):
        total = mul(a_ref[...], g_ref[...], 0, 0) + mul(am_ref[...], gm_ref[...], 0, 0)
        out_ref[...] = (total * grad_scale).astype(BF16)

    column = pl.BlockSpec((toks, rows), lambda i, c: (0, i))
    return pl.pallas_call(
        kernel,
        grid_spec=pltpu.PrefetchScalarGridSpec(
            num_scalar_prefetch=1,
            grid=(width // rows,),
            in_specs=[
                column,
                column,
                pl.BlockSpec((toks, half), lambda i, c: (0, c[0])),
                pl.BlockSpec((toks, half), lambda i, c: (0, 0)),
            ],
            out_specs=pl.BlockSpec((rows, half), lambda i, c: (i, 0)),
        ),
        out_shape=jax.ShapeDtypeStruct((width, half), BF16),
        compiler_params=params(),
        name="pair_weight_grad",
    )(core, attended, attended_mate, grad, grad_mate)


def sum_plane(pieces):
    count, rows, width = pieces.shape
    keep = rows // 2
    slices = width // HEAD_DIM

    def kernel(x_ref, out_ref):
        for part in range(slices):
            lanes = slice(part * HEAD_DIM, (part + 1) * HEAD_DIM)
            total = x_ref[0, :, lanes].astype(F32)
            for at in range(1, count):
                total = total + x_ref[at, :, lanes].astype(F32)
            total = total.astype(BF16)
            out_ref[part, 0] = total[:keep]
            out_ref[part, 1] = total[keep:]

    return pl.pallas_call(
        kernel,
        out_shape=jax.ShapeDtypeStruct((slices, 2, keep, HEAD_DIM), BF16),
        compiler_params=params(),
        name="sum_plane",
    )(pieces)


def sum_groups(pieces):
    count = pieces.shape[0]

    def kernel(x_ref, out_ref):
        total = x_ref[0].astype(F32)
        for at in range(1, count):
            total = total + x_ref[at].astype(F32)
        total = total.astype(BF16)
        for at in range(count):
            out_ref[at] = total

    return pl.pallas_call(
        kernel,
        out_shape=jax.ShapeDtypeStruct(pieces.shape, BF16),
        compiler_params=params(),
        name="sum_groups",
    )(pieces)


def lay_rows(pieces):
    slices, halves, rows, lanes = pieces.shape

    def kernel(x_ref, out_ref):
        for half in range(halves):
            for part in range(slices):
                start = (half * slices + part) * lanes
                out_ref[:, start : start + lanes] = x_ref[part, half].astype(F32)

    return pl.pallas_call(
        kernel,
        out_shape=jax.ShapeDtypeStruct((rows, halves * slices * lanes), F32),
        compiler_params=params(),
        name="lay_rows",
    )(pieces)


def head_grads(grad, weight, queries):
    toks, model = grad.shape
    width = weight.shape[0]
    rows = 256

    def kernel(g_ref, w_ref, q_ref, hg_ref, qg_ref):
        head_grad = mul(g_ref[...], w_ref[...], 1, 1).astype(BF16)
        hg_ref[...] = head_grad
        for h in range(rows // HEAD_DIM):
            lanes = slice(h * HEAD_DIM, (h + 1) * HEAD_DIM)
            qg_ref[lanes, :] = mul(q_ref[:, lanes], head_grad[:, lanes], 0, 0).astype(BF16)

    column = pl.BlockSpec((toks, rows), lambda i: (0, i))
    return pl.pallas_call(
        kernel,
        grid=(width // rows,),
        in_specs=[
            pl.BlockSpec((toks, model), lambda i: (0, 0)),
            pl.BlockSpec((rows, model), lambda i: (i, 0)),
            column,
        ],
        out_specs=[column, pl.BlockSpec((rows, HEAD_DIM), lambda i: (i, 0))],
        out_shape=[
            jax.ShapeDtypeStruct((toks, width), BF16),
            jax.ShapeDtypeStruct((width, HEAD_DIM), BF16),
        ],
        compiler_params=params(),
        name="head_grads",
    )(grad, weight, queries)


def project(attended, weight):
    toks, width = attended.shape
    model = weight.shape[1]
    columns = 512

    def kernel(a_ref, w_ref, out_ref):
        out_ref[...] = mul(a_ref[...], w_ref[...], 1, 0).astype(BF16)

    return pl.pallas_call(
        kernel,
        grid=(model // columns,),
        in_specs=[
            pl.BlockSpec((toks, width), lambda i: (0, 0)),
            pl.BlockSpec((width, columns), lambda i: (0, i)),
        ],
        out_specs=pl.BlockSpec((toks, columns), lambda i: (0, i)),
        out_shape=jax.ShapeDtypeStruct((toks, model), BF16),
        compiler_params=params(),
        name="project",
    )(attended, weight)


def input_grads(queries, keys, values, head_grad, kv_before, qg_after, att_scale):
    toks, width = queries.shape
    half = toks // 2

    def kernel(q_ref, k_ref, v_ref, g_ref, kv_ref, qg_ref, dq_ref, dk_ref, dv_ref):
        mask = causal_mask(half)
        q0, q1 = q_ref[:half], q_ref[half:]
        k0, k1 = k_ref[:half], k_ref[half:]
        v0, v1 = v_ref[:half], v_ref[half:]
        g0, g1 = g_ref[:half], g_ref[half:]
        kv, qg = kv_ref[...], qg_ref[...]
        s00 = jnp.where(mask, mul(q0, k0, 1, 1) * att_scale, 0.0).astype(BF16)
        s10 = (mul(q1, k0, 1, 1) * att_scale).astype(BF16)
        s11 = jnp.where(mask, mul(q1, k1, 1, 1) * att_scale, 0.0).astype(BF16)
        dv_ref[:half] = (
            mul(s00, g0, 0, 0) + mul(s10, g1, 0, 0) + att_scale * mul(k0, qg, 1, 0)
        ).astype(BF16)
        dv_ref[half:] = (mul(s11, g1, 0, 0) + att_scale * mul(k1, qg, 1, 0)).astype(BF16)
        b00 = jnp.where(mask, mul(g0, v0, 1, 1) * att_scale, 0.0).astype(BF16)
        b10 = (mul(g1, v0, 1, 1) * att_scale).astype(BF16)
        b11 = jnp.where(mask, mul(g1, v1, 1, 1) * att_scale, 0.0).astype(BF16)
        dq_ref[:half] = (mul(b00, k0, 1, 0) + att_scale * mul(g0, kv, 1, 1)).astype(BF16)
        dq_ref[half:] = (
            mul(b10, k0, 1, 0) + mul(b11, k1, 1, 0) + att_scale * mul(g1, kv, 1, 1)
        ).astype(BF16)
        dk_ref[:half] = (
            mul(b00, q0, 0, 0) + mul(b10, q1, 0, 0) + att_scale * mul(v0, qg, 1, 1)
        ).astype(BF16)
        dk_ref[half:] = (mul(b11, q1, 0, 0) + att_scale * mul(v1, qg, 1, 1)).astype(BF16)

    column = pl.BlockSpec((toks, HEAD_DIM), lambda h: (0, h))
    state = pl.BlockSpec((HEAD_DIM, HEAD_DIM), lambda h: (h, 0))
    return pl.pallas_call(
        kernel,
        grid=(HEADS,),
        in_specs=[column] * 4 + [state] * 2,
        out_specs=[column] * 3,
        out_shape=[jax.ShapeDtypeStruct((toks, width), BF16)] * 3,
        compiler_params=params(),
        name="input_grads",
    )(queries, keys, values, head_grad, kv_before, qg_after)


def swap_cores(value):
    return lax.ppermute(value, "core", [(0, 1), (1, 0)])


def on_device(query_in, key_in, value_in, out_grad, out_weight):
    queries, keys, values, grad = query_in[0], key_in[0], value_in[0], out_grad[0]
    toks = queries.shape[0]
    length = toks * 32
    att_scale = 1.0 / math.sqrt(HEAD_DIM * length)
    grad_scale = 1.0 / math.sqrt(length * 8)
    core = lax.axis_index("core")
    half = grad.shape[1] // 2

    weight = lax.all_gather(out_weight, CONTEXT, axis=0, tiled=True)
    grad_mate = swap_cores(lax.dynamic_slice_in_dim(grad, (1 - core) * half, half, 1))

    kv_before = scan_states(kv_states(keys, values), False)
    attended = attended_states(queries, keys, values, kv_before, att_scale)
    attended_mate = swap_cores(attended)
    terms = pair_weight_grad(
        jnp.reshape(core, (1,)), attended, attended_mate, grad, grad_mate, grad_scale
    )
    terms = lax.all_to_all(terms.reshape(16, 64, half), PLANE, 0, 0)
    plane_sum = sum_plane(terms).reshape(16, 32, HEAD_DIM)
    group_terms = lax.all_to_all(plane_sum, ("z", "core"), 0, 0)
    group_sum = sum_groups(group_terms.reshape(8, 2, 32, HEAD_DIM))
    weight_grad = lay_rows(lax.all_to_all(group_sum, "z", 0, 0))

    head_grad, qg_block = head_grads(grad, weight, queries)
    qg_after = scan_states(qg_block, True)
    output = project(attended, weight)
    query_grad, key_grad, value_grad = input_grads(
        queries, keys, values, head_grad, kv_before, qg_after, att_scale
    )
    return (output[None], query_grad[None], key_grad[None], value_grad[None], weight_grad)


def solution(mesh):
    fine = Mesh(mesh.devices.reshape(8, 4, 4, 2), ("z", "y", "x", "core"))
    rows = P("z", CONTEXT, None)
    owned = P(CONTEXT, None)
    return jax.shard_map(
        on_device,
        mesh=fine,
        in_specs=(rows, rows, rows, rows, owned),
        out_specs=(rows, rows, rows, rows, owned),
        check_vma=False,
    )
```

time: 470 us -> 179 us (0.38)
  waiting for transfers between devices: 297 us -> 28.3 us
  other arithmetic: 78 us -> 0 us
  Pallas kernels: 0 us -> 53.1 us
  blocking collectives: 0 us -> 50 us
  matrix products: 44.3 us -> 0 us
  local copies, waits for them, and re-layouts: 31.5 us -> 2.49 us
  starting transfers between devices: 0.38 us -> 29.1 us
    all_gather x3 -> x1, waiting for transfers between devices: 159 us -> 0.01 us  [on_device(): weight = lax.all_gather(out_weight, CONTEXT, axis=0, tiled=True)]
    reduce_scatter x1 -> x0, waiting for transfers between devices: 83.8 us -> none  [on_device(): lax.psum_scatter((lax.dot_general(attended, grad_flat, (((0,), (0,)), (()...]
    select_n x62 -> x0, other arithmetic: 76.3 us -> none  [turn(): return jnp.where(position < mine, longer, so_far)]
    psum x1 -> x0, waiting for transfers between devices: 53.3 us -> none  [on_device(): weight_grad = lax.psum(group_part, 'dp').astype(jnp.float32)]
    pallas_call x0 -> x11, Pallas kernels: none -> 53.1 us  [the longest x1 10.7 us: input_grads(): pl.pallas_call(kernel, grid=(HEADS,), in_specs=[column] * 4 + [state] * 2...]
    all_to_all x0 -> x2, blocking collectives: none -> 50 us  [the longest x1 32.4 us: on_device(): terms = lax.all_to_all(terms.reshape(16, 64, half), PLANE, 0, 0)]
    dot_general x15 -> x0, matrix products: 44.3 us -> none  [the longest x1 6.2 us: on_device(): jnp.dot(attended, full_weight, preferred_element_type=jnp.float32)]
    all_to_all x0 -> x5, starting transfers between devices: none -> 28.4 us  [the longest x1 10 us: on_device(): group_terms = lax.all_to_all(plane_sum, ('z', 'core'), 0, 0)]
  transfers between devices with their start and end apart: 5 -> 8, of which waited for: 5 -> 6; matrix products, arithmetic and copies ran while one was open for 17% -> 0% of each run, Pallas kernels for 0% -> 24%
where the time goes in v1:
time: 179 us; the launch traced here: 177 us
  Pallas kernels  53.1 us (30%)
  blocking collectives  50 us (28%)
  starting transfers between devices  29.1 us (16%)
  waiting for transfers between devices  28.3 us (16%)
  between operations  14.1 us (8%)
  local copies, waits for them, and re-layouts  2.49 us (1%)
    all_to_all x1, blocking collectives, on_device(): terms = lax.all_to_all(terms.reshape(16, 64, half), PLANE, 0, 0)  32.4 us
    all_to_all x1, blocking collectives, scan_states(): pieces = lax.all_to_all(sent, CONTEXT, 0, 0)  17.6 us
    pallas_call x1, Pallas kernels, input_grads(): pl.pallas_call(kernel, grid=(HEADS,), in_specs=[column] * 4 + [state] * 2...  10.7 us
    all_to_all x1, starting transfers between devices, on_device(): group_terms = lax.all_to_all(plane_sum, ('z', 'core'), 0, 0)  10 us
    all_to_all x2, waiting for transfers between devices, scan_states(): return lax.all_to_all(prefixes, CONTEXT, 0, 0).reshape(states.shape)  9.84 us
    all_to_all x2, starting transfers between devices, scan_states(): return lax.all_to_all(prefixes, CONTEXT, 0, 0).reshape(states.shape)  9.12 us
    pallas_call x1, Pallas kernels, attended_states(): pl.pallas_call(kernel, grid=(HEADS,), in_specs=[column] * 3 + [pl.BlockSp...  7.52 us
    pallas_call x1, Pallas kernels, head_grads(): pl.pallas_call(kernel, grid=(width // rows,), in_specs=[pl.BlockSpec((tok...  7.49 us
  transfers between devices with their start and end apart: 8, of which 6 were waited for; matrix products, arithmetic and copies ran while one was open for 0% of the time, Pallas kernels for 24%

profile of v1, /device:TPU:1, one launch (start us, length us, event | category | flops | bytes accessed | tf_op | source)
XLA Modules:
  0.0 177.1 jit_solution(13976516364911757046)
XLA Ops:
  7.9 6.2 %kv_states.1 = bf16[1024,128]{1,0:T(8,128)(2,1)} custom-call(bf16[512,1024]{1,0:T(8,128)(2,1)} %bitcast.23, bf16[512,1024]{1,0:T(8,128)(2,1)} %bitcast.26), custom_call_target="tpu_custom_call" | custom-call | tf_op jit(solution)/shard_map/kv_states/pallas_call | solution.py:36
  14.1 17.6 %all_to_all.35.x_ref = bf16[32,32,128]{2,1,0:T(8,128)(2,1)} all-to-all(bf16[32,32,128]{2,1,0:T(8,128)(2,1)} %bitcast.34), channel_id=1, replica_groups=mesh['z'=8,'y'=4,'x'=4,'core'=2] {'y','x','core'}, dimensions={0} | all-to-all | bytes 524288 | tf_op jit(solution)/shard_map/all_to_all | solution.py:68
  31.7 1.7 strict_prefix.2
  33.4 3.8 %all-to-all-start.1 = ((bf16[32,32,128]{2,1,0:T(8,128)(2,1)}), bf16[32,32,128]{2,1,0:T(8,128)(2,1)S(1)}, u32[]{:S(2)}, u32[]{:S(2)}) async-start(bf16[32,32,128]{2,1,0:T(8,128)(2,1)} %strict_prefix.2), calls=%async_computation.1 | async-start | bytes 524288 | tf_op jit(solution)/shard_map/all_to_all | solution.py:70
  37.7 8.5 %all-to-all-done.1 = bf16[32,32,128]{2,1,0:T(8,128)(2,1)S(1)} async-done(((bf16[32,32,128]{2,1,0:T(8,128)(2,1)}), bf16[32,32,128]{2,1,0:T(8,128)(2,1)S(1)}, u32[]{:S(2)}, u32[]{:S(2)}) %all-to-all-start.1) | async-done | bytes 262176 | tf_op jit(solution)/shard_map/all_to_all | solution.py:70
  46.9 7.5 %attended.1.a_ref = bf16[512,1024]{1,0:T(8,128)(2,1)} custom-call(bf16[512,1024]{1,0:T(8,128)(2,1)} %bitcast.20, bf16[512,1024]{1,0:T(8,128)(2,1)} %bitcast.24, bf16[512,1024]{1,0:T(8,128)(2,1)} %bitcast.27, bf16[1024,128]{1,0:T(8,128)(2,1)} %bitcast.30), custom_call_target="tpu_custom_call" | custom-call | tf_op jit(solution)/shard_map/attended/pallas_call | solution.py:98
  54.6 2.7 %collective-permute-done.am_ref = bf16[512,1024]{1,0:T(8,128)(2,1)S(1)} collective-permute-done((bf16[512,1024]{1,0:T(8,128)(2,1)}, bf16[512,1024]{1,0:T(8,128)(2,1)S(1)}, u32[]{:S(2)}, u32[]{:S(2)}) %collective-permute-start) | collective-permute-done | bytes 1048608 | tf_op jit(solution)/shard_map/ppermute | solution.py:294
  58.2 6.0 %pair_weight_grad.1 = bf16[1024,1024]{1,0:T(8,128)(2,1)} custom-call(s32[1]{0:T(128)} %bitcast.12.core_ref, bf16[512,1024]{1,0:T(8,128)(2,1)} %attended.1.a_ref, bf16[512,1024]{1,0:T(8,128)(2,1)} %copy-done.5, bf16[512,2048]{1,0:T(8,128)(2,1)} %bitcast.18, bf16[512,1024]{1,0:T(8,128)(2,1)} %copy-done.4), custom_call_target="tpu_custom_call" | custom-call | tf_op jit(solution)/shard_map/pair_weight_grad/pallas_call | solution.py:119
  64.3 32.4 %all_to_all.36.x_ref = bf16[16,64,1024]{2,1,0:T(8,128)(2,1)} all-to-all(bf16[16,64,1024]{2,1,0:T(8,128)(2,1)} %bitcast.29), channel_id=1, replica_groups=mesh['z'=8,'y'=4,'x'=4,'core'=2] {'y','x'}, dimensions={0} | all-to-all | bytes 4194304 | tf_op jit(solution)/shard_map/all_to_all | solution.py:315
  96.7 2.6 %sum_plane.1 = bf16[8,2,32,128]{3,2,1,0:T(8,128)(2,1)} custom-call(bf16[16,64,1024]{2,1,0:T(8,128)(2,1)} %all_to_all.36.x_ref), custom_call_target="tpu_custom_call" | custom-call | tf_op jit(solution)/shard_map/sum_plane/pallas_call | solution.py:153
  99.3 10.0 %all-to-all-start.5 = ((bf16[16,32,128]{2,1,0:T(8,128)(2,1)}), bf16[16,32,128]{2,1,0:T(8,128)(2,1)S(1)}, u32[]{:S(2)}, u32[]{:S(2)}) async-start(bf16[16,32,128]{2,1,0:T(8,128)(2,1)} %bitcast.35), calls=%async_computation.5 | async-start | bytes 262144 | tf_op jit(solution)/shard_map/all_to_all | solution.py:317
  109.3 7.5 %head_grads.1 = (bf16[512,1024]{1,0:T(8,128)(2,1)}, bf16[1024,128]{1,0:T(8,128)(2,1)}) custom-call(bf16[512,2048]{1,0:T(8,128)(2,1)} %bitcast.19, bf16[1024,2048]{1,0:T(8,128)(2,1)} %all-gather.2.cloned.1.call-done.w_ref, bf16[512,1024]{1,0:T(8,128)(2,1)} %bitcast.21), custom_call_target="tpu_custom_call" | custom-call | tf_op jit(solution)/shard_map/head_grads/pallas_call | solution.py:210
  116.8 1.7 all-to-all-done.5
  118.5 3.7 %all-to-all-start.2 = ((bf16[32,32,128]{2,1,0:T(8,128)(2,1)}), bf16[32,32,128]{2,1,0:T(8,128)(2,1)S(1)}, u32[]{:S(2)}, u32[]{:S(2)}) async-start(bf16[32,32,128]{2,1,0:T(8,128)(2,1)} %bitcast.37), calls=%async_computation.2 | async-start | bytes 524288 | tf_op jit(solution)/shard_map/all_to_all | solution.py:68
  122.2 1.6 sum_groups.1
  123.7 7.0 %all-to-all-done.2.x_ref = bf16[32,32,128]{2,1,0:T(8,128)(2,1)S(1)} async-done(((bf16[32,32,128]{2,1,0:T(8,128)(2,1)}), bf16[32,32,128]{2,1,0:T(8,128)(2,1)S(1)}, u32[]{:S(2)}, u32[]{:S(2)}) %all-to-all-start.2) | async-done | bytes 262176 | tf_op jit(solution)/shard_map/all_to_all | solution.py:68
  130.7 5.6 %all-to-all-start.6 = ((bf16[8,2,32,128]{3,2,1,0:T(8,128)(2,1)}), bf16[8,2,32,128]{3,2,1,0:T(8,128)(2,1)S(1)}, u32[]{:S(2)}, u32[]{:S(2)}) async-start(bf16[8,2,32,128]{3,2,1,0:T(8,128)(2,1)} %sum_groups.1), calls=%async_computation.6 | async-start | bytes 262144 | tf_op jit(solution)/shard_map/all_to_all | solution.py:319
  136.3 1.7 strict_prefix.3
  138.0 6.5 %all-to-all-done.6.x_ref = bf16[8,2,32,128]{3,2,1,0:T(8,128)(2,1)S(1)} async-done(((bf16[8,2,32,128]{3,2,1,0:T(8,128)(2,1)}), bf16[8,2,32,128]{3,2,1,0:T(8,128)(2,1)S(1)}, u32[]{:S(2)}, u32[]{:S(2)}) %all-to-all-start.6) | async-done | bytes 131104 | tf_op jit(solution)/shard_map/all_to_all | solution.py:319
  144.5 5.4 %all-to-all-start.3 = ((bf16[32,32,128]{2,1,0:T(8,128)(2,1)}), bf16[32,32,128]{2,1,0:T(8,128)(2,1)S(1)}, u32[]{:S(2)}, u32[]{:S(2)}) async-start(bf16[32,32,128]{2,1,0:T(8,128)(2,1)} %strict_prefix.3), calls=%async_computation.3 | async-start | bytes 524288 | tf_op jit(solution)/shard_map/all_to_all | solution.py:70
  149.9 1.6 lay_rows.1
  151.5 6.0 %project.1 = bf16[512,2048]{1,0:T(8,128)(2,1)} custom-call(bf16[512,1024]{1,0:T(8,128)(2,1)} %attended.1.a_ref, bf16[1024,2048]{1,0:T(8,128)(2,1)} %all-gather.2.cloned.1.call-done.w_ref), custom_call_target="tpu_custom_call" | custom-call | tf_op jit(solution)/shard_map/project/pallas_call | solution.py:236
  157.5 1.4 all-to-all-done.3
  159.6 10.7 %input_grads.1 = (bf16[512,1024]{1,0:T(8,128)(2,1)}, bf16[512,1024]{1,0:T(8,128)(2,1)}, bf16[512,1024]{1,0:T(8,128)(2,1)}) custom-call(bf16[512,1024]{1,0:T(8,128)(2,1)} %bitcast.22, bf16[512,1024]{1,0:T(8,128)(2,1)} %bitcast.25, bf16[512,1024]{1,0:T(8,128)(2,1)} %bitcast.28, bf16[512,1024]{1,0:T(8,128)(2,1)} %get-tuple-element.10.g_ref, ...), custom_call_target="tpu_custom_call" | custom-call | tf_op jit(solution)/shard_map/input_grads/pallas_call | solution.py:282
  (23 shorter events, 3.9 us)
Async XLA Ops:
  7.2 30.0 %copy-start = (bf16[1,512,2048]{2,1,0:T(8,128)(2,1)S(1)}, bf16[1,512,2048]{2,1,0:T(8,128)(2,1)}, u32[]{:S(2)}) copy-start(bf16[1,512,2048]{2,1,0:T(8,128)(2,1)} %param.8) | copy-start | bytes 6291460
  7.2 102.2 %all-gather.2.cloned.1.call-start = ((), (), s32[]{:S(2)}) async-start(), calls=%async_computation.7 | async-start | bytes 4325376 | tf_op jit(solution)/shard_map/all_gather | solution.py:306
  33.4 12.8 %all-to-all-start.1 = ((bf16[32,32,128]{2,1,0:T(8,128)(2,1)}), bf16[32,32,128]{2,1,0:T(8,128)(2,1)S(1)}, u32[]{:S(2)}, u32[]{:S(2)}) async-start(bf16[32,32,128]{2,1,0:T(8,128)(2,1)} %strict_prefix.2), calls=%async_computation.1 | async-start | bytes 524288 | tf_op jit(solution)/shard_map/all_to_all | solution.py:70
  37.3 17.3 %collective-permute-start.1 = (bf16[512,1024]{1,0:T(8,128)(2,1)S(1)}, bf16[512,1024]{1,0:T(8,128)(2,1)S(1)}, u32[]{:S(2)}, u32[]{:S(2)}) collective-permute-start(bf16[512,1024]{1,0:T(8,128)(2,1)S(1)} %dynamic-slice_bitcast_fusion), channel_id=1, source_target_pairs={{0,1},{1,0},{2,3},{3,2},{4,5},{5,4},{6,7},{7,6},{8,9},{9,8},{10,11... | collective-permute-start | bytes 3145736 | tf_op jit(solution)/shard_map/ppermute | solution.py:294
  46.2 0.7 copy-start.1
  54.4 2.9 %collective-permute-start = (bf16[512,1024]{1,0:T(8,128)(2,1)}, bf16[512,1024]{1,0:T(8,128)(2,1)S(1)}, u32[]{:S(2)}, u32[]{:S(2)}) collective-permute-start(bf16[512,1024]{1,0:T(8,128)(2,1)} %attended.1.a_ref), channel_id=1, source_target_pairs={{0,1},{1,0},{2,3},{3,2},{4,5},{5,4},{6,7},{7,6},{8,9},{9,8},{10,11... | collective-permute-start | bytes 3145736 | tf_op jit(solution)/shard_map/ppermute | solution.py:294
  54.6 2.7 %copy-start.4 = (bf16[512,1024]{1,0:T(8,128)(2,1)}, bf16[512,1024]{1,0:T(8,128)(2,1)S(1)}, u32[]{:S(2)}) copy-start(bf16[512,1024]{1,0:T(8,128)(2,1)S(1)} %collective-permute-done.1.gm_ref) | copy-start | bytes 3145732
  57.3 1.0 copy-start.5
  99.3 19.2 %all-to-all-start.5 = ((bf16[16,32,128]{2,1,0:T(8,128)(2,1)}), bf16[16,32,128]{2,1,0:T(8,128)(2,1)S(1)}, u32[]{:S(2)}, u32[]{:S(2)}) async-start(bf16[16,32,128]{2,1,0:T(8,128)(2,1)} %bitcast.35), calls=%async_computation.5 | async-start | bytes 262144 | tf_op jit(solution)/shard_map/all_to_all | solution.py:317
  118.5 3.7 %copy-start.7 = (bf16[16,32,128]{2,1,0:T(8,128)(2,1)}, bf16[16,32,128]{2,1,0:T(8,128)(2,1)S(1)}, u32[]{:S(2)}) copy-start(bf16[16,32,128]{2,1,0:T(8,128)(2,1)S(1)} %all-to-all-done.5) | copy-start | bytes 393220
  118.5 12.2 %all-to-all-start.2 = ((bf16[32,32,128]{2,1,0:T(8,128)(2,1)}), bf16[32,32,128]{2,1,0:T(8,128)(2,1)S(1)}, u32[]{:S(2)}, u32[]{:S(2)}) async-start(bf16[32,32,128]{2,1,0:T(8,128)(2,1)} %bitcast.37), calls=%async_computation.2 | async-start | bytes 524288 | tf_op jit(solution)/shard_map/all_to_all | solution.py:68
  130.7 5.6 %copy-start.3 = (bf16[32,32,128]{2,1,0:T(8,128)(2,1)}, bf16[32,32,128]{2,1,0:T(8,128)(2,1)S(1)}, u32[]{:S(2)}) copy-start(bf16[32,32,128]{2,1,0:T(8,128)(2,1)S(1)} %all-to-all-done.2.x_ref) | copy-start | bytes 786436
  130.7 13.8 %all-to-all-start.6 = ((bf16[8,2,32,128]{3,2,1,0:T(8,128)(2,1)}), bf16[8,2,32,128]{3,2,1,0:T(8,128)(2,1)S(1)}, u32[]{:S(2)}, u32[]{:S(2)}) async-start(bf16[8,2,32,128]{3,2,1,0:T(8,128)(2,1)} %sum_groups.1), calls=%async_computation.6 | async-start | bytes 262144 | tf_op jit(solution)/shard_map/all_to_all | solution.py:319
  144.5 5.4 %copy-start.6 = (bf16[8,2,32,128]{3,2,1,0:T(8,128)(2,1)}, bf16[8,2,32,128]{3,2,1,0:T(8,128)(2,1)S(1)}, u32[]{:S(2)}) copy-start(bf16[8,2,32,128]{3,2,1,0:T(8,128)(2,1)S(1)} %all-to-all-done.6.x_ref) | copy-start | bytes 393220
  144.5 14.4 %all-to-all-start.3 = ((bf16[32,32,128]{2,1,0:T(8,128)(2,1)}), bf16[32,32,128]{2,1,0:T(8,128)(2,1)S(1)}, u32[]{:S(2)}, u32[]{:S(2)}) async-start(bf16[32,32,128]{2,1,0:T(8,128)(2,1)} %strict_prefix.3), calls=%async_computation.3 | async-start | bytes 524288 | tf_op jit(solution)/shard_map/all_to_all | solution.py:70
  158.9 0.7 copy-start.2
Sparse Core Ops, SparseCore 0:
  10.6 55.3 all-gather.1

commit v2 on v1

--- a/solution.py
+++ b/solution.py
@@ -14,11 +14,15 @@
 F32 = jnp.float32
 CONTEXT = ("y", "x", "core")
 PLANE = ("y", "x")
-VMEM_BYTES = 56 * 1024 * 1024
-
-
-def params():
-    return pltpu.CompilerParams(vmem_limit_bytes=VMEM_BYTES)
+WHOLE = pl.BlockSpec(memory_space=pltpu.VMEM)
+
+
+def params(mib=16):
+    return pltpu.CompilerParams(vmem_limit_bytes=mib * 1024 * 1024)
+
+
+def in_hbm(value):
+    return pltpu.with_memory_space_constraint(value, pltpu.HBM)
 
 
 def mul(a, b, a_dim, b_dim):
@@ -27,21 +31,24 @@
     )
 
 
-def kv_kernel(k_ref, v_ref, out_ref):
-    out_ref[...] = mul(k_ref[...], v_ref[...], 0, 0).astype(BF16)
-
-
 def kv_states(keys, values):
     toks, width = keys.shape
-    return pl.pallas_call(
-        kv_kernel,
-        grid=(HEADS,),
-        in_specs=[pl.BlockSpec((toks, HEAD_DIM), lambda h: (0, h))] * 2,
-        out_specs=pl.BlockSpec((HEAD_DIM, HEAD_DIM), lambda h: (h, 0)),
-        out_shape=jax.ShapeDtypeStruct((width, HEAD_DIM), BF16),
+    wide = 2 * HEAD_DIM
+
+    def kernel(k_ref, v_ref, out_ref):
+        both = mul(k_ref[...], v_ref[...], 0, 0)
+        out_ref[:HEAD_DIM] = both[:HEAD_DIM, :HEAD_DIM].astype(BF16)
+        out_ref[HEAD_DIM:] = both[HEAD_DIM:, HEAD_DIM:].astype(BF16)
+
+    return pl.pallas_call(
+        kernel,
+        grid=(width // wide,),
+        in_specs=[pl.BlockSpec((toks, wide), lambda h: (0, h))] * 2,
+        out_specs=pl.BlockSpec((wide, HEAD_DIM), lambda h: (h, 0)),
+        out_shape=pltpu.HBM((width, HEAD_DIM), BF16),
         compiler_params=params(),
         name="kv_states",
-    )(keys, values)
+    )(in_hbm(keys), in_hbm(values))
 
 
 def strict_prefix(pieces, backward):
@@ -57,17 +64,11 @@
     return pl.pallas_call(
         kernel,
         out_shape=jax.ShapeDtypeStruct(pieces.shape, BF16),
-        compiler_params=params(),
+        in_specs=[WHOLE],
+        out_specs=WHOLE,
+        compiler_params=params(4),
         name="strict_prefix",
     )(pieces)
-
-
-def scan_states(states, backward):
-    count = 32
-    sent = states.reshape(count, states.shape[0] // count, HEAD_DIM)
-    pieces = lax.all_to_all(sent, CONTEXT, 0, 0)
-    prefixes = strict_prefix(pieces, backward)
-    return lax.all_to_all(prefixes, CONTEXT, 0, 0).reshape(states.shape)
 
 
 def causal_mask(rows):
@@ -100,10 +101,10 @@
         grid=(HEADS,),
         in_specs=[column] * 3 + [pl.BlockSpec((HEAD_DIM, HEAD_DIM), lambda h: (h, 0))],
         out_specs=column,
-        out_shape=jax.ShapeDtypeStruct((toks, width), BF16),
+        out_shape=pltpu.HBM((toks, width), BF16),
         compiler_params=params(),
         name="attended",
-    )(queries, keys, values, kv_before)
+    )(in_hbm(queries), in_hbm(keys), in_hbm(values), kv_before)
 
 
 def pair_weight_grad(core, attended, attended_mate, grad, grad_mate, grad_scale):
@@ -129,10 +130,10 @@
             ],
             out_specs=pl.BlockSpec((rows, half), lambda i, c: (i, 0)),
         ),
-        out_shape=jax.ShapeDtypeStruct((width, half), BF16),
+        out_shape=pltpu.HBM((width, half), BF16),
         compiler_params=params(),
         name="pair_weight_grad",
-    )(core, attended, attended_mate, grad, grad_mate)
+    )(core, in_hbm(attended), attended_mate, in_hbm(grad), grad_mate)
 
 
 def sum_plane(pieces):
@@ -152,8 +153,10 @@
 
     return pl.pallas_call(
         kernel,
-        out_shape=jax.ShapeDtypeStruct((slices, 2, keep, HEAD_DIM), BF16),
-        compiler_params=params(),
+        out_shape=pltpu.HBM((slices, 2, keep, HEAD_DIM), BF16),
+        in_specs=[WHOLE],
+        out_specs=WHOLE,
+        compiler_params=params(4),
         name="sum_plane",
     )(pieces)
 
@@ -171,8 +174,10 @@
 
     return pl.pallas_call(
         kernel,
-        out_shape=jax.ShapeDtypeStruct(pieces.shape, BF16),
-        compiler_params=params(),
+        out_shape=pltpu.HBM(pieces.shape, BF16),
+        in_specs=[WHOLE],
+        out_specs=WHOLE,
+        compiler_params=params(4),
         name="sum_groups",
     )(pieces)
 
@@ -189,40 +194,113 @@
     return pl.pallas_call(
         kernel,
         out_shape=jax.ShapeDtypeStruct((rows, halves * slices * lanes), F32),
-        compiler_params=params(),
+        in_specs=[WHOLE],
+        out_specs=WHOLE,
+        compiler_params=params(4),
         name="lay_rows",
     )(pieces)
 
 
-def head_grads(grad, weight, queries):
+def head_grads(core, grad, weight, queries):
     toks, model = grad.shape
     width = weight.shape[0]
     rows = 256
-
-    def kernel(g_ref, w_ref, q_ref, hg_ref, qg_ref):
+    steps = width // rows // 2
+
+    def kernel(core_ref, g_ref, w_ref, q_ref, hg_ref, mine_ref, give_ref):
         head_grad = mul(g_ref[...], w_ref[...], 1, 1).astype(BF16)
         hg_ref[...] = head_grad
+        step = pl.program_id(0)
         for h in range(rows // HEAD_DIM):
             lanes = slice(h * HEAD_DIM, (h + 1) * HEAD_DIM)
-            qg_ref[lanes, :] = mul(q_ref[:, lanes], head_grad[:, lanes], 0, 0).astype(BF16)
-
-    column = pl.BlockSpec((toks, rows), lambda i: (0, i))
-    return pl.pallas_call(
-        kernel,
-        grid=(width // rows,),
-        in_specs=[
-            pl.BlockSpec((toks, model), lambda i: (0, 0)),
-            pl.BlockSpec((rows, model), lambda i: (i, 0)),
-            column,
+            state = mul(q_ref[:, lanes], head_grad[:, lanes], 0, 0).astype(BF16)
+            at = pl.ds(pl.multiple_of((step % steps) * rows + h * HEAD_DIM, HEAD_DIM), HEAD_DIM)
+
+            @pl.when(step // steps == core_ref[0])
+            def _():
+                mine_ref[at, :] = state
+
+            @pl.when(step // steps != core_ref[0])
+            def _():
+                give_ref[at, :] = state
+
+    column = pl.BlockSpec((toks, rows), lambda i, c: (0, i))
+    return pl.pallas_call(
+        kernel,
+        grid_spec=pltpu.PrefetchScalarGridSpec(
+            num_scalar_prefetch=1,
+            grid=(width // rows,),
+            in_specs=[
+                pl.BlockSpec((toks, model), lambda i, c: (0, 0)),
+                pl.BlockSpec((rows, model), lambda i, c: (i, 0)),
+                column,
+            ],
+            out_specs=[column, WHOLE, WHOLE],
+        ),
+        out_shape=[
+            pltpu.HBM((toks, width), BF16),
+            jax.ShapeDtypeStruct((width // 2, HEAD_DIM), BF16),
+            jax.ShapeDtypeStruct((width // 2, HEAD_DIM), BF16),
         ],
-        out_specs=[column, pl.BlockSpec((rows, HEAD_DIM), lambda i: (i, 0))],
-        out_shape=[
-            jax.ShapeDtypeStruct((toks, width), BF16),
-            jax.ShapeDtypeStruct((width, HEAD_DIM), BF16),
-        ],
-        compiler_params=params(),
+        compiler_params=params(20),
         name="head_grads",
-    )(grad, weight, queries)
+    )(core, in_hbm(grad), in_hbm(weight), in_hbm(queries))
+
+
+def chip_states(mine, mate):
+    def kernel(a_ref, b_ref, out_ref):
+        out_ref[...] = (a_ref[...].astype(F32) + b_ref[...].astype(F32)).astype(BF16)
+
+    return pl.pallas_call(
+        kernel,
+        in_specs=[WHOLE] * 2,
+        out_specs=WHOLE,
+        out_shape=jax.ShapeDtypeStruct(mine.shape, BF16),
+        compiler_params=params(4),
+        name="chip_states",
+    )(mine, mate)
+
+
+def row_states(places, chip, pieces):
+    def kernel(place_ref, chip_ref, a_ref, b_ref, c_ref, row_ref, later_ref):
+        x = place_ref[1]
+        total, later = chip_ref[...].astype(F32), jnp.zeros(chip_ref.shape, F32)
+        for by, ref in enumerate((a_ref, b_ref, c_ref), 1):
+            piece = ref[...].astype(F32)
+            total = total + piece
+            later = later + jnp.where(x + by < 4, piece, 0.0)
+        row_ref[...] = total.astype(BF16)
+        later_ref[...] = later
+
+    return pl.pallas_call(
+        kernel,
+        in_specs=[pl.BlockSpec(memory_space=pltpu.SMEM)] + [WHOLE] * 4,
+        out_specs=[WHOLE] * 2,
+        out_shape=[jax.ShapeDtypeStruct(chip.shape, BF16), jax.ShapeDtypeStruct(chip.shape, F32)],
+        compiler_params=params(4),
+        name="row_states",
+    )(places, chip, *pieces)
+
+
+def final_states(places, later_here, mine, mate, pieces):
+    def kernel(place_ref, later_ref, mine_ref, mate_ref, a_ref, b_ref, c_ref, keep_ref, give_ref):
+        y, core = place_ref[0], place_ref[2]
+        later = later_ref[...]
+        for by, ref in enumerate((a_ref, b_ref, c_ref), 1):
+            later = later + jnp.where(y + by < 4, ref[...].astype(F32), 0.0)
+        second = jnp.where(core == 0, mate_ref[...], mine_ref[...]).astype(F32)
+        first_core, second_core = later + second, later
+        keep_ref[...] = jnp.where(core == 0, first_core, second_core).astype(BF16)
+        give_ref[...] = jnp.where(core == 0, second_core, first_core).astype(BF16)
+
+    return pl.pallas_call(
+        kernel,
+        in_specs=[pl.BlockSpec(memory_space=pltpu.SMEM)] + [WHOLE] * 6,
+        out_specs=[WHOLE] * 2,
+        out_shape=[jax.ShapeDtypeStruct(mine.shape, BF16)] * 2,
+        compiler_params=params(4),
+        name="final_states",
+    )(places, later_here, mine, mate, *pieces)
 
 
 def project(attended, weight):
@@ -241,30 +319,28 @@
             pl.BlockSpec((width, columns), lambda i: (0, i)),
         ],
         out_specs=pl.BlockSpec((toks, columns), lambda i: (0, i)),
-        out_shape=jax.ShapeDtypeStruct((toks, model), BF16),
+        out_shape=pltpu.HBM((toks, model), BF16),
         compiler_params=params(),
         name="project",
-    )(attended, weight)
-
-
-def input_grads(queries, keys, values, head_grad, kv_before, qg_after, att_scale):
+    )(in_hbm(attended), in_hbm(weight))
+
+
+def local_grads(queries, keys, values, head_grad, kv_before, att_scale):
     toks, width = queries.shape
     half = toks // 2
 
-    def kernel(q_ref, k_ref, v_ref, g_ref, kv_ref, qg_ref, dq_ref, dk_ref, dv_ref):
+    def kernel(q_ref, k_ref, v_ref, g_ref, kv_ref, dq_ref, dk_ref, dv_ref):
         mask = causal_mask(half)
         q0, q1 = q_ref[:half], q_ref[half:]
         k0, k1 = k_ref[:half], k_ref[half:]
         v0, v1 = v_ref[:half], v_ref[half:]
         g0, g1 = g_ref[:half], g_ref[half:]
-        kv, qg = kv_ref[...], qg_ref[...]
+        kv = kv_ref[...]
         s00 = jnp.where(mask, mul(q0, k0, 1, 1) * att_scale, 0.0).astype(BF16)
         s10 = (mul(q1, k0, 1, 1) * att_scale).astype(BF16)
         s11 = jnp.where(mask, mul(q1, k1, 1, 1) * att_scale, 0.0).astype(BF16)
-        dv_ref[:half] = (
-            mul(s00, g0, 0, 0) + mul(s10, g1, 0, 0) + att_scale * mul(k0, qg, 1, 0)
-        ).astype(BF16)
-        dv_ref[half:] = (mul(s11, g1, 0, 0) + att_scale * mul(k1, qg, 1, 0)).astype(BF16)
+        dv_ref[:half] = mul(s00, g0, 0, 0) + mul(s10, g1, 0, 0)
+        dv_ref[half:] = mul(s11, g1, 0, 0)
         b00 = jnp.where(mask, mul(g0, v0, 1, 1) * att_scale, 0.0).astype(BF16)
         b10 = (mul(g1, v0, 1, 1) * att_scale).astype(BF16)
         b11 = jnp.where(mask, mul(g1, v1, 1, 1) * att_scale, 0.0).astype(BF16)
@@ -272,26 +348,67 @@
         dq_ref[half:] = (
             mul(b10, k0, 1, 0) + mul(b11, k1, 1, 0) + att_scale * mul(g1, kv, 1, 1)
         ).astype(BF16)
-        dk_ref[:half] = (
-            mul(b00, q0, 0, 0) + mul(b10, q1, 0, 0) + att_scale * mul(v0, qg, 1, 1)
-        ).astype(BF16)
-        dk_ref[half:] = (mul(b11, q1, 0, 0) + att_scale * mul(v1, qg, 1, 1)).astype(BF16)
+        dk_ref[:half] = mul(b00, q0, 0, 0) + mul(b10, q1, 0, 0)
+        dk_ref[half:] = mul(b11, q1, 0, 0)
 
     column = pl.BlockSpec((toks, HEAD_DIM), lambda h: (0, h))
     state = pl.BlockSpec((HEAD_DIM, HEAD_DIM), lambda h: (h, 0))
     return pl.pallas_call(
         kernel,
         grid=(HEADS,),
-        in_specs=[column] * 4 + [state] * 2,
+        in_specs=[column] * 4 + [state],
         out_specs=[column] * 3,
-        out_shape=[jax.ShapeDtypeStruct((toks, width), BF16)] * 3,
-        compiler_params=params(),
-        name="input_grads",
-    )(queries, keys, values, head_grad, kv_before, qg_after)
+        out_shape=[
+            pltpu.HBM((toks, width), BF16),
+            pltpu.HBM((toks, width), F32),
+            pltpu.HBM((toks, width), F32),
+        ],
+        compiler_params=params(12),
+        name="local_grads",
+    )(in_hbm(queries), in_hbm(keys), in_hbm(values), in_hbm(head_grad), kv_before)
+
+
+def later_grads(core, keys, values, key_local, value_local, keep, back, att_scale):
+    toks, width = keys.shape
+    rows = keep.shape[0]
+    heads = rows // HEAD_DIM
+
+    def kernel(core_ref, k_ref, v_ref, dkl_ref, dvl_ref, keep_ref, back_ref, dk_ref, dv_ref):
+        mine = pl.program_id(0) // heads == core_ref[0]
+        qg = jnp.where(mine, keep_ref[...], back_ref[...])
+        dk_ref[...] = (dkl_ref[...] + att_scale * mul(v_ref[...], qg, 1, 1)).astype(BF16)
+        dv_ref[...] = (dvl_ref[...] + att_scale * mul(k_ref[...], qg, 1, 0)).astype(BF16)
+
+    column = pl.BlockSpec((toks, HEAD_DIM), lambda h, c: (0, h))
+    state = pl.BlockSpec((HEAD_DIM, HEAD_DIM), lambda h, c: (h % heads, 0))
+    return pl.pallas_call(
+        kernel,
+        grid_spec=pltpu.PrefetchScalarGridSpec(
+            num_scalar_prefetch=1,
+            grid=(HEADS,),
+            in_specs=[column] * 4 + [state] * 2,
+            out_specs=[column] * 2,
+        ),
+        out_shape=[pltpu.HBM((toks, width), BF16)] * 2,
+        compiler_params=params(12),
+        name="later_grads",
+    )(core, in_hbm(keys), in_hbm(values), in_hbm(key_local), in_hbm(value_local), keep, back)
 
 
 def swap_cores(value):
     return lax.ppermute(value, "core", [(0, 1), (1, 0)])
+
+
+def turn(value, axis, count, by):
+    return lax.ppermute(value, axis, [(at, (at + by) % count) for at in range(count)])
+
+
+def after(value, *others):
+    return lax.optimization_barrier((value,) + others)[0]
+
+
+def around(value, axis, sign):
+    return [turn(value, axis, 4, sign * by) for by in (1, 2, 3)]
 
 
 def on_device(query_in, key_in, value_in, out_grad, out_weight):
@@ -302,27 +419,42 @@
     grad_scale = 1.0 / math.sqrt(length * 8)
     core = lax.axis_index("core")
     half = grad.shape[1] // 2
-
+    places = jnp.stack([lax.axis_index("y"), lax.axis_index("x"), core])
+    core_place = jnp.reshape(core, (1,))
+
+    grad_mate = swap_cores(lax.dynamic_slice_in_dim(grad, (1 - core) * half, half, 1))
     weight = lax.all_gather(out_weight, CONTEXT, axis=0, tiled=True)
-    grad_mate = swap_cores(lax.dynamic_slice_in_dim(grad, (1 - core) * half, half, 1))
-
-    kv_before = scan_states(kv_states(keys, values), False)
+    kv_block = kv_states(keys, values)
+
+    pieces = lax.all_to_all(kv_block.reshape(32, -1, HEAD_DIM), CONTEXT, 0, 0)
+    prefixes = strict_prefix(after(pieces, grad_mate), False)
+    kv_before = lax.all_to_all(prefixes, CONTEXT, 0, 0).reshape(kv_block.shape)
+
     attended = attended_states(queries, keys, values, kv_before, att_scale)
     attended_mate = swap_cores(attended)
-    terms = pair_weight_grad(
-        jnp.reshape(core, (1,)), attended, attended_mate, grad, grad_mate, grad_scale
+    terms = pair_weight_grad(core_place, attended, attended_mate, grad, grad_mate, grad_scale)
+    plane_terms = lax.all_to_all(terms.reshape(16, 64, half), PLANE, 0, 0)
+
+    head_grad, mine, give = head_grads(core_place, after(grad, terms), weight, queries)
+    mate = swap_cores(give)
+    chip = chip_states(mine, mate)
+    row_state, later_here = row_states(places, chip, around(chip, "x", -1))
+    query_grad, key_local, value_local = local_grads(
+        queries, keys, values, head_grad, kv_before, att_scale
     )
-    terms = lax.all_to_all(terms.reshape(16, 64, half), PLANE, 0, 0)
-    plane_sum = sum_plane(terms).reshape(16, 32, HEAD_DIM)
-    group_terms = lax.all_to_all(plane_sum, ("z", "core"), 0, 0)
+    output = project(attended, weight)
+
+    plane_terms = after(plane_terms, key_local, output, row_state)
+    plane_sum = sum_plane(plane_terms)
+    group_terms = lax.all_to_all(plane_sum.reshape(16, 32, HEAD_DIM), ("z", "core"), 0, 0)
+    row_pieces = around(after(row_state, plane_sum), "y", -1)
+    keep, give = final_states(places, later_here, mine, mate, row_pieces)
+    back = swap_cores(give)
     group_sum = sum_groups(group_terms.reshape(8, 2, 32, HEAD_DIM))
     weight_grad = lay_rows(lax.all_to_all(group_sum, "z", 0, 0))
 
-    head_grad, qg_block = head_grads(grad, weight, queries)
-    qg_after = scan_states(qg_block, True)
-    output = project(attended, weight)
-    query_grad, key_grad, value_grad = input_grads(
-        queries, keys, values, head_grad, kv_before, qg_after, att_scale
+    key_grad, value_grad = later_grads(
+        core_place, keys, values, key_local, value_local, after(keep, group_sum), back, att_scale
     )
     return (output[None], query_grad[None], key_grad[None], value_grad[None], weight_grad)
 

time: 179 us -> 143 us (0.80)
  blocking collectives: 50 us -> 26.9 us
  waiting for transfers between devices: 28.3 us -> 17.1 us
    all_to_all x2, blocking collectives: 50 us -> 26.9 us  [the longest x1 14.4 us: on_device(): pieces = lax.all_to_all(kv_block.reshape(32, -1, HEAD_DIM), CONTEXT, 0, 0)]
    all_to_all x4 -> x2, waiting for transfers between devices: 18.5 us -> 4.6 us  [the longest x1 4.6 us: on_device(): lax.all_to_all(plane_sum.reshape(16, 32, HEAD_DIM), ('z', 'core'), 0, 0)]
    all_to_all x4 -> x2, starting transfers between devices: 22.8 us -> 12.9 us  [the longest x1 9.14 us: on_device(): lax.all_to_all(plane_sum.reshape(16, 32, HEAD_DIM), ('z', 'core'), 0, 0)]
    ppermute x0 -> x6, starting transfers between devices: none -> 8.62 us  [turn(): lax.ppermute(value, axis, [(at, (at + by) % count) for at in range(count)])]
    all_to_all x1, waiting for transfers between devices: 6.49 us -> 0.01 us  [on_device(): weight_grad = lay_rows(lax.all_to_all(group_sum, 'z', 0, 0))]
    ppermute x0 -> x6, waiting for transfers between devices: none -> 4.47 us  [turn(): lax.ppermute(value, axis, [(at, (at + by) % count) for at in range(count)])]
    pallas_call x5 -> x9, Pallas kernels: 28.5 us -> 33 us  [the longest x1 10.6 us: local_grads(): pl.pallas_call(kernel, grid=(HEADS,), in_specs=[column] * 4 + [state], ou...]
    ppermute x2 -> x4, starting transfers between devices: 0.63 us -> 4.5 us  [swap_cores(): return lax.ppermute(value, 'core', [(0, 1), (1, 0)])]
  transfers between devices with their start and end apart: 8 -> 14, of which waited for: 6 -> 6; matrix products, arithmetic and copies ran while one was open for 0% -> 1% of each run, Pallas kernels for 24% -> 36%
where the time goes in v2:
time: 143 us; the launch traced here: 142 us
  Pallas kernels  52.8 us (37%)
  starting transfers between devices  29.4 us (21%)
  blocking collectives  26.9 us (19%)
  waiting for transfers between devices  17.1 us (12%)
  between operations  14.1 us (10%)
    all_to_all x1, blocking collectives, on_device(): pieces = lax.all_to_all(kv_block.reshape(32, -1, HEAD_DIM), CONTEXT, 0, 0)  14.4 us
    all_to_all x1, blocking collectives, on_device(): kv_before = lax.all_to_all(prefixes, CONTEXT, 0, 0).reshape(kv_block.shape)  12.5 us
    pallas_call x1, Pallas kernels, local_grads(): pl.pallas_call(kernel, grid=(HEADS,), in_specs=[column] * 4 + [state], ou...  10.6 us
    all_to_all x1, starting transfers between devices, on_device(): lax.all_to_all(plane_sum.reshape(16, 32, HEAD_DIM), ('z', 'core'), 0, 0)  9.14 us
    ppermute x6, starting transfers between devices, turn(): lax.ppermute(value, axis, [(at, (at + by) % count) for at in range(count)])  8.62 us
    pallas_call x1, Pallas kernels, head_grads(): pl.pallas_call(kernel, grid_spec=pltpu.PrefetchScalarGridSpec(num_scalar_...  8.11 us
    pallas_call x1, Pallas kernels, attended_states(): pl.pallas_call(kernel, grid=(HEADS,), in_specs=[column] * 3 + [pl.BlockSp...  7.45 us
    pallas_call x1, Pallas kernels, later_grads(): pl.pallas_call(kernel, grid_spec=pltpu.PrefetchScalarGridSpec(num_scalar_...  7.26 us
  transfers between devices with their start and end apart: 14, of which 6 were waited for; matrix products, arithmetic and copies ran while one was open for 1% of the time, Pallas kernels for 36%

profile of v2, /device:TPU:1, one launch (start us, length us, event | category | flops | bytes accessed | tf_op | source)
XLA Modules:
  0.0 141.7 jit_solution(11241979449103301826)
XLA Ops:
  7.9 1.3 dynamic-slice_bitcast_fusion
  9.2 3.3 %collective-permute-start = (bf16[512,1024]{1,0:T(8,128)(2,1)S(1)}, bf16[512,1024]{1,0:T(8,128)(2,1)S(1)}, u32[]{:S(2)}, u32[]{:S(2)}) collective-permute-start(bf16[512,1024]{1,0:T(8,128)(2,1)S(1)} %dynamic-slice_bitcast_fusion), channel_id=1, source_target_pairs={{0,1},{1,0},{2,3},{3,2},{4,5},{5,4},{6,7},{7,6},{8,9},{9,8},{10,11... | collective-permute-start | bytes 3145736 | tf_op jit(solution)/shard_map/ppermute | solution.py:399
  12.5 3.9 %kv_states.1 = bf16[1024,128]{1,0:T(8,128)(2,1)} custom-call(bf16[512,1024]{1,0:T(8,128)(2,1)} %bitcast.21, bf16[512,1024]{1,0:T(8,128)(2,1)} %bitcast.25), custom_call_target="tpu_custom_call" | custom-call | tf_op jit(solution)/shard_map/kv_states/pallas_call | solution.py:43
  16.4 14.4 %all_to_all.25.x_ref = bf16[32,32,128]{2,1,0:T(8,128)(2,1)S(1)} all-to-all(bf16[32,32,128]{2,1,0:T(8,128)(2,1)} %bitcast.36), channel_id=1, replica_groups=mesh['z'=8,'y'=4,'x'=4,'core'=2] {'y','x','core'}, dimensions={0} | all-to-all | bytes 524288 | tf_op jit(solution)/shard_map/all_to_all | solution.py:429
  30.9 12.5 %all_to_all.26 = bf16[32,32,128]{2,1,0:T(8,128)(2,1)S(1)} all-to-all(bf16[32,32,128]{2,1,0:T(8,128)(2,1)S(1)} %strict_prefix.1), channel_id=1, replica_groups=mesh['z'=8,'y'=4,'x'=4,'core'=2] {'y','x','core'}, dimensions={0} | all-to-all | bytes 524288 | tf_op jit(solution)/shard_map/all_to_all | solution.py:431
  43.4 7.4 %attended.1.a_ref = bf16[512,1024]{1,0:T(8,128)(2,1)} custom-call(bf16[512,1024]{1,0:T(8,128)(2,1)} %bitcast.31, bf16[512,1024]{1,0:T(8,128)(2,1)} %bitcast.22, bf16[512,1024]{1,0:T(8,128)(2,1)} %bitcast.26, bf16[1024,128]{1,0:T(8,128)(2,1)S(1)} %bitcast.18), custom_call_target="tpu_custom_call" | custom-call | tf_op jit(solution)/shard_map/attended/pallas_call | solution.py:99
  51.6 2.5 %collective-permute-done.1.am_ref = bf16[512,1024]{1,0:T(8,128)(2,1)S(1)} collective-permute-done((bf16[512,1024]{1,0:T(8,128)(2,1)}, bf16[512,1024]{1,0:T(8,128)(2,1)S(1)}, u32[]{:S(2)}, u32[]{:S(2)}) %collective-permute-start.1) | collective-permute-done | bytes 1048608 | tf_op jit(solution)/shard_map/ppermute | solution.py:399
  54.1 5.6 %pair_weight_grad.1 = bf16[1024,1024]{1,0:T(8,128)(2,1)} custom-call(s32[1]{0:T(128)} %bitcast.7.core_ref, bf16[512,1024]{1,0:T(8,128)(2,1)} %attended.1.a_ref, bf16[512,1024]{1,0:T(8,128)(2,1)S(1)} %collective-permute-done.1.am_ref, bf16[512,2048]{1,0:T(8,128)(2,1)} %bitcast.29, bf16[512,1024]{1,0:T(8,128)(2,1)S(1)} %collective-permute-done.gm_ref), custom_call_target="tpu_custom_call" | custom-call | tf_op jit(solution)/shard_map/pair_weight_grad/pallas_call | solution.py:120
  59.6 3.7 %all-to-all-start.2 = ((bf16[16,64,1024]{2,1,0:T(8,128)(2,1)}), bf16[16,64,1024]{2,1,0:T(8,128)(2,1)S(1)}, u32[]{:S(2)}, u32[]{:S(2)}) async-start(bf16[16,64,1024]{2,1,0:T(8,128)(2,1)} %bitcast.34), calls=%async_computation.2 | async-start | bytes 4194304 | tf_op jit(solution)/shard_map/all_to_all | solution.py:436
  63.4 2.5 %all-gather.2.cloned.1.call-done.w_ref = bf16[1024,2048]{1,0:T(8,128)(2,1)} async-done(((bf16[32,2048]{1,0:T(8,128)(2,1)}), bf16[1024,2048]{1,0:T(8,128)(2,1)}) %all-gather.2.cloned.1.call-update) | async-done | bytes 4194320 | tf_op jit(solution)/shard_map/all_gather | solution.py:426
  65.9 8.1 %head_grads.1 = (bf16[512,1024]{1,0:T(8,128)(2,1)}, bf16[512,128]{1,0:T(8,128)(2,1)S(1)}, bf16[512,128]{1,0:T(8,128)(2,1)S(1)}) custom-call(s32[1]{0:T(128)} %bitcast.7.core_ref, bf16[512,2048]{1,0:T(8,128)(2,1)} %bitcast.30, bf16[1024,2048]{1,0:T(8,128)(2,1)} %all-gather.2.cloned.1.call-done.w_ref, bf16[512,1024]{1,0:T(8,128)(2,1)} %bitcast.32), custom_call_target="tpu_custom_call" | custom-call | tf_op jit(solution)/shard_map/head_grads/pallas_call | solution.py:228
  74.3 1.1 collective-permute-done.2.b_ref.mate_ref
  76.4 2.3 %collective-permute-start.4 = (bf16[512,128]{1,0:T(8,128)(2,1)S(1)}, bf16[512,128]{1,0:T(8,128)(2,1)S(1)}, u32[]{:S(2)}, u32[]{:S(2)}) collective-permute-start(bf16[512,128]{1,0:T(8,128)(2,1)S(1)} %chip_states.1.chip_ref), channel_id=1, source_target_pairs={{0,4},{2,6},{4,0},{6,2},{1,5},{3,7},{5,1},{7,3},{8,12},{10,14},{12... | collective-permute-start | bytes 393224 | tf_op jit(solution)/shard_map/ppermute | solution.py:403
  79.5 10.6 %local_grads.1 = (bf16[512,1024]{1,0:T(8,128)(2,1)}, f32[512,1024]{1,0:T(8,128)}, f32[512,1024]{1,0:T(8,128)}) custom-call(bf16[512,1024]{1,0:T(8,128)(2,1)} %bitcast.33, bf16[512,1024]{1,0:T(8,128)(2,1)} %bitcast.23, bf16[512,1024]{1,0:T(8,128)(2,1)} %bitcast.27, bf16[512,1024]{1,0:T(8,128)(2,1)} %get-tuple-element.24.g_ref, bf16[1024,128]{1,0:T(8,128)(2,1)S(1)} %bitcast.19), custom_call_target="tpu_custom_call" | custom-call | tf_op jit(solution)/shard_map/local_grads/pallas_call | solution.py:356
  90.2 6.0 %project.1 = bf16[512,2048]{1,0:T(8,128)(2,1)} custom-call(bf16[512,1024]{1,0:T(8,128)(2,1)} %attended.1.a_ref, bf16[1024,2048]{1,0:T(8,128)(2,1)} %all-gather.2.cloned.1.call-done.w_ref), custom_call_target="tpu_custom_call" | custom-call | tf_op jit(solution)/shard_map/project/pallas_call | solution.py:314
  96.2 4.5 %collective-permute-done.4.b_ref = bf16[512,128]{1,0:T(8,128)(2,1)S(1)} collective-permute-done((bf16[512,128]{1,0:T(8,128)(2,1)S(1)}, bf16[512,128]{1,0:T(8,128)(2,1)S(1)}, u32[]{:S(2)}, u32[]{:S(2)}) %collective-permute-start.4) | collective-permute-done | bytes 131104 | tf_op jit(solution)/shard_map/ppermute | solution.py:403
  101.3 1.0 sum_plane.1
  102.3 9.1 %all-to-all-start.3 = ((bf16[16,32,128]{2,1,0:T(8,128)(2,1)}), bf16[16,32,128]{2,1,0:T(8,128)(2,1)S(1)}, u32[]{:S(2)}, u32[]{:S(2)}) async-start(bf16[16,32,128]{2,1,0:T(8,128)(2,1)} %bitcast.37), calls=%async_computation.3 | async-start | bytes 262144 | tf_op jit(solution)/shard_map/all_to_all | solution.py:449
  111.6 2.5 %collective-permute-start.7 = (bf16[512,128]{1,0:T(8,128)(2,1)S(1)}, bf16[512,128]{1,0:T(8,128)(2,1)S(1)}, u32[]{:S(2)}, u32[]{:S(2)}) collective-permute-start(bf16[512,128]{1,0:T(8,128)(2,1)S(1)} %get-tuple-element.33), channel_id=1, source_target_pairs={{0,16},{8,24},{16,0},{24,8},{1,17},{9,25},{17,1},{25,9},{2,18},{10... | collective-permute-start | bytes 393224 | tf_op jit(solution)/shard_map/ppermute | solution.py:403
  114.0 2.0 %collective-permute-start.6 = (bf16[512,128]{1,0:T(8,128)(2,1)S(1)}, bf16[512,128]{1,0:T(8,128)(2,1)S(1)}, u32[]{:S(2)}, u32[]{:S(2)}) collective-permute-start(bf16[512,128]{1,0:T(8,128)(2,1)S(1)} %get-tuple-element.33), channel_id=1, source_target_pairs={{0,24},{8,0},{16,8},{24,16},{1,25},{9,1},{17,9},{25,17},{2,26},{10... | collective-permute-start | bytes 393224 | tf_op jit(solution)/shard_map/ppermute | solution.py:403
  116.0 4.6 %all-to-all-done.3 = bf16[16,32,128]{2,1,0:T(8,128)(2,1)S(1)} async-done(((bf16[16,32,128]{2,1,0:T(8,128)(2,1)}), bf16[16,32,128]{2,1,0:T(8,128)(2,1)S(1)}, u32[]{:S(2)}, u32[]{:S(2)}) %all-to-all-start.3) | async-done | bytes 131104 | tf_op jit(solution)/shard_map/all_to_all | solution.py:449
  121.3 3.4 %all-to-all-start.4 = ((bf16[8,2,32,128]{3,2,1,0:T(8,128)(2,1)}), bf16[8,2,32,128]{3,2,1,0:T(8,128)(2,1)S(1)}, u32[]{:S(2)}, u32[]{:S(2)}) async-start(bf16[8,2,32,128]{3,2,1,0:T(8,128)(2,1)} %sum_groups.1), calls=%async_computation.4 | async-start | bytes 262144 | tf_op jit(solution)/shard_map/all_to_all | solution.py:454
  125.6 1.3 collective-permute-done.9.back_ref
  126.8 7.3 %later_grads.1 = (bf16[512,1024]{1,0:T(8,128)(2,1)}, bf16[512,1024]{1,0:T(8,128)(2,1)}) custom-call(s32[1]{0:T(128)} %bitcast.7.core_ref, bf16[512,1024]{1,0:T(8,128)(2,1)} %bitcast.24, bf16[512,1024]{1,0:T(8,128)(2,1)} %bitcast.28, f32[512,1024]{1,0:T(8,128)} %get-tuple-element.26.dkl_ref, f32[512,1024]{1,0:T(8,128)} %get-tuple-element.27.dvl_ref, ...), custom_call_target="tpu_custom_call" | custom-call | tf_op jit(solution)/shard_map/later_grads/pallas_call | solution.py:384
  (23 shorter events, 6.7 us)
Async XLA Ops:
  7.2 58.7 %all-gather.2.cloned.1.call-start = ((), (), s32[]{:S(2)}) async-start(), calls=%async_computation.5 | async-start | bytes 4325376 | tf_op jit(solution)/shard_map/all_gather | solution.py:426
  9.2 21.6 %collective-permute-start = (bf16[512,1024]{1,0:T(8,128)(2,1)S(1)}, bf16[512,1024]{1,0:T(8,128)(2,1)S(1)}, u32[]{:S(2)}, u32[]{:S(2)}) collective-permute-start(bf16[512,1024]{1,0:T(8,128)(2,1)S(1)} %dynamic-slice_bitcast_fusion), channel_id=1, source_target_pairs={{0,1},{1,0},{2,3},{3,2},{4,5},{5,4},{6,7},{7,6},{8,9},{9,8},{10,11... | collective-permute-start | bytes 3145736 | tf_op jit(solution)/shard_map/ppermute | solution.py:399
  50.8 3.2 %collective-permute-start.1 = (bf16[512,1024]{1,0:T(8,128)(2,1)}, bf16[512,1024]{1,0:T(8,128)(2,1)S(1)}, u32[]{:S(2)}, u32[]{:S(2)}) collective-permute-start(bf16[512,1024]{1,0:T(8,128)(2,1)} %attended.1.a_ref), channel_id=1, source_target_pairs={{0,1},{1,0},{2,3},{3,2},{4,5},{5,4},{6,7},{7,6},{8,9},{9,8},{10,11... | collective-permute-start | bytes 3145736 | tf_op jit(solution)/shard_map/ppermute | solution.py:399
  59.6 41.7 %all-to-all-start.2 = ((bf16[16,64,1024]{2,1,0:T(8,128)(2,1)}), bf16[16,64,1024]{2,1,0:T(8,128)(2,1)S(1)}, u32[]{:S(2)}, u32[]{:S(2)}) async-start(bf16[16,64,1024]{2,1,0:T(8,128)(2,1)} %bitcast.34), calls=%async_computation.2 | async-start | bytes 4194304 | tf_op jit(solution)/shard_map/all_to_all | solution.py:436
  74.0 1.3 collective-permute-start.2
  75.4 20.8 %collective-permute-start.5 = (bf16[512,128]{1,0:T(8,128)(2,1)S(1)}, bf16[512,128]{1,0:T(8,128)(2,1)S(1)}, u32[]{:S(2)}, u32[]{:S(2)}) collective-permute-start(bf16[512,128]{1,0:T(8,128)(2,1)S(1)} %chip_states.1.chip_ref), channel_id=1, source_target_pairs={{0,2},{2,4},{4,6},{6,0},{1,3},{3,5},{5,7},{7,1},{8,10},{10,12},{12... | collective-permute-start | bytes 393224 | tf_op jit(solution)/shard_map/ppermute | solution.py:403
  76.4 24.2 %collective-permute-start.4 = (bf16[512,128]{1,0:T(8,128)(2,1)S(1)}, bf16[512,128]{1,0:T(8,128)(2,1)S(1)}, u32[]{:S(2)}, u32[]{:S(2)}) collective-permute-start(bf16[512,128]{1,0:T(8,128)(2,1)S(1)} %chip_states.1.chip_ref), channel_id=1, source_target_pairs={{0,4},{2,6},{4,0},{6,2},{1,5},{3,7},{5,1},{7,3},{8,12},{10,14},{12... | collective-permute-start | bytes 393224 | tf_op jit(solution)/shard_map/ppermute | solution.py:403
  78.7 21.9 %collective-permute-start.3 = (bf16[512,128]{1,0:T(8,128)(2,1)S(1)}, bf16[512,128]{1,0:T(8,128)(2,1)S(1)}, u32[]{:S(2)}, u32[]{:S(2)}) collective-permute-start(bf16[512,128]{1,0:T(8,128)(2,1)S(1)} %chip_states.1.chip_ref), channel_id=1, source_target_pairs={{0,6},{2,0},{4,2},{6,4},{1,7},{3,1},{5,3},{7,5},{8,14},{10,8},{12,... | collective-permute-start | bytes 393224 | tf_op jit(solution)/shard_map/ppermute | solution.py:403
  102.3 18.3 %all-to-all-start.3 = ((bf16[16,32,128]{2,1,0:T(8,128)(2,1)}), bf16[16,32,128]{2,1,0:T(8,128)(2,1)S(1)}, u32[]{:S(2)}, u32[]{:S(2)}) async-start(bf16[16,32,128]{2,1,0:T(8,128)(2,1)} %bitcast.37), calls=%async_computation.3 | async-start | bytes 262144 | tf_op jit(solution)/shard_map/all_to_all | solution.py:449
  111.5 13.2 %collective-permute-start.8 = (bf16[512,128]{1,0:T(8,128)(2,1)S(1)}, bf16[512,128]{1,0:T(8,128)(2,1)S(1)}, u32[]{:S(2)}, u32[]{:S(2)}) collective-permute-start(bf16[512,128]{1,0:T(8,128)(2,1)S(1)} %get-tuple-element.33), channel_id=1, source_target_pairs={{0,8},{8,16},{16,24},{24,0},{1,9},{9,17},{17,25},{25,1},{2,10},{10... | collective-permute-start | bytes 393224 | tf_op jit(solution)/shard_map/ppermute | solution.py:403
  111.6 13.1 %collective-permute-start.7 = (bf16[512,128]{1,0:T(8,128)(2,1)S(1)}, bf16[512,128]{1,0:T(8,128)(2,1)S(1)}, u32[]{:S(2)}, u32[]{:S(2)}) collective-permute-start(bf16[512,128]{1,0:T(8,128)(2,1)S(1)} %get-tuple-element.33), channel_id=1, source_target_pairs={{0,16},{8,24},{16,0},{24,8},{1,17},{9,25},{17,1},{25,9},{2,18},{10... | collective-permute-start | bytes 393224 | tf_op jit(solution)/shard_map/ppermute | solution.py:403
  114.0 10.7 %collective-permute-start.6 = (bf16[512,128]{1,0:T(8,128)(2,1)S(1)}, bf16[512,128]{1,0:T(8,128)(2,1)S(1)}, u32[]{:S(2)}, u32[]{:S(2)}) collective-permute-start(bf16[512,128]{1,0:T(8,128)(2,1)S(1)} %get-tuple-element.33), channel_id=1, source_target_pairs={{0,24},{8,0},{16,8},{24,16},{1,25},{9,1},{17,9},{25,17},{2,26},{10... | collective-permute-start | bytes 393224 | tf_op jit(solution)/shard_map/ppermute | solution.py:403
  121.3 12.8 %all-to-all-start.4 = ((bf16[8,2,32,128]{3,2,1,0:T(8,128)(2,1)}), bf16[8,2,32,128]{3,2,1,0:T(8,128)(2,1)S(1)}, u32[]{:S(2)}, u32[]{:S(2)}) async-start(bf16[8,2,32,128]{3,2,1,0:T(8,128)(2,1)} %sum_groups.1), calls=%async_computation.4 | async-start | bytes 262144 | tf_op jit(solution)/shard_map/all_to_all | solution.py:454
  125.4 1.4 %collective-permute-start.9 = (bf16[512,128]{1,0:T(8,128)(2,1)S(1)}, bf16[512,128]{1,0:T(8,128)(2,1)S(1)}, u32[]{:S(2)}, u32[]{:S(2)}) collective-permute-start(bf16[512,128]{1,0:T(8,128)(2,1)S(1)} %get-tuple-element.36), channel_id=1, source_target_pairs={{0,1},{1,0},{2,3},{3,2},{4,5},{5,4},{6,7},{7,6},{8,9},{9,8},{10,11... | collective-permute-start | bytes 393224 | tf_op jit(solution)/shard_map/ppermute | solution.py:399
Sparse Core Ops, SparseCore 0:
  10.6 55.3 all-gather.1

commit v3 on v2

v3 whole, which is shorter than its diff:
```python
import math

import jax
import jax.numpy as jnp
from jax import lax
from jax.experimental import pallas as pl
from jax.experimental.pallas import tpu as pltpu
from jax.sharding import Mesh
from jax.sharding import PartitionSpec as P

HEADS = 8
HEAD_DIM = 128
BF16 = jnp.bfloat16
F32 = jnp.float32
CONTEXT = ("y", "x", "core")
PLANE = ("y", "x")
WHOLE = pl.BlockSpec(memory_space=pltpu.VMEM)
SCALARS = pl.BlockSpec(memory_space=pltpu.SMEM)
IN_PLACE = pl.BlockSpec(memory_space=pl.ANY)


def params(mib=16):
    return pltpu.CompilerParams(vmem_limit_bytes=mib * 1024 * 1024)


def in_hbm(value):
    return pltpu.with_memory_space_constraint(value, pltpu.HBM)


def mul(a, b, a_dim, b_dim):
    return lax.dot_general(
        a, b, (((a_dim,), (b_dim,)), ((), ())), preferred_element_type=F32
    )


def kv_states(keys, values):
    toks, width = keys.shape
    wide = 2 * HEAD_DIM
    parts = 2
    span = width // parts

    def kernel(k_ref, v_ref, out_ref, k_buf, v_buf, sems):
        copies = []
        for part in range(parts):
            lanes = slice(part * span, (part + 1) * span)
            for at, (src, dst) in enumerate(((k_ref, k_buf), (v_ref, v_buf))):
                copy = pltpu.make_async_copy(src.at[:, lanes], dst.at[:, lanes], sems.at[at, part])
                copy.start()
                copies.append(copy)
        for part in range(parts):
            copies[2 * part].wait()
            copies[2 * part + 1].wait()
            for start in range(part * span, (part + 1) * span, wide):
                both = mul(k_buf[:, start : start + wide], v_buf[:, start : start + wide], 0, 0)
                middle = start + HEAD_DIM
                out_ref[start:middle] = both[:HEAD_DIM, :HEAD_DIM].astype(BF16)
                out_ref[middle : start + wide] = both[HEAD_DIM:, HEAD_DIM:].astype(BF16)

    return pl.pallas_call(
        kernel,
        in_specs=[IN_PLACE] * 2,
        out_specs=WHOLE,
        out_shape=jax.ShapeDtypeStruct((width, HEAD_DIM), BF16),
        scratch_shapes=[pltpu.VMEM((toks, width), BF16)] * 2
        + [pltpu.SemaphoreType.DMA((2, parts))],
        compiler_params=params(8),
        name="kv_states",
    )(in_hbm(keys), in_hbm(values))


def strict_prefix(pieces, backward):
    count = pieces.shape[0]

    def kernel(x_ref, out_ref):
        total = jnp.zeros(x_ref.shape[1:], F32)
        for step in range(count):
            at = count - 1 - step if backward else step
            out_ref[at] = total.astype(BF16)
            total = total + x_ref[at].astype(F32)

    return pl.pallas_call(
        kernel,
        out_shape=jax.ShapeDtypeStruct(pieces.shape, BF16),
        in_specs=[WHOLE],
        out_specs=WHOLE,
        compiler_params=params(4),
        name="strict_prefix",
    )(pieces)


def causal_mask(rows):
    later = lax.broadcasted_iota(jnp.int32, (rows, rows), 0)
    earlier = lax.broadcasted_iota(jnp.int32, (rows, rows), 1)
    return later >= earlier


def head_lanes(head):
    return slice(head * HEAD_DIM, (head + 1) * HEAD_DIM)


def attended_states(queries, keys, values, kv_before, att_scale):
    toks, width = queries.shape
    half = toks // 2

    def kernel(q_ref, k_ref, v_ref, s_ref, out_ref):
        mask = causal_mask(half)
        for head in range(HEADS):
            lanes = head_lanes(head)
            q0, q1 = q_ref[:half, lanes], q_ref[half:, lanes]
            k0, k1 = k_ref[:half, lanes], k_ref[half:, lanes]
            v0, v1 = v_ref[:half, lanes], v_ref[half:, lanes]
            state = s_ref[lanes, :]
            s00 = jnp.where(mask, mul(q0, k0, 1, 1) * att_scale, 0.0).astype(BF16)
            s10 = (mul(q1, k0, 1, 1) * att_scale).astype(BF16)
            s11 = jnp.where(mask, mul(q1, k1, 1, 1) * att_scale, 0.0).astype(BF16)
            out_ref[:half, lanes] = (
                mul(s00, v0, 1, 0) + att_scale * mul(q0, state, 1, 0)
            ).astype(BF16)
            out_ref[half:, lanes] = (
                mul(s10, v0, 1, 0) + mul(s11, v1, 1, 0) + att_scale * mul(q1, state, 1, 0)
            ).astype(BF16)

    return pl.pallas_call(
        kernel,
        in_specs=[WHOLE] * 4,
        out_specs=WHOLE,
        out_shape=jax.ShapeDtypeStruct((toks, width), BF16),
        compiler_params=params(8),
        name="attended",
    )(queries, keys, values, kv_before)


def pair_weight_grad(core, attended, attended_mate, grad, grad_mate, grad_scale):
    width = attended.shape[1]
    half = grad.shape[1] // 2
    rows = 512

    def kernel(core_ref, a_ref, am_ref, g_ref, gm_ref, out_ref):
        features = pl.ds(pl.multiple_of(pl.program_id(0) * rows, rows), rows)
        columns = pl.ds(pl.multiple_of(core_ref[0] * half, half), half)
        total = mul(a_ref[:, features], g_ref[:, columns], 0, 0)
        total = total + mul(am_ref[:, features], gm_ref[:, columns], 0, 0)
        out_ref[...] = (total * grad_scale).astype(BF16)

    return pl.pallas_call(
        kernel,
        grid=(width // rows,),
        in_specs=[SCALARS] + [WHOLE] * 4,
        out_specs=pl.BlockSpec((rows, half), lambda i: (i, 0)),
        out_shape=pltpu.HBM((width, half), BF16),
        compiler_params=params(12),
        name="pair_weight_grad",
    )(core, attended, attended_mate, grad, grad_mate)


def sum_plane(pieces):
    count, rows, width = pieces.shape
    keep = rows // 2
    slices = width // HEAD_DIM

    def kernel(x_ref, out_ref):
        for part in range(slices):
            lanes = slice(part * HEAD_DIM, (part + 1) * HEAD_DIM)
            total = x_ref[0, :, lanes].astype(F32)
            for at in range(1, count):
                total = total + x_ref[at, :, lanes].astype(F32)
            total = total.astype(BF16)
            out_ref[part, 0] = total[:keep]
            out_ref[part, 1] = total[keep:]

    return pl.pallas_call(
        kernel,
        out_shape=pltpu.HBM((slices, 2, keep, HEAD_DIM), BF16),
        in_specs=[WHOLE],
        out_specs=WHOLE,
        compiler_params=params(4),
        name="sum_plane",
    )(pieces)


def sum_groups(pieces):
    count = pieces.shape[0]

    def kernel(x_ref, out_ref):
        total = x_ref[0].astype(F32)
        for at in range(1, count):
            total = total + x_ref[at].astype(F32)
        total = total.astype(BF16)
        for at in range(count):
            out_ref[at] = total

    return pl.pallas_call(
        kernel,
        out_shape=pltpu.HBM(pieces.shape, BF16),
        in_specs=[WHOLE],
        out_specs=WHOLE,
        compiler_params=params(4),
        name="sum_groups",
    )(pieces)


def lay_rows(pieces):
    slices, halves, rows, lanes = pieces.shape

    def kernel(x_ref, out_ref):
        for half in range(halves):
            for part in range(slices):
                start = (half * slices + part) * lanes
                out_ref[:, start : start + lanes] = x_ref[part, half].astype(F32)

    return pl.pallas_call(
        kernel,
        out_shape=jax.ShapeDtypeStruct((rows, halves * slices * lanes), F32),
        in_specs=[WHOLE],
        out_specs=WHOLE,
        compiler_params=params(4),
        name="lay_rows",
    )(pieces)


def join_row(places, own, others):
    def kernel(place_ref, own_ref, a_ref, b_ref, c_ref, out_ref):
        x = place_ref[1]
        for by, ref in enumerate((own_ref, a_ref, b_ref, c_ref)):
            out_ref[lax.rem(x - by + 4, 4)] = ref[...]

    return pl.pallas_call(
        kernel,
        in_specs=[SCALARS] + [WHOLE] * 4,
        out_specs=WHOLE,
        out_shape=jax.ShapeDtypeStruct((4, *own.shape), BF16),
        compiler_params=params(4),
        name="join_row",
    )(places, own, *others)


def head_grads(places, grad, queries, attended, mine_parts, mate_parts):
    toks, model = grad.shape
    width = queries.shape[1]
    piece = mine_parts[0].shape[1]
    rows = 8 * piece
    half = width // 2

    def kernel(place_ref, grad_ref, query_ref, a_ref, *refs):
        sides = refs[:4], refs[4:8]
        hg_ref, mine_ref, give_ref, out_ref, g_ref, q_ref, buf, grad_sem, query_sem, sems = refs[8:]
        grad_copy = pltpu.make_async_copy(grad_ref, g_ref, grad_sem)
        grad_copy.start()
        query_copy = pltpu.make_async_copy(query_ref, q_ref, query_sem)
        query_copy.start()
        y, core = place_ref[0], place_ref[2]
        blocks = [lax.rem(y - by + 4, 4) for by in range(4)]
        waits = []
        for by in range(4):
            group = []
            for side in range(2):
                owner = core if side == 0 else 1 - core
                target = buf.at[blocks[by], :, owner]
                group.append(pltpu.make_async_copy(sides[side][by], target, sems.at[by, side]))
            waits.append(group)
        order = (0, 1, 3, 2)
        for by in order:
            for copy in waits[by]:
                copy.start()
        grad_copy.wait()
        query_copy.wait()
        for by in order:
            for copy in waits[by]:
                copy.wait()
            lanes = pl.ds(pl.multiple_of(blocks[by] * rows, rows), rows)
            block = buf[blocks[by]].reshape(rows, model)
            middle = toks // 2
            head_grad = jnp.concatenate(
                [mul(g_ref[:middle], block, 1, 1), mul(g_ref[middle:], block, 1, 1)], 0
            ).astype(BF16)
            hg_ref[:, lanes] = head_grad
            query = q_ref[:, lanes]
            states = [
                mul(query[:, head_lanes(h)], head_grad[:, head_lanes(h)], 0, 0)
                for h in range(rows // HEAD_DIM)
            ]
            state = jnp.concatenate(states, 0).astype(BF16)
            place = pl.ds(pl.multiple_of(lax.rem(blocks[by], 2) * rows, rows), rows)
            here = blocks[by] // 2 == core

            @pl.when(here)
            def _():
                mine_ref[place, :] = state

            @pl.when(jnp.logical_not(here))
            def _():
                give_ref[place, :] = state

        for start in range(0, model, 512):
            columns = slice(start, start + 512)
            wide = buf[:, :, :, :, columns].reshape(width, 512)
            out_ref[:, columns] = mul(a_ref[...], wide, 1, 0).astype(BF16)

    return pl.pallas_call(
        kernel,
        in_specs=[SCALARS, IN_PLACE, IN_PLACE, WHOLE] + [IN_PLACE] * 8,
        out_specs=[WHOLE] * 4,
        out_shape=[
            jax.ShapeDtypeStruct((toks, width), BF16),
            jax.ShapeDtypeStruct((half, HEAD_DIM), BF16),
            jax.ShapeDtypeStruct((half, HEAD_DIM), BF16),
            jax.ShapeDtypeStruct((toks, model), BF16),
        ],
        scratch_shapes=[
            pltpu.VMEM((toks, model), BF16),
            pltpu.VMEM((toks, width), BF16),
            pltpu.VMEM((4, 4, 2, piece, model), BF16),
            pltpu.SemaphoreType.DMA,
            pltpu.SemaphoreType.DMA,
            pltpu.SemaphoreType.DMA((4, 2)),
        ],
        compiler_params=params(12),
        name="head_grads",
    )(places, in_hbm(grad), in_hbm(queries), attended, *[in_hbm(part) for part in (*mine_parts, *mate_parts)])


def chip_states(mine, mate):
    def kernel(a_ref, b_ref, out_ref):
        out_ref[...] = (a_ref[...].astype(F32) + b_ref[...].astype(F32)).astype(BF16)

    return pl.pallas_call(
        kernel,
        in_specs=[WHOLE] * 2,
        out_specs=WHOLE,
        out_shape=jax.ShapeDtypeStruct(mine.shape, BF16),
        compiler_params=params(4),
        name="chip_states",
    )(mine, mate)


def row_states(places, chip, pieces):
    def kernel(place_ref, chip_ref, a_ref, b_ref, c_ref, row_ref, later_ref):
        x = place_ref[1]
        total, later = chip_ref[...].astype(F32), jnp.zeros(chip_ref.shape, F32)
        for by, ref in enumerate((a_ref, b_ref, c_ref), 1):
            piece = ref[...].astype(F32)
            total = total + piece
            later = later + jnp.where(x + by < 4, piece, 0.0)
        row_ref[...] = total.astype(BF16)
        later_ref[...] = later

    return pl.pallas_call(
        kernel,
        in_specs=[pl.BlockSpec(memory_space=pltpu.SMEM)] + [WHOLE] * 4,
        out_specs=[WHOLE] * 2,
        out_shape=[jax.ShapeDtypeStruct(chip.shape, BF16), jax.ShapeDtypeStruct(chip.shape, F32)],
        compiler_params=params(4),
        name="row_states",
    )(places, chip, *pieces)


def final_states(places, later_here, mine, mate, pieces):
    def kernel(place_ref, later_ref, mine_ref, mate_ref, a_ref, b_ref, c_ref, keep_ref, give_ref):
        y, core = place_ref[0], place_ref[2]
        later = later_ref[...]
        for by, ref in enumerate((a_ref, b_ref, c_ref), 1):
            later = later + jnp.where(y + by < 4, ref[...].astype(F32), 0.0)
        second = jnp.where(core == 0, mate_ref[...], mine_ref[...]).astype(F32)
        first_core, second_core = later + second, later
        keep_ref[...] = jnp.where(core == 0, first_core, second_core).astype(BF16)
        give_ref[...] = jnp.where(core == 0, second_core, first_core).astype(BF16)

    return pl.pallas_call(
        kernel,
        in_specs=[pl.BlockSpec(memory_space=pltpu.SMEM)] + [WHOLE] * 6,
        out_specs=[WHOLE] * 2,
        out_shape=[jax.ShapeDtypeStruct(mine.shape, BF16)] * 2,
        compiler_params=params(4),
        name="final_states",
    )(places, later_here, mine, mate, *pieces)


def local_grads(queries, keys, values, head_grad, kv_before, att_scale):
    toks, width = queries.shape
    half = toks // 2
    group = HEADS // 2

    def kernel(q_ref, k_ref, v_ref, g_ref, kv_ref, dq_ref, dk_ref, dv_ref):
        positions = lax.broadcasted_iota(jnp.int32, (half, half), 0)
        sources = lax.broadcasted_iota(jnp.int32, (half, half), 1)
        causal, turned = positions >= sources, positions <= sources

        def scaled(left, right, mask=None):
            scores = mul(left, right, 1, 1) * att_scale
            return (scores if mask is None else jnp.where(mask, scores, 0.0)).astype(BF16)

        for head in range(group):
            first = (pl.program_id(0) * group + head) * HEAD_DIM
            lanes = pl.ds(pl.multiple_of(first, HEAD_DIM), HEAD_DIM)
            here = head_lanes(head)
            q0, q1 = q_ref[:half, lanes], q_ref[half:, lanes]
            k0, k1 = k_ref[:half, lanes], k_ref[half:, lanes]
            v0, v1 = v_ref[:half, lanes], v_ref[half:, lanes]
            g0, g1 = g_ref[:half, lanes], g_ref[half:, lanes]
            kv = kv_ref[lanes, :]
            dv_ref[:half, here] = mul(scaled(k0, q0, turned), g0, 1, 0) + mul(
                scaled(k0, q1), g1, 1, 0
            )
            dv_ref[half:, here] = mul(scaled(k1, q1, turned), g1, 1, 0)
            b00, b10, b11 = scaled(g0, v0, causal), scaled(g1, v0), scaled(g1, v1, causal)
            dk_ref[:half, here] = mul(b00, q0, 0, 0) + mul(b10, q1, 0, 0)
            dk_ref[half:, here] = mul(b11, q1, 0, 0)
            dq_ref[:half, here] = (mul(b00, k0, 1, 0) + att_scale * mul(g0, kv, 1, 1)).astype(BF16)
            dq_ref[half:, here] = (
                mul(b10, k0, 1, 0) + mul(b11, k1, 1, 0) + att_scale * mul(g1, kv, 1, 1)
            ).astype(BF16)

    return pl.pallas_call(
        kernel,
        grid=(HEADS // group,),
        in_specs=[WHOLE] * 5,
        out_specs=[pl.BlockSpec((toks, group * HEAD_DIM), lambda i: (0, i))] * 3,
        out_shape=[
            pltpu.HBM((toks, width), BF16),
            pltpu.HBM((toks, width), F32),
            pltpu.HBM((toks, width), F32),
        ],
        compiler_params=params(12),
        name="local_grads",
    )(queries, keys, values, head_grad, kv_before)


def later_grads(core, keys, values, key_local, value_local, keep, back, att_scale):
    toks, width = keys.shape
    heads = keep.shape[0] // HEAD_DIM
    rows = 128

    def kernel(core_ref, k_ref, v_ref, dkl_ref, dvl_ref, keep_ref, back_ref, dk_ref, dv_ref):
        here = pl.ds(pl.multiple_of(pl.program_id(0) * rows, rows), rows)
        for head in range(HEADS):
            lanes, state = head_lanes(head), head_lanes(head % heads)
            mine = core_ref[0] == head // heads
            qg = jnp.where(mine, keep_ref[state, :], back_ref[state, :])
            dk_ref[:, lanes] = (
                dkl_ref[:, lanes] + att_scale * mul(v_ref[here, lanes], qg, 1, 1)
            ).astype(BF16)
            dv_ref[:, lanes] = (
                dvl_ref[:, lanes] + att_scale * mul(k_ref[here, lanes], qg, 1, 0)
            ).astype(BF16)

    block = pl.BlockSpec((rows, width), lambda i: (i, 0))
    return pl.pallas_call(
        kernel,
        grid=(toks // rows,),
        in_specs=[SCALARS, WHOLE, WHOLE, block, block, WHOLE, WHOLE],
        out_specs=[block] * 2,
        out_shape=[pltpu.HBM((toks, width), BF16)] * 2,
        compiler_params=params(8),
        name="later_grads",
    )(core, keys, values, in_hbm(key_local), in_hbm(value_local), keep, back)


def swap_cores(value):
    return lax.ppermute(value, "core", [(0, 1), (1, 0)])


def turn(value, axis, count, by):
    return lax.ppermute(value, axis, [(at, (at + by) % count) for at in range(count)])


def after(value, *others):
    return lax.optimization_barrier((value,) + others)[0]


def around(value, axis, sign):
    return [turn(value, axis, 4, sign * by) for by in (1, 2, 3)]


def on_device(query_in, key_in, value_in, out_grad, out_weight):
    queries, keys, values, grad = query_in[0], key_in[0], value_in[0], out_grad[0]
    toks = queries.shape[0]
    length = toks * 32
    att_scale = 1.0 / math.sqrt(HEAD_DIM * length)
    grad_scale = 1.0 / math.sqrt(length * 8)
    core = lax.axis_index("core")
    half = grad.shape[1] // 2
    places = jnp.stack([lax.axis_index("y"), lax.axis_index("x"), core])
    core_place = jnp.reshape(core, (1,))

    shards = around(out_weight, "x", 1)
    far_shard = turn(out_weight, "y", 4, 2)
    grad_mate = swap_cores(grad)
    kv_block = kv_states(keys, values)

    pieces = lax.all_to_all(kv_block.reshape(32, -1, HEAD_DIM), CONTEXT, 0, 0)
    prefixes = strict_prefix(after(pieces, grad_mate, far_shard, *shards), False)
    row = join_row(places, after(out_weight, prefixes), shards)
    low, high = turn(row, "y", 4, 1), turn(row, "y", 4, -1)
    far_shard = after(far_shard, prefixes)
    far_shards = around(far_shard, "x", 1)
    kv_before = lax.all_to_all(prefixes, CONTEXT, 0, 0).reshape(kv_block.shape)

    far_row = join_row(places, far_shard, far_shards)
    kv_before = after(kv_before, low, high, far_row)
    attended = attended_states(queries, keys, values, kv_before, att_scale)
    attended_mate = swap_cores(attended)
    terms = pair_weight_grad(core_place, attended, attended_mate, grad, grad_mate, grad_scale)
    plane_terms = lax.all_to_all(terms.reshape(16, 64, half), PLANE, 0, 0)

    weight_mine = [row, low, far_row, high]
    weight_mate = [swap_cores(after(part, terms)) for part in weight_mine]
    head_grad, mine, give, output = head_grads(
        after(places, terms), grad, queries, attended, weight_mine, weight_mate
    )
    mate = swap_cores(give)
    chip = chip_states(mine, mate)
    row_state, later_here = row_states(places, chip, around(chip, "x", -1))
    query_grad, key_local, value_local = local_grads(
        queries, keys, values, head_grad, kv_before, att_scale
    )

    plane_terms = after(plane_terms, key_local, row_state)
    plane_sum = sum_plane(plane_terms)
    group_terms = lax.all_to_all(plane_sum.reshape(16, 32, HEAD_DIM), ("z", "core"), 0, 0)
    row_pieces = around(after(row_state, plane_sum), "y", -1)
    keep, give = final_states(places, later_here, mine, mate, row_pieces)
    back = swap_cores(give)
    group_sum = sum_groups(group_terms.reshape(8, 2, 32, HEAD_DIM))
    weight_grad = lay_rows(lax.all_to_all(group_sum, "z", 0, 0))

    key_grad, value_grad = later_grads(
        core_place, keys, values, key_local, value_local, after(keep, group_sum), back, att_scale
    )
    return (output[None], query_grad[None], key_grad[None], value_grad[None], weight_grad)


def solution(mesh):
    fine = Mesh(mesh.devices.reshape(8, 4, 4, 2), ("z", "y", "x", "core"))
    rows = P("z", CONTEXT, None)
    owned = P(CONTEXT, None)
    return jax.shard_map(
        on_device,
        mesh=fine,
        in_specs=(rows, rows, rows, rows, owned),
        out_specs=(rows, rows, rows, rows, owned),
        check_vma=False,
    )
```

time: 143 us -> 140 us (0.979)
  starting transfers between devices: 29.4 us -> 60.8 us
  blocking collectives: 26.9 us -> 0 us
  waiting for transfers between devices: 17.1 us -> 32.2 us
  between operations: 14.1 us -> 0.91 us
  Pallas kernels: 52.8 us -> 42.6 us
    all_to_all x2 -> x0, blocking collectives: 26.9 us -> none  [the longest x1 14.4 us: on_device(): pieces = lax.all_to_all(kv_block.reshape(32, -1, HEAD_DIM), CONTEXT, 0, 0)]
    ppermute x6 -> x15, starting transfers between devices: 8.62 us -> 24.4 us  [turn(): lax.ppermute(value, axis, [(at, (at + by) % count) for at in range(count)])]
    ppermute x6 -> x15, waiting for transfers between devices: 4.47 us -> 17.8 us  [turn(): lax.ppermute(value, axis, [(at, (at + by) % count) for at in range(count)])]
    all_to_all x0 -> x2, starting transfers between devices: none -> 12.3 us  [the longest x1 6.54 us: on_device(): kv_before = lax.all_to_all(prefixes, CONTEXT, 0, 0).reshape(kv_block.shape)]
    pallas_call x7 -> x8, Pallas kernels: 48.9 us -> 37.2 us  [the longest x1 10.3 us: head_grads(): pl.pallas_call(kernel, in_specs=[SCALARS, IN_PLACE, IN_PLACE, WHOLE] + [I...]
    ppermute x4 -> x8, waiting for transfers between devices: 4.86 us -> 7.98 us  [swap_cores(): return lax.ppermute(value, 'core', [(0, 1), (1, 0)])]
    all_gather x1 -> x0, waiting for transfers between devices: 2.51 us -> none  [on_device(): weight = lax.all_gather(out_weight, CONTEXT, axis=0, tiled=True)]
    unnamed x0 -> x28, local copies, waits for them, and re-layouts: none -> 2.37 us
  transfers between devices with their start and end apart: 14 -> 28, of which waited for: 6 -> 15; matrix products, arithmetic and copies ran while one was open for 1% -> 0% of each run, Pallas kernels for 36% -> 21%
where the time goes in v3:
time: 140 us; the launch traced here: 139 us
  starting transfers between devices  60.8 us (43%)
  Pallas kernels  42.6 us (30%)
  waiting for transfers between devices  32.2 us (23%)
  local copies, waits for them, and re-layouts  2.37 us (2%)
    ppermute x15, starting transfers between devices, turn(): lax.ppermute(value, axis, [(at, (at + by) % count) for at in range(count)])  24.4 us
    ppermute x15, waiting for transfers between devices, turn(): lax.ppermute(value, axis, [(at, (at + by) % count) for at in range(count)])  17.8 us
    pallas_call x1, Pallas kernels, head_grads(): pl.pallas_call(kernel, in_specs=[SCALARS, IN_PLACE, IN_PLACE, WHOLE] + [I...  10.3 us
    all_to_all x1, starting transfers between devices, on_device(): lax.all_to_all(plane_sum.reshape(16, 32, HEAD_DIM), ('z', 'core'), 0, 0)  9.98 us
    pallas_call x1, Pallas kernels, local_grads(): pl.pallas_call(kernel, grid=(HEADS // group,), in_specs=[WHOLE] * 5, out_...  8.92 us
    ppermute x8, waiting for transfers between devices, swap_cores(): return lax.ppermute(value, 'core', [(0, 1), (1, 0)])  7.98 us
    all_to_all x1, starting transfers between devices, on_device(): kv_before = lax.all_to_all(prefixes, CONTEXT, 0, 0).reshape(kv_block.shape)  6.54 us
    ppermute x8, starting transfers between devices, swap_cores(): return lax.ppermute(value, 'core', [(0, 1), (1, 0)])  5.95 us
  transfers between devices with their start and end apart: 28, of which 15 were waited for; matrix products, arithmetic and copies ran while one was open for 0% of the time, Pallas kernels for 21%

profile of v3, /device:TPU:1, one launch (start us, length us, event | category | flops | bytes accessed | tf_op | source)
XLA Modules:
  0.0 138.9 jit_solution(17213641968736245669)
XLA Ops:
  0.6 3.3 %collective-permute-start = (bf16[512,2048]{1,0:T(8,128)(2,1)}, bf16[512,2048]{1,0:T(8,128)(2,1)}, u32[]{:S(2)}, u32[]{:S(2)}) collective-permute-start(bf16[512,2048]{1,0:T(8,128)(2,1)} %bitcast.27), channel_id=1, source_target_pairs={{0,1},{1,0},{2,3},{3,2},{4,5},{5,4},{6,7},{7,6},{8,9},{9,8},{10,11... | collective-permute-start | bytes 6291464 | tf_op jit(solution)/shard_map/ppermute | solution.py:459
  4.0 2.6 %kv_states.1 = bf16[1024,128]{1,0:T(8,128)(2,1)} custom-call(bf16[512,1024]{1,0:T(8,128)(2,1)} %bitcast.16, bf16[512,1024]{1,0:T(8,128)(2,1)} %bitcast.20), custom_call_target="tpu_custom_call" | custom-call | tf_op jit(solution)/shard_map/kv_states/pallas_call | solution.py:59
  6.7 5.7 %all-to-all-start = ((bf16[32,32,128]{2,1,0:T(8,128)(2,1)}), bf16[32,32,128]{2,1,0:T(8,128)(2,1)S(1)}, u32[]{:S(2)}, u32[]{:S(2)}) async-start(bf16[32,32,128]{2,1,0:T(8,128)(2,1)} %bitcast.6), calls=%async_computation | async-start | bytes 524288 | tf_op jit(solution)/shard_map/all_to_all | solution.py:490
  12.4 3.0 %collective-permute-start.3 = (bf16[32,2048]{1,0:T(8,128)(2,1)S(1)}, bf16[32,2048]{1,0:T(8,128)(2,1)}, u32[]{:S(2)}, u32[]{:S(2)}) collective-permute-start(bf16[32,2048]{1,0:T(8,128)(2,1)S(1)} %copy-done.9), channel_id=1, source_target_pairs={{0,4},{2,6},{4,0},{6,2},{1,5},{3,7},{5,1},{7,3},{8,12},{10,14},{12... | collective-permute-start | bytes 393224 | tf_op jit(solution)/shard_map/ppermute | solution.py:463
  15.7 2.7 %collective-permute-start.1 = (bf16[32,2048]{1,0:T(8,128)(2,1)S(1)}, bf16[32,2048]{1,0:T(8,128)(2,1)}, u32[]{:S(2)}, u32[]{:S(2)}) collective-permute-start(bf16[32,2048]{1,0:T(8,128)(2,1)S(1)} %copy-done.9), channel_id=1, source_target_pairs={{0,16},{8,24},{16,0},{24,8},{1,17},{9,25},{17,1},{25,9},{2,18},{10... | collective-permute-start | bytes 393224 | tf_op jit(solution)/shard_map/ppermute | solution.py:463
  21.9 2.9 %collective-permute-done.2.a_ref = bf16[32,2048]{1,0:T(8,128)(2,1)} collective-permute-done((bf16[32,2048]{1,0:T(8,128)(2,1)S(1)}, bf16[32,2048]{1,0:T(8,128)(2,1)}, u32[]{:S(2)}, u32[]{:S(2)}) %collective-permute-start.2) | collective-permute-done | bytes 131104 | tf_op jit(solution)/shard_map/ppermute | solution.py:463
  27.4 2.5 %collective-permute-start.6 = (bf16[4,32,2048]{2,1,0:T(8,128)(2,1)}, bf16[4,32,2048]{2,1,0:T(8,128)(2,1)}, u32[]{:S(2)}, u32[]{:S(2)}) collective-permute-start(bf16[4,32,2048]{2,1,0:T(8,128)(2,1)} %join_row.2.refs_0_), channel_id=1, source_target_pairs={{0,24},{8,0},{16,8},{24,16},{1,25},{9,1},{17,9},{25,17},{2,26},{10... | collective-permute-start | bytes 1572872 | tf_op jit(solution)/shard_map/ppermute | solution.py:463
  29.9 6.5 %all-to-all-start.1 = ((bf16[32,32,128]{2,1,0:T(8,128)(2,1)}), bf16[32,32,128]{2,1,0:T(8,128)(2,1)S(1)}, u32[]{:S(2)}, u32[]{:S(2)}) async-start(bf16[32,32,128]{2,1,0:T(8,128)(2,1)} %copy-done.8), calls=%async_computation.1 | async-start | bytes 524288 | tf_op jit(solution)/shard_map/all_to_all | solution.py:496
  36.4 2.7 %collective-permute-start.9 = (bf16[32,2048]{1,0:T(8,128)(2,1)}, bf16[32,2048]{1,0:T(8,128)(2,1)S(1)}, u32[]{:S(2)}, u32[]{:S(2)}) collective-permute-start(bf16[32,2048]{1,0:T(8,128)(2,1)} %collective-permute-done.1.own_ref), channel_id=1, source_target_pairs={{0,6},{2,0},{4,2},{6,4},{1,7},{3,1},{5,3},{7,5},{8,14},{10,8},{12,... | collective-permute-start | bytes 393224 | tf_op jit(solution)/shard_map/ppermute | solution.py:463
  40.3 4.1 %collective-permute-done.9.c_ref = bf16[32,2048]{1,0:T(8,128)(2,1)S(1)} collective-permute-done((bf16[32,2048]{1,0:T(8,128)(2,1)}, bf16[32,2048]{1,0:T(8,128)(2,1)S(1)}, u32[]{:S(2)}, u32[]{:S(2)}) %collective-permute-start.9) | collective-permute-done | bytes 131104 | tf_op jit(solution)/shard_map/ppermute | solution.py:463
  45.2 3.9 %collective-permute-done.7.a_ref = bf16[32,2048]{1,0:T(8,128)(2,1)S(1)} collective-permute-done((bf16[32,2048]{1,0:T(8,128)(2,1)}, bf16[32,2048]{1,0:T(8,128)(2,1)S(1)}, u32[]{:S(2)}, u32[]{:S(2)}) %collective-permute-start.7) | collective-permute-done | bytes 131104 | tf_op jit(solution)/shard_map/ppermute | solution.py:463
  50.9 2.5 %attended.1.a_ref = bf16[512,1024]{1,0:T(8,128)(2,1)S(1)} custom-call(bf16[512,1024]{1,0:T(8,128)(2,1)S(1)} %bitcast.25, bf16[512,1024]{1,0:T(8,128)(2,1)S(1)} %bitcast.17, bf16[512,1024]{1,0:T(8,128)(2,1)S(1)} %bitcast.21, bf16[1024,128]{1,0:T(8,128)(2,1)S(1)} %bitcast.30), custom_call_target="tpu_custom_call" | custom-call | tf_op jit(solution)/shard_map/attended/pallas_call | solution.py:123
  56.5 5.2 %pair_weight_grad.1 = bf16[1024,1024]{1,0:T(8,128)(2,1)} custom-call(s32[1]{0:T(128)} %bitcast.2.core_ref, bf16[512,1024]{1,0:T(8,128)(2,1)S(1)} %attended.1.a_ref, bf16[512,1024]{1,0:T(8,128)(2,1)S(1)} %collective-permute-done.10.am_ref, bf16[512,2048]{1,0:T(8,128)(2,1)S(1)} %bitcast.29, bf16[512,2048]{1,0:T(8,128)(2,1)} %collective-permute-done.gm_ref), custom_call_target="tpu_custom_call" | custom-call | tf_op jit(solution)/shard_map/pair_weight_grad/pallas_call | solution.py:145
  61.6 4.8 %all-to-all-start.2 = ((bf16[16,64,1024]{2,1,0:T(8,128)(2,1)}), bf16[16,64,1024]{2,1,0:T(8,128)(2,1)}, u32[]{:S(2)}, u32[]{:S(2)}) async-start(bf16[16,64,1024]{2,1,0:T(8,128)(2,1)} %bitcast.33), calls=%async_computation.2 | async-start | bytes 4194304 | tf_op jit(solution)/shard_map/all_to_all | solution.py:503
  72.0 10.3 %head_grads.1 = (bf16[512,1024]{1,0:T(8,128)(2,1)S(1)}, bf16[512,128]{1,0:T(8,128)(2,1)S(1)}, bf16[512,128]{1,0:T(8,128)(2,1)S(1)}, bf16[512,2048]{1,0:T(8,128)(2,1)}) custom-call(s32[3]{0:T(128)S(1)} %pad_add_fusion.place_ref, bf16[512,2048]{1,0:T(8,128)(2,1)} %bitcast.28, bf16[512,1024]{1,0:T(8,128)(2,1)} %bitcast.24, bf16[512,1024]{1,0:T(8,128)(2,1)S(1)} %copy-done.5, ...), custom_call_target="tpu_custom_call" | custom-call | tf_op jit(solution)/shard_map/head_grads/pallas_call | solution.py:299
  85.5 2.4 %collective-permute-start.17 = (bf16[512,128]{1,0:T(8,128)(2,1)S(1)}, bf16[512,128]{1,0:T(8,128)(2,1)S(1)}, u32[]{:S(2)}, u32[]{:S(2)}) collective-permute-start(bf16[512,128]{1,0:T(8,128)(2,1)S(1)} %chip_states.1.chip_ref), channel_id=1, source_target_pairs={{0,4},{2,6},{4,0},{6,2},{1,5},{3,7},{5,1},{7,3},{8,12},{10,14},{12... | collective-permute-start | bytes 393224 | tf_op jit(solution)/shard_map/ppermute | solution.py:463
  89.0 8.9 %local_grads.1 = (bf16[512,1024]{1,0:T(8,128)(2,1)}, f32[512,1024]{1,0:T(8,128)}, f32[512,1024]{1,0:T(8,128)}) custom-call(bf16[512,1024]{1,0:T(8,128)(2,1)S(1)} %bitcast.26, bf16[512,1024]{1,0:T(8,128)(2,1)S(1)} %bitcast.18, bf16[512,1024]{1,0:T(8,128)(2,1)S(1)} %bitcast.22, bf16[512,1024]{1,0:T(8,128)(2,1)S(1)} %get-tuple-element.40.g_ref, ...), custom_call_target="tpu_custom_call" | custom-call | tf_op jit(solution)/shard_map/local_grads/pallas_call | solution.py:413
  98.0 5.0 %collective-permute-done.17.b_ref = bf16[512,128]{1,0:T(8,128)(2,1)S(1)} collective-permute-done((bf16[512,128]{1,0:T(8,128)(2,1)S(1)}, bf16[512,128]{1,0:T(8,128)(2,1)S(1)}, u32[]{:S(2)}, u32[]{:S(2)}) %collective-permute-start.17) | collective-permute-done | bytes 131104 | tf_op jit(solution)/shard_map/ppermute | solution.py:463
  103.6 2.6 %sum_plane.1 = bf16[8,2,32,128]{3,2,1,0:T(8,128)(2,1)} custom-call(bf16[16,64,1024]{2,1,0:T(8,128)(2,1)} %all-to-all-done.2.x_ref), custom_call_target="tpu_custom_call" | custom-call | tf_op jit(solution)/shard_map/sum_plane/pallas_call | solution.py:171
  106.2 10.0 %all-to-all-start.3 = ((bf16[16,32,128]{2,1,0:T(8,128)(2,1)}), bf16[16,32,128]{2,1,0:T(8,128)(2,1)S(1)}, u32[]{:S(2)}, u32[]{:S(2)}) async-start(bf16[16,32,128]{2,1,0:T(8,128)(2,1)} %bitcast.34), calls=%async_computation.3 | async-start | bytes 262144 | tf_op jit(solution)/shard_map/all_to_all | solution.py:519
  116.2 2.6 %collective-permute-start.20 = (bf16[512,128]{1,0:T(8,128)(2,1)S(1)}, bf16[512,128]{1,0:T(8,128)(2,1)S(1)}, u32[]{:S(2)}, u32[]{:S(2)}) collective-permute-start(bf16[512,128]{1,0:T(8,128)(2,1)S(1)} %get-tuple-element.49), channel_id=1, source_target_pairs={{0,16},{8,24},{16,0},{24,8},{1,17},{9,25},{17,1},{25,9},{2,18},{10... | collective-permute-start | bytes 393224 | tf_op jit(solution)/shard_map/ppermute | solution.py:463
  120.7 4.7 %all-to-all-done.3 = bf16[16,32,128]{2,1,0:T(8,128)(2,1)S(1)} async-done(((bf16[16,32,128]{2,1,0:T(8,128)(2,1)}), bf16[16,32,128]{2,1,0:T(8,128)(2,1)S(1)}, u32[]{:S(2)}, u32[]{:S(2)}) %all-to-all-start.3) | async-done | bytes 131104 | tf_op jit(solution)/shard_map/all_to_all | solution.py:519
  126.1 3.4 %all-to-all-start.4 = ((bf16[8,2,32,128]{3,2,1,0:T(8,128)(2,1)}), bf16[8,2,32,128]{3,2,1,0:T(8,128)(2,1)S(1)}, u32[]{:S(2)}, u32[]{:S(2)}) async-start(bf16[8,2,32,128]{3,2,1,0:T(8,128)(2,1)} %sum_groups.1), calls=%async_computation.4 | async-start | bytes 262144 | tf_op jit(solution)/shard_map/all_to_all | solution.py:524
  131.6 4.8 %later_grads.1 = (bf16[512,1024]{1,0:T(8,128)(2,1)}, bf16[512,1024]{1,0:T(8,128)(2,1)}) custom-call(s32[1]{0:T(128)} %bitcast.2.core_ref, bf16[512,1024]{1,0:T(8,128)(2,1)S(1)} %bitcast.19, bf16[512,1024]{1,0:T(8,128)(2,1)S(1)} %bitcast.23, f32[512,1024]{1,0:T(8,128)} %get-tuple-element.42.dkl_ref, f32[512,1024]{1,0:T(8,128)} %get-tuple-element.43.dvl_ref, ...), custom_call_target="tpu_custom_call" | custom-call | tf_op jit(solution)/shard_map/later_grads/pallas_call | solution.py:447
  (76 shorter events, 31.0 us)
Async XLA Ops:
  0.6 24.1 %collective-permute-start = (bf16[512,2048]{1,0:T(8,128)(2,1)}, bf16[512,2048]{1,0:T(8,128)(2,1)}, u32[]{:S(2)}, u32[]{:S(2)}) collective-permute-start(bf16[512,2048]{1,0:T(8,128)(2,1)} %bitcast.27), channel_id=1, source_target_pairs={{0,1},{1,0},{2,3},{3,2},{4,5},{5,4},{6,7},{7,6},{8,9},{9,8},{10,11... | collective-permute-start | bytes 6291464 | tf_op jit(solution)/shard_map/ppermute | solution.py:459
  6.7 18.1 %all-to-all-start = ((bf16[32,32,128]{2,1,0:T(8,128)(2,1)}), bf16[32,32,128]{2,1,0:T(8,128)(2,1)S(1)}, u32[]{:S(2)}, u32[]{:S(2)}) async-start(bf16[32,32,128]{2,1,0:T(8,128)(2,1)} %bitcast.6), calls=%async_computation | async-start | bytes 524288 | tf_op jit(solution)/shard_map/all_to_all | solution.py:490
  12.4 9.5 %collective-permute-start.3 = (bf16[32,2048]{1,0:T(8,128)(2,1)S(1)}, bf16[32,2048]{1,0:T(8,128)(2,1)}, u32[]{:S(2)}, u32[]{:S(2)}) collective-permute-start(bf16[32,2048]{1,0:T(8,128)(2,1)S(1)} %copy-done.9), channel_id=1, source_target_pairs={{0,4},{2,6},{4,0},{6,2},{1,5},{3,7},{5,1},{7,3},{8,12},{10,14},{12... | collective-permute-start | bytes 393224 | tf_op jit(solution)/shard_map/ppermute | solution.py:463
  15.4 9.4 %collective-permute-start.2 = (bf16[32,2048]{1,0:T(8,128)(2,1)S(1)}, bf16[32,2048]{1,0:T(8,128)(2,1)}, u32[]{:S(2)}, u32[]{:S(2)}) collective-permute-start(bf16[32,2048]{1,0:T(8,128)(2,1)S(1)} %copy-done.9), channel_id=1, source_target_pairs={{0,2},{2,4},{4,6},{6,0},{1,3},{3,5},{5,7},{7,1},{8,10},{10,12},{12... | collective-permute-start | bytes 393224 | tf_op jit(solution)/shard_map/ppermute | solution.py:463
  15.7 9.1 %collective-permute-start.1 = (bf16[32,2048]{1,0:T(8,128)(2,1)S(1)}, bf16[32,2048]{1,0:T(8,128)(2,1)}, u32[]{:S(2)}, u32[]{:S(2)}) collective-permute-start(bf16[32,2048]{1,0:T(8,128)(2,1)S(1)} %copy-done.9), channel_id=1, source_target_pairs={{0,16},{8,24},{16,0},{24,8},{1,17},{9,25},{17,1},{25,9},{2,18},{10... | collective-permute-start | bytes 393224 | tf_op jit(solution)/shard_map/ppermute | solution.py:463
  18.4 6.4 %collective-permute-start.4 = (bf16[32,2048]{1,0:T(8,128)(2,1)S(1)}, bf16[32,2048]{1,0:T(8,128)(2,1)}, u32[]{:S(2)}, u32[]{:S(2)}) collective-permute-start(bf16[32,2048]{1,0:T(8,128)(2,1)S(1)} %copy-done.9), channel_id=1, source_target_pairs={{0,6},{2,0},{4,2},{6,4},{1,7},{3,1},{5,3},{7,5},{8,14},{10,8},{12,... | collective-permute-start | bytes 393224 | tf_op jit(solution)/shard_map/ppermute | solution.py:463
  27.4 23.4 %collective-permute-start.6 = (bf16[4,32,2048]{2,1,0:T(8,128)(2,1)}, bf16[4,32,2048]{2,1,0:T(8,128)(2,1)}, u32[]{:S(2)}, u32[]{:S(2)}) collective-permute-start(bf16[4,32,2048]{2,1,0:T(8,128)(2,1)} %join_row.2.refs_0_), channel_id=1, source_target_pairs={{0,24},{8,0},{16,8},{24,16},{1,25},{9,1},{17,9},{25,17},{2,26},{10... | collective-permute-start | bytes 1572872 | tf_op jit(solution)/shard_map/ppermute | solution.py:463
  29.9 21.0 %collective-permute-start.5 = (bf16[4,32,2048]{2,1,0:T(8,128)(2,1)}, bf16[4,32,2048]{2,1,0:T(8,128)(2,1)}, u32[]{:S(2)}, u32[]{:S(2)}) collective-permute-start(bf16[4,32,2048]{2,1,0:T(8,128)(2,1)} %join_row.2.refs_0_), channel_id=1, source_target_pairs={{0,8},{8,16},{16,24},{24,0},{1,9},{9,17},{17,25},{25,1},{2,10},{10... | collective-permute-start | bytes 1572872 | tf_op jit(solution)/shard_map/ppermute | solution.py:463
  29.9 21.0 %all-to-all-start.1 = ((bf16[32,32,128]{2,1,0:T(8,128)(2,1)}), bf16[32,32,128]{2,1,0:T(8,128)(2,1)S(1)}, u32[]{:S(2)}, u32[]{:S(2)}) async-start(bf16[32,32,128]{2,1,0:T(8,128)(2,1)} %copy-done.8), calls=%async_computation.1 | async-start | bytes 524288 | tf_op jit(solution)/shard_map/all_to_all | solution.py:496
  36.4 8.0 %collective-permute-start.9 = (bf16[32,2048]{1,0:T(8,128)(2,1)}, bf16[32,2048]{1,0:T(8,128)(2,1)S(1)}, u32[]{:S(2)}, u32[]{:S(2)}) collective-permute-start(bf16[32,2048]{1,0:T(8,128)(2,1)} %collective-permute-done.1.own_ref), channel_id=1, source_target_pairs={{0,6},{2,0},{4,2},{6,4},{1,7},{3,1},{5,3},{7,5},{8,14},{10,8},{12,... | collective-permute-start | bytes 393224 | tf_op jit(solution)/shard_map/ppermute | solution.py:463
  39.1 6.1 %collective-permute-start.8 = (bf16[32,2048]{1,0:T(8,128)(2,1)}, bf16[32,2048]{1,0:T(8,128)(2,1)S(1)}, u32[]{:S(2)}, u32[]{:S(2)}) collective-permute-start(bf16[32,2048]{1,0:T(8,128)(2,1)} %collective-permute-done.1.own_ref), channel_id=1, source_target_pairs={{0,4},{2,6},{4,0},{6,2},{1,5},{3,7},{5,1},{7,3},{8,12},{10,14},{12... | collective-permute-start | bytes 393224 | tf_op jit(solution)/shard_map/ppermute | solution.py:463
  39.7 9.4 %collective-permute-start.7 = (bf16[32,2048]{1,0:T(8,128)(2,1)}, bf16[32,2048]{1,0:T(8,128)(2,1)S(1)}, u32[]{:S(2)}, u32[]{:S(2)}) collective-permute-start(bf16[32,2048]{1,0:T(8,128)(2,1)} %collective-permute-done.1.own_ref), channel_id=1, source_target_pairs={{0,2},{2,4},{4,6},{6,0},{1,3},{3,5},{5,7},{7,1},{8,10},{10,12},{12... | collective-permute-start | bytes 393224 | tf_op jit(solution)/shard_map/ppermute | solution.py:463
  53.5 3.0 %collective-permute-start.10 = (bf16[512,1024]{1,0:T(8,128)(2,1)S(1)}, bf16[512,1024]{1,0:T(8,128)(2,1)S(1)}, u32[]{:S(2)}, u32[]{:S(2)}) collective-permute-start(bf16[512,1024]{1,0:T(8,128)(2,1)S(1)} %attended.1.a_ref), channel_id=1, source_target_pairs={{0,1},{1,0},{2,3},{3,2},{4,5},{5,4},{6,7},{7,6},{8,9},{9,8},{10,11... | collective-permute-start | bytes 3145736 | tf_op jit(solution)/shard_map/ppermute | solution.py:459
  61.6 42.0 %all-to-all-start.2 = ((bf16[16,64,1024]{2,1,0:T(8,128)(2,1)}), bf16[16,64,1024]{2,1,0:T(8,128)(2,1)}, u32[]{:S(2)}, u32[]{:S(2)}) async-start(bf16[16,64,1024]{2,1,0:T(8,128)(2,1)} %bitcast.33), calls=%async_computation.2 | async-start | bytes 4194304 | tf_op jit(solution)/shard_map/all_to_all | solution.py:503
  67.3 3.1 %collective-permute-start.13 = (bf16[4,32,2048]{2,1,0:T(8,128)(2,1)}, bf16[4,32,2048]{2,1,0:T(8,128)(2,1)S(1)}, u32[]{:S(2)}, u32[]{:S(2)}) collective-permute-start(bf16[4,32,2048]{2,1,0:T(8,128)(2,1)} %copy-done.7), channel_id=1, source_target_pairs={{0,1},{1,0},{2,3},{3,2},{4,5},{5,4},{6,7},{7,6},{8,9},{9,8},{10,11... | collective-permute-start | bytes 1572872 | tf_op jit(solution)/shard_map/ppermute | solution.py:459
  67.7 3.5 %collective-permute-start.14 = (bf16[4,32,2048]{2,1,0:T(8,128)(2,1)}, bf16[4,32,2048]{2,1,0:T(8,128)(2,1)S(1)}, u32[]{:S(2)}, u32[]{:S(2)}) collective-permute-start(bf16[4,32,2048]{2,1,0:T(8,128)(2,1)} %collective-permute-done.6.refs_3_), channel_id=1, source_target_pairs={{0,1},{1,0},{2,3},{3,2},{4,5},{5,4},{6,7},{7,6},{8,9},{9,8},{10,11... | collective-permute-start | bytes 1572872 | tf_op jit(solution)/shard_map/ppermute | solution.py:459
  83.8 14.2 %collective-permute-start.18 = (bf16[512,128]{1,0:T(8,128)(2,1)S(1)}, bf16[512,128]{1,0:T(8,128)(2,1)S(1)}, u32[]{:S(2)}, u32[]{:S(2)}) collective-permute-start(bf16[512,128]{1,0:T(8,128)(2,1)S(1)} %chip_states.1.chip_ref), channel_id=1, source_target_pairs={{0,2},{2,4},{4,6},{6,0},{1,3},{3,5},{5,7},{7,1},{8,10},{10,12},{12... | collective-permute-start | bytes 393224 | tf_op jit(solution)/shard_map/ppermute | solution.py:463
  85.5 17.5 %collective-permute-start.17 = (bf16[512,128]{1,0:T(8,128)(2,1)S(1)}, bf16[512,128]{1,0:T(8,128)(2,1)S(1)}, u32[]{:S(2)}, u32[]{:S(2)}) collective-permute-start(bf16[512,128]{1,0:T(8,128)(2,1)S(1)} %chip_states.1.chip_ref), channel_id=1, source_target_pairs={{0,4},{2,6},{4,0},{6,2},{1,5},{3,7},{5,1},{7,3},{8,12},{10,14},{12... | collective-permute-start | bytes 393224 | tf_op jit(solution)/shard_map/ppermute | solution.py:463
  87.9 15.1 %collective-permute-start.16 = (bf16[512,128]{1,0:T(8,128)(2,1)S(1)}, bf16[512,128]{1,0:T(8,128)(2,1)S(1)}, u32[]{:S(2)}, u32[]{:S(2)}) collective-permute-start(bf16[512,128]{1,0:T(8,128)(2,1)S(1)} %chip_states.1.chip_ref), channel_id=1, source_target_pairs={{0,6},{2,0},{4,2},{6,4},{1,7},{3,1},{5,3},{7,5},{8,14},{10,8},{12,... | collective-permute-start | bytes 393224 | tf_op jit(solution)/shard_map/ppermute | solution.py:463
  106.2 19.1 %all-to-all-start.3 = ((bf16[16,32,128]{2,1,0:T(8,128)(2,1)}), bf16[16,32,128]{2,1,0:T(8,128)(2,1)S(1)}, u32[]{:S(2)}, u32[]{:S(2)}) async-start(bf16[16,32,128]{2,1,0:T(8,128)(2,1)} %bitcast.34), calls=%async_computation.3 | async-start | bytes 262144 | tf_op jit(solution)/shard_map/all_to_all | solution.py:519
  116.2 13.2 %collective-permute-start.21 = (bf16[512,128]{1,0:T(8,128)(2,1)S(1)}, bf16[512,128]{1,0:T(8,128)(2,1)S(1)}, u32[]{:S(2)}, u32[]{:S(2)}) collective-permute-start(bf16[512,128]{1,0:T(8,128)(2,1)S(1)} %get-tuple-element.49), channel_id=1, source_target_pairs={{0,8},{8,16},{16,24},{24,0},{1,9},{9,17},{17,25},{25,1},{2,10},{10... | collective-permute-start | bytes 393224 | tf_op jit(solution)/shard_map/ppermute | solution.py:463
  116.2 13.2 %collective-permute-start.20 = (bf16[512,128]{1,0:T(8,128)(2,1)S(1)}, bf16[512,128]{1,0:T(8,128)(2,1)S(1)}, u32[]{:S(2)}, u32[]{:S(2)}) collective-permute-start(bf16[512,128]{1,0:T(8,128)(2,1)S(1)} %get-tuple-element.49), channel_id=1, source_target_pairs={{0,16},{8,24},{16,0},{24,8},{1,17},{9,25},{17,1},{25,9},{2,18},{10... | collective-permute-start | bytes 393224 | tf_op jit(solution)/shard_map/ppermute | solution.py:463
  118.8 10.7 %collective-permute-start.19 = (bf16[512,128]{1,0:T(8,128)(2,1)S(1)}, bf16[512,128]{1,0:T(8,128)(2,1)S(1)}, u32[]{:S(2)}, u32[]{:S(2)}) collective-permute-start(bf16[512,128]{1,0:T(8,128)(2,1)S(1)} %get-tuple-element.49), channel_id=1, source_target_pairs={{0,24},{8,0},{16,8},{24,16},{1,25},{9,1},{17,9},{25,17},{2,26},{10... | collective-permute-start | bytes 393224 | tf_op jit(solution)/shard_map/ppermute | solution.py:463
  126.1 12.2 %all-to-all-start.4 = ((bf16[8,2,32,128]{3,2,1,0:T(8,128)(2,1)}), bf16[8,2,32,128]{3,2,1,0:T(8,128)(2,1)S(1)}, u32[]{:S(2)}, u32[]{:S(2)}) async-start(bf16[8,2,32,128]{3,2,1,0:T(8,128)(2,1)} %sum_groups.1), calls=%async_computation.4 | async-start | bytes 262144 | tf_op jit(solution)/shard_map/all_to_all | solution.py:524
  (18 other events, 206.0 us)

commit v4 on v3

--- a/solution.py
+++ b/solution.py
@@ -80,9 +80,8 @@
 
     return pl.pallas_call(
         kernel,
-        out_shape=jax.ShapeDtypeStruct(pieces.shape, BF16),
+        out_shape=pltpu.HBM(pieces.shape, BF16),
         in_specs=[WHOLE],
-        out_specs=WHOLE,
         compiler_params=params(4),
         name="strict_prefix",
     )(pieces)
@@ -131,51 +130,75 @@
 
 
 def pair_weight_grad(core, attended, attended_mate, grad, grad_mate, grad_scale):
-    width = attended.shape[1]
+    toks, width = attended.shape
     half = grad.shape[1] // 2
     rows = 512
 
-    def kernel(core_ref, a_ref, am_ref, g_ref, gm_ref, out_ref):
+    def kernel(core_ref, a_ref, am_ref, g_ref, gm_ref, out_ref, mate_buf, sem):
         features = pl.ds(pl.multiple_of(pl.program_id(0) * rows, rows), rows)
         columns = pl.ds(pl.multiple_of(core_ref[0] * half, half), half)
+        copy = pltpu.make_async_copy(gm_ref.at[:, columns], mate_buf, sem)
+        first = pl.program_id(0) == 0
+
+        @pl.when(first)
+        def _():
+            copy.start()
+
         total = mul(a_ref[:, features], g_ref[:, columns], 0, 0)
-        total = total + mul(am_ref[:, features], gm_ref[:, columns], 0, 0)
+
+        @pl.when(first)
+        def _():
+            copy.wait()
+
+        total = total + mul(am_ref[:, features], mate_buf[...], 0, 0)
         out_ref[...] = (total * grad_scale).astype(BF16)
 
     return pl.pallas_call(
         kernel,
         grid=(width // rows,),
-        in_specs=[SCALARS] + [WHOLE] * 4,
+        in_specs=[SCALARS] + [WHOLE] * 3 + [IN_PLACE],
         out_specs=pl.BlockSpec((rows, half), lambda i: (i, 0)),
         out_shape=pltpu.HBM((width, half), BF16),
-        compiler_params=params(12),
+        scratch_shapes=[pltpu.VMEM((toks, half), BF16), pltpu.SemaphoreType.DMA],
+        compiler_params=params(14),
         name="pair_weight_grad",
-    )(core, attended, attended_mate, grad, grad_mate)
+    )(core, attended, attended_mate, grad, in_hbm(grad_mate))
 
 
 def sum_plane(pieces):
     count, rows, width = pieces.shape
     keep = rows // 2
     slices = width // HEAD_DIM
-
-    def kernel(x_ref, out_ref):
-        for part in range(slices):
-            lanes = slice(part * HEAD_DIM, (part + 1) * HEAD_DIM)
-            total = x_ref[0, :, lanes].astype(F32)
+    parts = 4
+    span = width // parts
+
+    def kernel(x_ref, out_ref, buf, sems):
+        copies = []
+        for part in range(parts):
+            lanes = slice(part * span, (part + 1) * span)
+            copies.append(
+                pltpu.make_async_copy(x_ref.at[:, :, lanes], buf.at[:, :, lanes], sems.at[part])
+            )
+            copies[part].start()
+        for at_slice in range(slices):
+            if at_slice % (slices // parts) == 0:
+                copies[at_slice // (slices // parts)].wait()
+            lanes = head_lanes(at_slice)
+            total = buf[0, :, lanes].astype(F32)
             for at in range(1, count):
-                total = total + x_ref[at, :, lanes].astype(F32)
+                total = total + buf[at, :, lanes].astype(F32)
             total = total.astype(BF16)
-            out_ref[part, 0] = total[:keep]
-            out_ref[part, 1] = total[keep:]
-
-    return pl.pallas_call(
-        kernel,
+            out_ref[at_slice, 0] = total[:keep]
+            out_ref[at_slice, 1] = total[keep:]
+
+    return pl.pallas_call(
+        kernel,
+        in_specs=[IN_PLACE],
         out_shape=pltpu.HBM((slices, 2, keep, HEAD_DIM), BF16),
-        in_specs=[WHOLE],
-        out_specs=WHOLE,
-        compiler_params=params(4),
+        scratch_shapes=[pltpu.VMEM(pieces.shape, BF16), pltpu.SemaphoreType.DMA((parts,))],
+        compiler_params=params(8),
         name="sum_plane",
-    )(pieces)
+    )(in_hbm(pieces))
 
 
 def sum_groups(pieces):
@@ -428,7 +451,7 @@
 def later_grads(core, keys, values, key_local, value_local, keep, back, att_scale):
     toks, width = keys.shape
     heads = keep.shape[0] // HEAD_DIM
-    rows = 128
+    rows = 256
 
     def kernel(core_ref, k_ref, v_ref, dkl_ref, dvl_ref, keep_ref, back_ref, dk_ref, dv_ref):
         here = pl.ds(pl.multiple_of(pl.program_id(0) * rows, rows), rows)
@@ -496,26 +519,29 @@
     kv_before = lax.all_to_all(prefixes, CONTEXT, 0, 0).reshape(kv_block.shape)
 
     far_row = join_row(places, far_shard, far_shards)
-    kv_before = after(kv_before, low, high, far_row)
+    row_mate = swap_cores(row)
+    kv_before = after(kv_before, low, high, far_row, row_mate)
     attended = attended_states(queries, keys, values, kv_before, att_scale)
     attended_mate = swap_cores(attended)
     terms = pair_weight_grad(core_place, attended, attended_mate, grad, grad_mate, grad_scale)
     plane_terms = lax.all_to_all(terms.reshape(16, 64, half), PLANE, 0, 0)
 
     weight_mine = [row, low, far_row, high]
-    weight_mate = [swap_cores(after(part, terms)) for part in weight_mine]
+    weight_mate = [row_mate] + [swap_cores(after(part, terms)) for part in weight_mine[1:]]
     head_grad, mine, give, output = head_grads(
         after(places, terms), grad, queries, attended, weight_mine, weight_mate
     )
     mate = swap_cores(give)
     chip = chip_states(mine, mate)
-    row_state, later_here = row_states(places, chip, around(chip, "x", -1))
+    chip_pieces = around(chip, "x", -1)
     query_grad, key_local, value_local = local_grads(
         queries, keys, values, head_grad, kv_before, att_scale
     )
 
-    plane_terms = after(plane_terms, key_local, row_state)
-    plane_sum = sum_plane(plane_terms)
+    plane_sum = sum_plane(after(plane_terms, key_local))
+    chip_pieces = [after(piece, plane_sum) for piece in chip_pieces]
+    row_state, later_here = row_states(places, chip, chip_pieces)
+    plane_sum = after(plane_sum, row_state)
     group_terms = lax.all_to_all(plane_sum.reshape(16, 32, HEAD_DIM), ("z", "core"), 0, 0)
     row_pieces = around(after(row_state, plane_sum), "y", -1)
     keep, give = final_states(places, later_here, mine, mate, row_pieces)

time: 140 us -> 138 us (0.986)
    ppermute x15, waiting for transfers between devices: 17.8 us -> 14.9 us  [turn(): lax.ppermute(value, axis, [(at, (at + by) % count) for at in range(count)])]
    all_to_all x1, waiting for transfers between devices: 0.01 us -> 2.04 us  [on_device(): plane_terms = lax.all_to_all(terms.reshape(16, 64, half), PLANE, 0, 0)]
  transfers between devices with their start and end apart: 28 -> 28, of which waited for: 15 -> 14; matrix products, arithmetic and copies ran while one was open for 0% -> 0% of each run, Pallas kernels for 21% -> 22%
where the time goes in v4:
time: 138 us; the launch traced here: 137 us
  starting transfers between devices  60.9 us (44%)
  Pallas kernels  41.6 us (30%)
  waiting for transfers between devices  32 us (23%)
  local copies, waits for them, and re-layouts  1.66 us (1%)
    ppermute x15, starting transfers between devices, turn(): lax.ppermute(value, axis, [(at, (at + by) % count) for at in range(count)])  25.7 us
    ppermute x15, waiting for transfers between devices, turn(): lax.ppermute(value, axis, [(at, (at + by) % count) for at in range(count)])  14.9 us
    pallas_call x1, Pallas kernels, head_grads(): pl.pallas_call(kernel, in_specs=[SCALARS, IN_PLACE, IN_PLACE, WHOLE] + [I...  10.3 us
    all_to_all x1, starting transfers between devices, on_device(): lax.all_to_all(plane_sum.reshape(16, 32, HEAD_DIM), ('z', 'core'), 0, 0)  9.9 us
    pallas_call x1, Pallas kernels, local_grads(): pl.pallas_call(kernel, grid=(HEADS // group,), in_specs=[WHOLE] * 5, out_...  8.92 us
    ppermute x8, waiting for transfers between devices, swap_cores(): return lax.ppermute(value, 'core', [(0, 1), (1, 0)])  7.34 us
    ppermute x8, starting transfers between devices, swap_cores(): return lax.ppermute(value, 'core', [(0, 1), (1, 0)])  6.41 us
    all_to_all x1, starting transfers between devices, on_device(): pieces = lax.all_to_all(kv_block.reshape(32, -1, HEAD_DIM), CONTEXT, 0, 0)  5.74 us
  transfers between devices with their start and end apart: 28, of which 14 were waited for; matrix products, arithmetic and copies ran while one was open for 0% of the time, Pallas kernels for 22%

profile of v4, /device:TPU:1, one launch (start us, length us, event | category | flops | bytes accessed | tf_op | source)
XLA Modules:
  0.0 137.2 jit_solution(7783187733586929968)
XLA Ops:
  0.6 3.3 %collective-permute-start = (bf16[512,2048]{1,0:T(8,128)(2,1)}, bf16[512,2048]{1,0:T(8,128)(2,1)}, u32[]{:S(2)}, u32[]{:S(2)}) collective-permute-start(bf16[512,2048]{1,0:T(8,128)(2,1)} %bitcast.27), channel_id=1, source_target_pairs={{0,1},{1,0},{2,3},{3,2},{4,5},{5,4},{6,7},{7,6},{8,9},{9,8},{10,11... | collective-permute-start | bytes 6291464 | tf_op jit(solution)/shard_map/ppermute | solution.py:482
  4.0 2.6 %kv_states.1 = bf16[1024,128]{1,0:T(8,128)(2,1)} custom-call(bf16[512,1024]{1,0:T(8,128)(2,1)} %bitcast.16, bf16[512,1024]{1,0:T(8,128)(2,1)} %bitcast.20), custom_call_target="tpu_custom_call" | custom-call | tf_op jit(solution)/shard_map/kv_states/pallas_call | solution.py:59
  6.7 5.7 %all-to-all-start = ((bf16[32,32,128]{2,1,0:T(8,128)(2,1)}), bf16[32,32,128]{2,1,0:T(8,128)(2,1)S(1)}, u32[]{:S(2)}, u32[]{:S(2)}) async-start(bf16[32,32,128]{2,1,0:T(8,128)(2,1)} %bitcast.6), calls=%async_computation | async-start | bytes 524288 | tf_op jit(solution)/shard_map/all_to_all | solution.py:513
  12.4 3.0 %collective-permute-start.3 = (bf16[32,2048]{1,0:T(8,128)(2,1)S(1)}, bf16[32,2048]{1,0:T(8,128)(2,1)}, u32[]{:S(2)}, u32[]{:S(2)}) collective-permute-start(bf16[32,2048]{1,0:T(8,128)(2,1)S(1)} %copy-done.8), channel_id=1, source_target_pairs={{0,4},{2,6},{4,0},{6,2},{1,5},{3,7},{5,1},{7,3},{8,12},{10,14},{12... | collective-permute-start | bytes 393224 | tf_op jit(solution)/shard_map/ppermute | solution.py:486
  15.7 2.7 %collective-permute-start.1 = (bf16[32,2048]{1,0:T(8,128)(2,1)S(1)}, bf16[32,2048]{1,0:T(8,128)(2,1)}, u32[]{:S(2)}, u32[]{:S(2)}) collective-permute-start(bf16[32,2048]{1,0:T(8,128)(2,1)S(1)} %copy-done.8), channel_id=1, source_target_pairs={{0,16},{8,24},{16,0},{24,8},{1,17},{9,25},{17,1},{25,9},{2,18},{10... | collective-permute-start | bytes 393224 | tf_op jit(solution)/shard_map/ppermute | solution.py:486
  18.4 2.4 %collective-permute-start.4 = (bf16[32,2048]{1,0:T(8,128)(2,1)S(1)}, bf16[32,2048]{1,0:T(8,128)(2,1)}, u32[]{:S(2)}, u32[]{:S(2)}) collective-permute-start(bf16[32,2048]{1,0:T(8,128)(2,1)S(1)} %copy-done.8), channel_id=1, source_target_pairs={{0,6},{2,0},{4,2},{6,4},{1,7},{3,1},{5,3},{7,5},{8,14},{10,8},{12,... | collective-permute-start | bytes 393224 | tf_op jit(solution)/shard_map/ppermute | solution.py:486
  21.9 2.9 %collective-permute-done.2.a_ref = bf16[32,2048]{1,0:T(8,128)(2,1)} collective-permute-done((bf16[32,2048]{1,0:T(8,128)(2,1)S(1)}, bf16[32,2048]{1,0:T(8,128)(2,1)}, u32[]{:S(2)}, u32[]{:S(2)}) %collective-permute-start.2) | collective-permute-done | bytes 131104 | tf_op jit(solution)/shard_map/ppermute | solution.py:486
  28.0 2.5 %collective-permute-start.6 = (bf16[4,32,2048]{2,1,0:T(8,128)(2,1)}, bf16[4,32,2048]{2,1,0:T(8,128)(2,1)}, u32[]{:S(2)}, u32[]{:S(2)}) collective-permute-start(bf16[4,32,2048]{2,1,0:T(8,128)(2,1)} %join_row.2.refs_0_), channel_id=1, source_target_pairs={{0,24},{8,0},{16,8},{24,16},{1,25},{9,1},{17,9},{25,17},{2,26},{10... | collective-permute-start | bytes 1572872 | tf_op jit(solution)/shard_map/ppermute | solution.py:486
  32.3 5.2 %all-to-all-start.1 = ((bf16[32,32,128]{2,1,0:T(8,128)(2,1)}), bf16[32,32,128]{2,1,0:T(8,128)(2,1)S(1)}, u32[]{:S(2)}, u32[]{:S(2)}) async-start(bf16[32,32,128]{2,1,0:T(8,128)(2,1)} %strict_prefix.1), calls=%async_computation.1 | async-start | bytes 524288 | tf_op jit(solution)/shard_map/all_to_all | solution.py:519
  37.6 3.0 %collective-permute-start.8 = (bf16[32,2048]{1,0:T(8,128)(2,1)}, bf16[32,2048]{1,0:T(8,128)(2,1)S(1)}, u32[]{:S(2)}, u32[]{:S(2)}) collective-permute-start(bf16[32,2048]{1,0:T(8,128)(2,1)} %collective-permute-done.1.own_ref), channel_id=1, source_target_pairs={{0,4},{2,6},{4,0},{6,2},{1,5},{3,7},{5,1},{7,3},{8,12},{10,14},{12... | collective-permute-start | bytes 393224 | tf_op jit(solution)/shard_map/ppermute | solution.py:486
  40.9 6.1 %collective-permute-done.8.b_ref = bf16[32,2048]{1,0:T(8,128)(2,1)S(1)} collective-permute-done((bf16[32,2048]{1,0:T(8,128)(2,1)}, bf16[32,2048]{1,0:T(8,128)(2,1)S(1)}, u32[]{:S(2)}, u32[]{:S(2)}) %collective-permute-start.8) | collective-permute-done | bytes 131104 | tf_op jit(solution)/shard_map/ppermute | solution.py:486
  47.0 3.0 %collective-permute-done.7.a_ref = bf16[32,2048]{1,0:T(8,128)(2,1)S(1)} collective-permute-done((bf16[32,2048]{1,0:T(8,128)(2,1)}, bf16[32,2048]{1,0:T(8,128)(2,1)S(1)}, u32[]{:S(2)}, u32[]{:S(2)}) %collective-permute-start.7) | collective-permute-done | bytes 131104 | tf_op jit(solution)/shard_map/ppermute | solution.py:486
  51.8 2.5 %attended.1.a_ref = bf16[512,1024]{1,0:T(8,128)(2,1)S(1)} custom-call(bf16[512,1024]{1,0:T(8,128)(2,1)S(1)} %bitcast.25, bf16[512,1024]{1,0:T(8,128)(2,1)S(1)} %bitcast.17, bf16[512,1024]{1,0:T(8,128)(2,1)S(1)} %bitcast.21, bf16[1024,128]{1,0:T(8,128)(2,1)S(1)} %bitcast.30), custom_call_target="tpu_custom_call" | custom-call | tf_op jit(solution)/shard_map/attended/pallas_call | solution.py:122
  57.5 4.9 %pair_weight_grad.1 = bf16[1024,1024]{1,0:T(8,128)(2,1)} custom-call(s32[1]{0:T(128)} %bitcast.2.core_ref, bf16[512,1024]{1,0:T(8,128)(2,1)S(1)} %attended.1.a_ref, bf16[512,1024]{1,0:T(8,128)(2,1)S(1)} %collective-permute-done.11.am_ref, bf16[512,2048]{1,0:T(8,128)(2,1)S(1)} %bitcast.29, bf16[512,2048]{1,0:T(8,128)(2,1)} %collective-permute-done.gm_ref), custom_call_target="tpu_custom_call" | custom-call | tf_op jit(solution)/shard_map/pair_weight_grad/pallas_call | solution.py:156
  62.4 4.6 %all-to-all-start.2 = ((bf16[16,64,1024]{2,1,0:T(8,128)(2,1)}), bf16[16,64,1024]{2,1,0:T(8,128)(2,1)}, u32[]{:S(2)}, u32[]{:S(2)}) async-start(bf16[16,64,1024]{2,1,0:T(8,128)(2,1)} %bitcast.33), calls=%async_computation.2 | async-start | bytes 4194304 | tf_op jit(solution)/shard_map/all_to_all | solution.py:527
  71.6 10.3 %head_grads.1 = (bf16[512,1024]{1,0:T(8,128)(2,1)S(1)}, bf16[512,128]{1,0:T(8,128)(2,1)S(1)}, bf16[512,128]{1,0:T(8,128)(2,1)S(1)}, bf16[512,2048]{1,0:T(8,128)(2,1)}) custom-call(s32[3]{0:T(128)S(1)} %pad_add_fusion.place_ref, bf16[512,2048]{1,0:T(8,128)(2,1)} %bitcast.28, bf16[512,1024]{1,0:T(8,128)(2,1)} %bitcast.24, bf16[512,1024]{1,0:T(8,128)(2,1)S(1)} %copy-done.5, ...), custom_call_target="tpu_custom_call" | custom-call | tf_op jit(solution)/shard_map/head_grads/pallas_call | solution.py:322
  85.1 2.4 %collective-permute-start.17 = (bf16[512,128]{1,0:T(8,128)(2,1)S(1)}, bf16[512,128]{1,0:T(8,128)(2,1)S(1)}, u32[]{:S(2)}, u32[]{:S(2)}) collective-permute-start(bf16[512,128]{1,0:T(8,128)(2,1)S(1)} %chip_states.1.chip_ref), channel_id=1, source_target_pairs={{0,4},{2,6},{4,0},{6,2},{1,5},{3,7},{5,1},{7,3},{8,12},{10,14},{12... | collective-permute-start | bytes 393224 | tf_op jit(solution)/shard_map/ppermute | solution.py:486
  88.7 8.9 %local_grads.1 = (bf16[512,1024]{1,0:T(8,128)(2,1)}, f32[512,1024]{1,0:T(8,128)}, f32[512,1024]{1,0:T(8,128)}) custom-call(bf16[512,1024]{1,0:T(8,128)(2,1)S(1)} %bitcast.26, bf16[512,1024]{1,0:T(8,128)(2,1)S(1)} %bitcast.18, bf16[512,1024]{1,0:T(8,128)(2,1)S(1)} %bitcast.22, bf16[512,1024]{1,0:T(8,128)(2,1)S(1)} %get-tuple-element.42.g_ref, ...), custom_call_target="tpu_custom_call" | custom-call | tf_op jit(solution)/shard_map/local_grads/pallas_call | solution.py:436
  104.5 9.9 %all-to-all-start.3 = ((bf16[16,32,128]{2,1,0:T(8,128)(2,1)}), bf16[16,32,128]{2,1,0:T(8,128)(2,1)S(1)}, u32[]{:S(2)}, u32[]{:S(2)}) async-start(bf16[16,32,128]{2,1,0:T(8,128)(2,1)} %bitcast.34), calls=%async_computation.3 | async-start | bytes 262144 | tf_op jit(solution)/shard_map/all_to_all | solution.py:545
  114.5 2.7 %collective-permute-start.20 = (bf16[512,128]{1,0:T(8,128)(2,1)S(1)}, bf16[512,128]{1,0:T(8,128)(2,1)S(1)}, u32[]{:S(2)}, u32[]{:S(2)}) collective-permute-start(bf16[512,128]{1,0:T(8,128)(2,1)S(1)} %get-tuple-element.55), channel_id=1, source_target_pairs={{0,16},{8,24},{16,0},{24,8},{1,17},{9,25},{17,1},{25,9},{2,18},{10... | collective-permute-start | bytes 393224 | tf_op jit(solution)/shard_map/ppermute | solution.py:486
  118.9 4.7 %all-to-all-done.3 = bf16[16,32,128]{2,1,0:T(8,128)(2,1)S(1)} async-done(((bf16[16,32,128]{2,1,0:T(8,128)(2,1)}), bf16[16,32,128]{2,1,0:T(8,128)(2,1)S(1)}, u32[]{:S(2)}, u32[]{:S(2)}) %all-to-all-start.3) | async-done | bytes 131104 | tf_op jit(solution)/shard_map/all_to_all | solution.py:545
  124.2 3.4 %all-to-all-start.4 = ((bf16[8,2,32,128]{3,2,1,0:T(8,128)(2,1)}), bf16[8,2,32,128]{3,2,1,0:T(8,128)(2,1)S(1)}, u32[]{:S(2)}, u32[]{:S(2)}) async-start(bf16[8,2,32,128]{3,2,1,0:T(8,128)(2,1)} %sum_groups.1), calls=%async_computation.4 | async-start | bytes 262144 | tf_op jit(solution)/shard_map/all_to_all | solution.py:550
  129.8 3.7 %later_grads.1 = (bf16[512,1024]{1,0:T(8,128)(2,1)}, bf16[512,1024]{1,0:T(8,128)(2,1)}) custom-call(s32[1]{0:T(128)} %bitcast.2.core_ref, bf16[512,1024]{1,0:T(8,128)(2,1)S(1)} %bitcast.19, bf16[512,1024]{1,0:T(8,128)(2,1)S(1)} %bitcast.23, f32[512,1024]{1,0:T(8,128)} %get-tuple-element.44.dkl_ref, f32[512,1024]{1,0:T(8,128)} %get-tuple-element.45.dvl_ref, ...), custom_call_target="tpu_custom_call" | custom-call | tf_op jit(solution)/shard_map/later_grads/pallas_call | solution.py:470
  133.4 3.1 %all-to-all-done.4.x_ref = bf16[8,2,32,128]{3,2,1,0:T(8,128)(2,1)S(1)} async-done(((bf16[8,2,32,128]{3,2,1,0:T(8,128)(2,1)}), bf16[8,2,32,128]{3,2,1,0:T(8,128)(2,1)S(1)}, u32[]{:S(2)}, u32[]{:S(2)}) %all-to-all-start.4) | async-done | bytes 131104 | tf_op jit(solution)/shard_map/all_to_all | solution.py:550
  (72 shorter events, 32.9 us)
Async XLA Ops:
  0.6 24.1 %collective-permute-start = (bf16[512,2048]{1,0:T(8,128)(2,1)}, bf16[512,2048]{1,0:T(8,128)(2,1)}, u32[]{:S(2)}, u32[]{:S(2)}) collective-permute-start(bf16[512,2048]{1,0:T(8,128)(2,1)} %bitcast.27), channel_id=1, source_target_pairs={{0,1},{1,0},{2,3},{3,2},{4,5},{5,4},{6,7},{7,6},{8,9},{9,8},{10,11... | collective-permute-start | bytes 6291464 | tf_op jit(solution)/shard_map/ppermute | solution.py:482
  6.7 18.1 %all-to-all-start = ((bf16[32,32,128]{2,1,0:T(8,128)(2,1)}), bf16[32,32,128]{2,1,0:T(8,128)(2,1)S(1)}, u32[]{:S(2)}, u32[]{:S(2)}) async-start(bf16[32,32,128]{2,1,0:T(8,128)(2,1)} %bitcast.6), calls=%async_computation | async-start | bytes 524288 | tf_op jit(solution)/shard_map/all_to_all | solution.py:513
  12.4 9.5 %collective-permute-start.3 = (bf16[32,2048]{1,0:T(8,128)(2,1)S(1)}, bf16[32,2048]{1,0:T(8,128)(2,1)}, u32[]{:S(2)}, u32[]{:S(2)}) collective-permute-start(bf16[32,2048]{1,0:T(8,128)(2,1)S(1)} %copy-done.8), channel_id=1, source_target_pairs={{0,4},{2,6},{4,0},{6,2},{1,5},{3,7},{5,1},{7,3},{8,12},{10,14},{12... | collective-permute-start | bytes 393224 | tf_op jit(solution)/shard_map/ppermute | solution.py:486
  15.4 9.4 %collective-permute-start.2 = (bf16[32,2048]{1,0:T(8,128)(2,1)S(1)}, bf16[32,2048]{1,0:T(8,128)(2,1)}, u32[]{:S(2)}, u32[]{:S(2)}) collective-permute-start(bf16[32,2048]{1,0:T(8,128)(2,1)S(1)} %copy-done.8), channel_id=1, source_target_pairs={{0,2},{2,4},{4,6},{6,0},{1,3},{3,5},{5,7},{7,1},{8,10},{10,12},{12... | collective-permute-start | bytes 393224 | tf_op jit(solution)/shard_map/ppermute | solution.py:486
  15.7 9.1 %collective-permute-start.1 = (bf16[32,2048]{1,0:T(8,128)(2,1)S(1)}, bf16[32,2048]{1,0:T(8,128)(2,1)}, u32[]{:S(2)}, u32[]{:S(2)}) collective-permute-start(bf16[32,2048]{1,0:T(8,128)(2,1)S(1)} %copy-done.8), channel_id=1, source_target_pairs={{0,16},{8,24},{16,0},{24,8},{1,17},{9,25},{17,1},{25,9},{2,18},{10... | collective-permute-start | bytes 393224 | tf_op jit(solution)/shard_map/ppermute | solution.py:486
  18.4 6.4 %collective-permute-start.4 = (bf16[32,2048]{1,0:T(8,128)(2,1)S(1)}, bf16[32,2048]{1,0:T(8,128)(2,1)}, u32[]{:S(2)}, u32[]{:S(2)}) collective-permute-start(bf16[32,2048]{1,0:T(8,128)(2,1)S(1)} %copy-done.8), channel_id=1, source_target_pairs={{0,6},{2,0},{4,2},{6,4},{1,7},{3,1},{5,3},{7,5},{8,14},{10,8},{12,... | collective-permute-start | bytes 393224 | tf_op jit(solution)/shard_map/ppermute | solution.py:486
  27.4 24.3 %collective-permute-start.10 = (bf16[4,32,2048]{2,1,0:T(8,128)(2,1)}, bf16[4,32,2048]{2,1,0:T(8,128)(2,1)}, u32[]{:S(2)}, u32[]{:S(2)}) collective-permute-start(bf16[4,32,2048]{2,1,0:T(8,128)(2,1)} %join_row.2.refs_0_), channel_id=1, source_target_pairs={{0,1},{1,0},{2,3},{3,2},{4,5},{5,4},{6,7},{7,6},{8,9},{9,8},{10,11... | collective-permute-start | bytes 1572872 | tf_op jit(solution)/shard_map/ppermute | solution.py:482
  28.0 23.7 %collective-permute-start.6 = (bf16[4,32,2048]{2,1,0:T(8,128)(2,1)}, bf16[4,32,2048]{2,1,0:T(8,128)(2,1)}, u32[]{:S(2)}, u32[]{:S(2)}) collective-permute-start(bf16[4,32,2048]{2,1,0:T(8,128)(2,1)} %join_row.2.refs_0_), channel_id=1, source_target_pairs={{0,24},{8,0},{16,8},{24,16},{1,25},{9,1},{17,9},{25,17},{2,26},{10... | collective-permute-start | bytes 1572872 | tf_op jit(solution)/shard_map/ppermute | solution.py:486
  30.5 21.3 %collective-permute-start.5 = (bf16[4,32,2048]{2,1,0:T(8,128)(2,1)}, bf16[4,32,2048]{2,1,0:T(8,128)(2,1)}, u32[]{:S(2)}, u32[]{:S(2)}) collective-permute-start(bf16[4,32,2048]{2,1,0:T(8,128)(2,1)} %join_row.2.refs_0_), channel_id=1, source_target_pairs={{0,8},{8,16},{16,24},{24,0},{1,9},{9,17},{17,25},{25,1},{2,10},{10... | collective-permute-start | bytes 1572872 | tf_op jit(solution)/shard_map/ppermute | solution.py:486
  30.5 10.1 %collective-permute-start.9 = (bf16[32,2048]{1,0:T(8,128)(2,1)}, bf16[32,2048]{1,0:T(8,128)(2,1)S(1)}, u32[]{:S(2)}, u32[]{:S(2)}) collective-permute-start(bf16[32,2048]{1,0:T(8,128)(2,1)} %collective-permute-done.1.own_ref), channel_id=1, source_target_pairs={{0,6},{2,0},{4,2},{6,4},{1,7},{3,1},{5,3},{7,5},{8,14},{10,8},{12,... | collective-permute-start | bytes 393224 | tf_op jit(solution)/shard_map/ppermute | solution.py:486
  32.3 19.4 %all-to-all-start.1 = ((bf16[32,32,128]{2,1,0:T(8,128)(2,1)}), bf16[32,32,128]{2,1,0:T(8,128)(2,1)S(1)}, u32[]{:S(2)}, u32[]{:S(2)}) async-start(bf16[32,32,128]{2,1,0:T(8,128)(2,1)} %strict_prefix.1), calls=%async_computation.1 | async-start | bytes 524288 | tf_op jit(solution)/shard_map/all_to_all | solution.py:519
  37.6 9.4 %collective-permute-start.8 = (bf16[32,2048]{1,0:T(8,128)(2,1)}, bf16[32,2048]{1,0:T(8,128)(2,1)S(1)}, u32[]{:S(2)}, u32[]{:S(2)}) collective-permute-start(bf16[32,2048]{1,0:T(8,128)(2,1)} %collective-permute-done.1.own_ref), channel_id=1, source_target_pairs={{0,4},{2,6},{4,0},{6,2},{1,5},{3,7},{5,1},{7,3},{8,12},{10,14},{12... | collective-permute-start | bytes 393224 | tf_op jit(solution)/shard_map/ppermute | solution.py:486
  40.6 9.4 %collective-permute-start.7 = (bf16[32,2048]{1,0:T(8,128)(2,1)}, bf16[32,2048]{1,0:T(8,128)(2,1)S(1)}, u32[]{:S(2)}, u32[]{:S(2)}) collective-permute-start(bf16[32,2048]{1,0:T(8,128)(2,1)} %collective-permute-done.1.own_ref), channel_id=1, source_target_pairs={{0,2},{2,4},{4,6},{6,0},{1,3},{3,5},{5,7},{7,1},{8,10},{10,12},{12... | collective-permute-start | bytes 393224 | tf_op jit(solution)/shard_map/ppermute | solution.py:486
  54.3 3.1 %collective-permute-start.11 = (bf16[512,1024]{1,0:T(8,128)(2,1)S(1)}, bf16[512,1024]{1,0:T(8,128)(2,1)S(1)}, u32[]{:S(2)}, u32[]{:S(2)}) collective-permute-start(bf16[512,1024]{1,0:T(8,128)(2,1)S(1)} %attended.1.a_ref), channel_id=1, source_target_pairs={{0,1},{1,0},{2,3},{3,2},{4,5},{5,4},{6,7},{7,6},{8,9},{9,8},{10,11... | collective-permute-start | bytes 3145736 | tf_op jit(solution)/shard_map/ppermute | solution.py:482
  62.4 37.2 %all-to-all-start.2 = ((bf16[16,64,1024]{2,1,0:T(8,128)(2,1)}), bf16[16,64,1024]{2,1,0:T(8,128)(2,1)}, u32[]{:S(2)}, u32[]{:S(2)}) async-start(bf16[16,64,1024]{2,1,0:T(8,128)(2,1)} %bitcast.33), calls=%async_computation.2 | async-start | bytes 4194304 | tf_op jit(solution)/shard_map/all_to_all | solution.py:527
  67.7 3.1 %collective-permute-start.14 = (bf16[4,32,2048]{2,1,0:T(8,128)(2,1)}, bf16[4,32,2048]{2,1,0:T(8,128)(2,1)S(1)}, u32[]{:S(2)}, u32[]{:S(2)}) collective-permute-start(bf16[4,32,2048]{2,1,0:T(8,128)(2,1)} %collective-permute-done.6.refs_3_), channel_id=1, source_target_pairs={{0,1},{1,0},{2,3},{3,2},{4,5},{5,4},{6,7},{7,6},{8,9},{9,8},{10,11... | collective-permute-start | bytes 1572872 | tf_op jit(solution)/shard_map/ppermute | solution.py:482
  83.4 18.6 %collective-permute-start.18 = (bf16[512,128]{1,0:T(8,128)(2,1)S(1)}, bf16[512,128]{1,0:T(8,128)(2,1)S(1)}, u32[]{:S(2)}, u32[]{:S(2)}) collective-permute-start(bf16[512,128]{1,0:T(8,128)(2,1)S(1)} %chip_states.1.chip_ref), channel_id=1, source_target_pairs={{0,2},{2,4},{4,6},{6,0},{1,3},{3,5},{5,7},{7,1},{8,10},{10,12},{12... | collective-permute-start | bytes 393224 | tf_op jit(solution)/shard_map/ppermute | solution.py:486
  85.1 18.7 %collective-permute-start.17 = (bf16[512,128]{1,0:T(8,128)(2,1)S(1)}, bf16[512,128]{1,0:T(8,128)(2,1)S(1)}, u32[]{:S(2)}, u32[]{:S(2)}) collective-permute-start(bf16[512,128]{1,0:T(8,128)(2,1)S(1)} %chip_states.1.chip_ref), channel_id=1, source_target_pairs={{0,4},{2,6},{4,0},{6,2},{1,5},{3,7},{5,1},{7,3},{8,12},{10,14},{12... | collective-permute-start | bytes 393224 | tf_op jit(solution)/shard_map/ppermute | solution.py:486
  87.5 16.3 %collective-permute-start.16 = (bf16[512,128]{1,0:T(8,128)(2,1)S(1)}, bf16[512,128]{1,0:T(8,128)(2,1)S(1)}, u32[]{:S(2)}, u32[]{:S(2)}) collective-permute-start(bf16[512,128]{1,0:T(8,128)(2,1)S(1)} %chip_states.1.chip_ref), channel_id=1, source_target_pairs={{0,6},{2,0},{4,2},{6,4},{1,7},{3,1},{5,3},{7,5},{8,14},{10,8},{12,... | collective-permute-start | bytes 393224 | tf_op jit(solution)/shard_map/ppermute | solution.py:486
  104.5 19.1 %all-to-all-start.3 = ((bf16[16,32,128]{2,1,0:T(8,128)(2,1)}), bf16[16,32,128]{2,1,0:T(8,128)(2,1)S(1)}, u32[]{:S(2)}, u32[]{:S(2)}) async-start(bf16[16,32,128]{2,1,0:T(8,128)(2,1)} %bitcast.34), calls=%async_computation.3 | async-start | bytes 262144 | tf_op jit(solution)/shard_map/all_to_all | solution.py:545
  114.4 13.2 %collective-permute-start.21 = (bf16[512,128]{1,0:T(8,128)(2,1)S(1)}, bf16[512,128]{1,0:T(8,128)(2,1)S(1)}, u32[]{:S(2)}, u32[]{:S(2)}) collective-permute-start(bf16[512,128]{1,0:T(8,128)(2,1)S(1)} %get-tuple-element.55), channel_id=1, source_target_pairs={{0,8},{8,16},{16,24},{24,0},{1,9},{9,17},{17,25},{25,1},{2,10},{10... | collective-permute-start | bytes 393224 | tf_op jit(solution)/shard_map/ppermute | solution.py:486
  114.5 13.1 %collective-permute-start.20 = (bf16[512,128]{1,0:T(8,128)(2,1)S(1)}, bf16[512,128]{1,0:T(8,128)(2,1)S(1)}, u32[]{:S(2)}, u32[]{:S(2)}) collective-permute-start(bf16[512,128]{1,0:T(8,128)(2,1)S(1)} %get-tuple-element.55), channel_id=1, source_target_pairs={{0,16},{8,24},{16,0},{24,8},{1,17},{9,25},{17,1},{25,9},{2,18},{10... | collective-permute-start | bytes 393224 | tf_op jit(solution)/shard_map/ppermute | solution.py:486
  117.1 10.5 %collective-permute-start.19 = (bf16[512,128]{1,0:T(8,128)(2,1)S(1)}, bf16[512,128]{1,0:T(8,128)(2,1)S(1)}, u32[]{:S(2)}, u32[]{:S(2)}) collective-permute-start(bf16[512,128]{1,0:T(8,128)(2,1)S(1)} %get-tuple-element.55), channel_id=1, source_target_pairs={{0,24},{8,0},{16,8},{24,16},{1,25},{9,1},{17,9},{25,17},{2,26},{10... | collective-permute-start | bytes 393224 | tf_op jit(solution)/shard_map/ppermute | solution.py:486
  124.2 12.2 %all-to-all-start.4 = ((bf16[8,2,32,128]{3,2,1,0:T(8,128)(2,1)}), bf16[8,2,32,128]{3,2,1,0:T(8,128)(2,1)S(1)}, u32[]{:S(2)}, u32[]{:S(2)}) async-start(bf16[8,2,32,128]{3,2,1,0:T(8,128)(2,1)} %sum_groups.1), calls=%async_computation.4 | async-start | bytes 262144 | tf_op jit(solution)/shard_map/all_to_all | solution.py:550
  (16 other events, 203.4 us)

commit v5 on v4

--- a/solution.py
+++ b/solution.py
@@ -169,7 +169,7 @@
     count, rows, width = pieces.shape
     keep = rows // 2
     slices = width // HEAD_DIM
-    parts = 4
+    parts = 8
     span = width // parts
 
     def kernel(x_ref, out_ref, buf, sems):

time: 138 us -> 138 us (level)
  no operation moved by 1% of the time
where the time goes in v5:
time: 138 us; the launch traced here: 137 us
  starting transfers between devices  60.9 us (44%)
  Pallas kernels  41.6 us (30%)
  waiting for transfers between devices  32 us (23%)
  local copies, waits for them, and re-layouts  1.66 us (1%)
    ppermute x15, starting transfers between devices, turn(): lax.ppermute(value, axis, [(at, (at + by) % count) for at in range(count)])  25.7 us
    ppermute x15, waiting for transfers between devices, turn(): lax.ppermute(value, axis, [(at, (at + by) % count) for at in range(count)])  14.8 us
    pallas_call x1, Pallas kernels, head_grads(): pl.pallas_call(kernel, in_specs=[SCALARS, IN_PLACE, IN_PLACE, WHOLE] + [I...  10.3 us
    all_to_all x1, starting transfers between devices, on_device(): lax.all_to_all(plane_sum.reshape(16, 32, HEAD_DIM), ('z', 'core'), 0, 0)  9.9 us
    pallas_call x1, Pallas kernels, local_grads(): pl.pallas_call(kernel, grid=(HEADS // group,), in_specs=[WHOLE] * 5, out_...  8.92 us
    ppermute x8, waiting for transfers between devices, swap_cores(): return lax.ppermute(value, 'core', [(0, 1), (1, 0)])  7.34 us
    ppermute x8, starting transfers between devices, swap_cores(): return lax.ppermute(value, 'core', [(0, 1), (1, 0)])  6.41 us
    all_to_all x1, starting transfers between devices, on_device(): pieces = lax.all_to_all(kv_block.reshape(32, -1, HEAD_DIM), CONTEXT, 0, 0)  5.74 us
  transfers between devices with their start and end apart: 28, of which 14 were waited for; matrix products, arithmetic and copies ran while one was open for 0% of the time, Pallas kernels for 22%

profile of v5, /device:TPU:1, one launch (start us, length us, event | category | flops | bytes accessed | tf_op | source)
XLA Modules:
  0.0 137.2 jit_solution(2074573925457382389)
XLA Ops:
  0.6 3.3 %collective-permute-start = (bf16[512,2048]{1,0:T(8,128)(2,1)}, bf16[512,2048]{1,0:T(8,128)(2,1)}, u32[]{:S(2)}, u32[]{:S(2)}) collective-permute-start(bf16[512,2048]{1,0:T(8,128)(2,1)} %bitcast.27), channel_id=1, source_target_pairs={{0,1},{1,0},{2,3},{3,2},{4,5},{5,4},{6,7},{7,6},{8,9},{9,8},{10,11... | collective-permute-start | bytes 6291464 | tf_op jit(solution)/shard_map/ppermute | solution.py:482
  4.0 2.6 %kv_states.1 = bf16[1024,128]{1,0:T(8,128)(2,1)} custom-call(bf16[512,1024]{1,0:T(8,128)(2,1)} %bitcast.16, bf16[512,1024]{1,0:T(8,128)(2,1)} %bitcast.20), custom_call_target="tpu_custom_call" | custom-call | tf_op jit(solution)/shard_map/kv_states/pallas_call | solution.py:59
  6.7 5.7 %all-to-all-start = ((bf16[32,32,128]{2,1,0:T(8,128)(2,1)}), bf16[32,32,128]{2,1,0:T(8,128)(2,1)S(1)}, u32[]{:S(2)}, u32[]{:S(2)}) async-start(bf16[32,32,128]{2,1,0:T(8,128)(2,1)} %bitcast.6), calls=%async_computation | async-start | bytes 524288 | tf_op jit(solution)/shard_map/all_to_all | solution.py:513
  12.4 3.0 %collective-permute-start.3 = (bf16[32,2048]{1,0:T(8,128)(2,1)S(1)}, bf16[32,2048]{1,0:T(8,128)(2,1)}, u32[]{:S(2)}, u32[]{:S(2)}) collective-permute-start(bf16[32,2048]{1,0:T(8,128)(2,1)S(1)} %copy-done.8), channel_id=1, source_target_pairs={{0,4},{2,6},{4,0},{6,2},{1,5},{3,7},{5,1},{7,3},{8,12},{10,14},{12... | collective-permute-start | bytes 393224 | tf_op jit(solution)/shard_map/ppermute | solution.py:486
  15.7 2.7 %collective-permute-start.1 = (bf16[32,2048]{1,0:T(8,128)(2,1)S(1)}, bf16[32,2048]{1,0:T(8,128)(2,1)}, u32[]{:S(2)}, u32[]{:S(2)}) collective-permute-start(bf16[32,2048]{1,0:T(8,128)(2,1)S(1)} %copy-done.8), channel_id=1, source_target_pairs={{0,16},{8,24},{16,0},{24,8},{1,17},{9,25},{17,1},{25,9},{2,18},{10... | collective-permute-start | bytes 393224 | tf_op jit(solution)/shard_map/ppermute | solution.py:486
  18.4 2.4 %collective-permute-start.4 = (bf16[32,2048]{1,0:T(8,128)(2,1)S(1)}, bf16[32,2048]{1,0:T(8,128)(2,1)}, u32[]{:S(2)}, u32[]{:S(2)}) collective-permute-start(bf16[32,2048]{1,0:T(8,128)(2,1)S(1)} %copy-done.8), channel_id=1, source_target_pairs={{0,6},{2,0},{4,2},{6,4},{1,7},{3,1},{5,3},{7,5},{8,14},{10,8},{12,... | collective-permute-start | bytes 393224 | tf_op jit(solution)/shard_map/ppermute | solution.py:486
  21.9 2.9 %collective-permute-done.2.a_ref = bf16[32,2048]{1,0:T(8,128)(2,1)} collective-permute-done((bf16[32,2048]{1,0:T(8,128)(2,1)S(1)}, bf16[32,2048]{1,0:T(8,128)(2,1)}, u32[]{:S(2)}, u32[]{:S(2)}) %collective-permute-start.2) | collective-permute-done | bytes 131104 | tf_op jit(solution)/shard_map/ppermute | solution.py:486
  28.0 2.5 %collective-permute-start.6 = (bf16[4,32,2048]{2,1,0:T(8,128)(2,1)}, bf16[4,32,2048]{2,1,0:T(8,128)(2,1)}, u32[]{:S(2)}, u32[]{:S(2)}) collective-permute-start(bf16[4,32,2048]{2,1,0:T(8,128)(2,1)} %join_row.2.refs_0_), channel_id=1, source_target_pairs={{0,24},{8,0},{16,8},{24,16},{1,25},{9,1},{17,9},{25,17},{2,26},{10... | collective-permute-start | bytes 1572872 | tf_op jit(solution)/shard_map/ppermute | solution.py:486
  32.3 5.2 %all-to-all-start.1 = ((bf16[32,32,128]{2,1,0:T(8,128)(2,1)}), bf16[32,32,128]{2,1,0:T(8,128)(2,1)S(1)}, u32[]{:S(2)}, u32[]{:S(2)}) async-start(bf16[32,32,128]{2,1,0:T(8,128)(2,1)} %strict_prefix.1), calls=%async_computation.1 | async-start | bytes 524288 | tf_op jit(solution)/shard_map/all_to_all | solution.py:519
  37.6 3.0 %collective-permute-start.8 = (bf16[32,2048]{1,0:T(8,128)(2,1)}, bf16[32,2048]{1,0:T(8,128)(2,1)S(1)}, u32[]{:S(2)}, u32[]{:S(2)}) collective-permute-start(bf16[32,2048]{1,0:T(8,128)(2,1)} %collective-permute-done.1.own_ref), channel_id=1, source_target_pairs={{0,4},{2,6},{4,0},{6,2},{1,5},{3,7},{5,1},{7,3},{8,12},{10,14},{12... | collective-permute-start | bytes 393224 | tf_op jit(solution)/shard_map/ppermute | solution.py:486
  40.9 6.1 %collective-permute-done.8.b_ref = bf16[32,2048]{1,0:T(8,128)(2,1)S(1)} collective-permute-done((bf16[32,2048]{1,0:T(8,128)(2,1)}, bf16[32,2048]{1,0:T(8,128)(2,1)S(1)}, u32[]{:S(2)}, u32[]{:S(2)}) %collective-permute-start.8) | collective-permute-done | bytes 131104 | tf_op jit(solution)/shard_map/ppermute | solution.py:486
  47.0 3.0 %collective-permute-done.7.a_ref = bf16[32,2048]{1,0:T(8,128)(2,1)S(1)} collective-permute-done((bf16[32,2048]{1,0:T(8,128)(2,1)}, bf16[32,2048]{1,0:T(8,128)(2,1)S(1)}, u32[]{:S(2)}, u32[]{:S(2)}) %collective-permute-start.7) | collective-permute-done | bytes 131104 | tf_op jit(solution)/shard_map/ppermute | solution.py:486
  51.8 2.5 %attended.1.a_ref = bf16[512,1024]{1,0:T(8,128)(2,1)S(1)} custom-call(bf16[512,1024]{1,0:T(8,128)(2,1)S(1)} %bitcast.25, bf16[512,1024]{1,0:T(8,128)(2,1)S(1)} %bitcast.17, bf16[512,1024]{1,0:T(8,128)(2,1)S(1)} %bitcast.21, bf16[1024,128]{1,0:T(8,128)(2,1)S(1)} %bitcast.30), custom_call_target="tpu_custom_call" | custom-call | tf_op jit(solution)/shard_map/attended/pallas_call | solution.py:122
  57.5 4.9 %pair_weight_grad.1 = bf16[1024,1024]{1,0:T(8,128)(2,1)} custom-call(s32[1]{0:T(128)} %bitcast.2.core_ref, bf16[512,1024]{1,0:T(8,128)(2,1)S(1)} %attended.1.a_ref, bf16[512,1024]{1,0:T(8,128)(2,1)S(1)} %collective-permute-done.11.am_ref, bf16[512,2048]{1,0:T(8,128)(2,1)S(1)} %bitcast.29, bf16[512,2048]{1,0:T(8,128)(2,1)} %collective-permute-done.gm_ref), custom_call_target="tpu_custom_call" | custom-call | tf_op jit(solution)/shard_map/pair_weight_grad/pallas_call | solution.py:156
  62.4 4.6 %all-to-all-start.2 = ((bf16[16,64,1024]{2,1,0:T(8,128)(2,1)}), bf16[16,64,1024]{2,1,0:T(8,128)(2,1)}, u32[]{:S(2)}, u32[]{:S(2)}) async-start(bf16[16,64,1024]{2,1,0:T(8,128)(2,1)} %bitcast.33), calls=%async_computation.2 | async-start | bytes 4194304 | tf_op jit(solution)/shard_map/all_to_all | solution.py:527
  71.6 10.3 %head_grads.1 = (bf16[512,1024]{1,0:T(8,128)(2,1)S(1)}, bf16[512,128]{1,0:T(8,128)(2,1)S(1)}, bf16[512,128]{1,0:T(8,128)(2,1)S(1)}, bf16[512,2048]{1,0:T(8,128)(2,1)}) custom-call(s32[3]{0:T(128)S(1)} %pad_add_fusion.place_ref, bf16[512,2048]{1,0:T(8,128)(2,1)} %bitcast.28, bf16[512,1024]{1,0:T(8,128)(2,1)} %bitcast.24, bf16[512,1024]{1,0:T(8,128)(2,1)S(1)} %copy-done.5, ...), custom_call_target="tpu_custom_call" | custom-call | tf_op jit(solution)/shard_map/head_grads/pallas_call | solution.py:322
  85.1 2.4 %collective-permute-start.17 = (bf16[512,128]{1,0:T(8,128)(2,1)S(1)}, bf16[512,128]{1,0:T(8,128)(2,1)S(1)}, u32[]{:S(2)}, u32[]{:S(2)}) collective-permute-start(bf16[512,128]{1,0:T(8,128)(2,1)S(1)} %chip_states.1.chip_ref), channel_id=1, source_target_pairs={{0,4},{2,6},{4,0},{6,2},{1,5},{3,7},{5,1},{7,3},{8,12},{10,14},{12... | collective-permute-start | bytes 393224 | tf_op jit(solution)/shard_map/ppermute | solution.py:486
  88.7 8.9 %local_grads.1 = (bf16[512,1024]{1,0:T(8,128)(2,1)}, f32[512,1024]{1,0:T(8,128)}, f32[512,1024]{1,0:T(8,128)}) custom-call(bf16[512,1024]{1,0:T(8,128)(2,1)S(1)} %bitcast.26, bf16[512,1024]{1,0:T(8,128)(2,1)S(1)} %bitcast.18, bf16[512,1024]{1,0:T(8,128)(2,1)S(1)} %bitcast.22, bf16[512,1024]{1,0:T(8,128)(2,1)S(1)} %get-tuple-element.42.g_ref, ...), custom_call_target="tpu_custom_call" | custom-call | tf_op jit(solution)/shard_map/local_grads/pallas_call | solution.py:436
  104.5 9.9 %all-to-all-start.3 = ((bf16[16,32,128]{2,1,0:T(8,128)(2,1)}), bf16[16,32,128]{2,1,0:T(8,128)(2,1)S(1)}, u32[]{:S(2)}, u32[]{:S(2)}) async-start(bf16[16,32,128]{2,1,0:T(8,128)(2,1)} %bitcast.34), calls=%async_computation.3 | async-start | bytes 262144 | tf_op jit(solution)/shard_map/all_to_all | solution.py:545
  114.5 2.7 %collective-permute-start.20 = (bf16[512,128]{1,0:T(8,128)(2,1)S(1)}, bf16[512,128]{1,0:T(8,128)(2,1)S(1)}, u32[]{:S(2)}, u32[]{:S(2)}) collective-permute-start(bf16[512,128]{1,0:T(8,128)(2,1)S(1)} %get-tuple-element.55), channel_id=1, source_target_pairs={{0,16},{8,24},{16,0},{24,8},{1,17},{9,25},{17,1},{25,9},{2,18},{10... | collective-permute-start | bytes 393224 | tf_op jit(solution)/shard_map/ppermute | solution.py:486
  118.9 4.7 %all-to-all-done.3 = bf16[16,32,128]{2,1,0:T(8,128)(2,1)S(1)} async-done(((bf16[16,32,128]{2,1,0:T(8,128)(2,1)}), bf16[16,32,128]{2,1,0:T(8,128)(2,1)S(1)}, u32[]{:S(2)}, u32[]{:S(2)}) %all-to-all-start.3) | async-done | bytes 131104 | tf_op jit(solution)/shard_map/all_to_all | solution.py:545
  124.2 3.4 %all-to-all-start.4 = ((bf16[8,2,32,128]{3,2,1,0:T(8,128)(2,1)}), bf16[8,2,32,128]{3,2,1,0:T(8,128)(2,1)S(1)}, u32[]{:S(2)}, u32[]{:S(2)}) async-start(bf16[8,2,32,128]{3,2,1,0:T(8,128)(2,1)} %sum_groups.1), calls=%async_computation.4 | async-start | bytes 262144 | tf_op jit(solution)/shard_map/all_to_all | solution.py:550
  129.8 3.7 %later_grads.1 = (bf16[512,1024]{1,0:T(8,128)(2,1)}, bf16[512,1024]{1,0:T(8,128)(2,1)}) custom-call(s32[1]{0:T(128)} %bitcast.2.core_ref, bf16[512,1024]{1,0:T(8,128)(2,1)S(1)} %bitcast.19, bf16[512,1024]{1,0:T(8,128)(2,1)S(1)} %bitcast.23, f32[512,1024]{1,0:T(8,128)} %get-tuple-element.44.dkl_ref, f32[512,1024]{1,0:T(8,128)} %get-tuple-element.45.dvl_ref, ...), custom_call_target="tpu_custom_call" | custom-call | tf_op jit(solution)/shard_map/later_grads/pallas_call | solution.py:470
  133.4 3.1 %all-to-all-done.4.x_ref = bf16[8,2,32,128]{3,2,1,0:T(8,128)(2,1)S(1)} async-done(((bf16[8,2,32,128]{3,2,1,0:T(8,128)(2,1)}), bf16[8,2,32,128]{3,2,1,0:T(8,128)(2,1)S(1)}, u32[]{:S(2)}, u32[]{:S(2)}) %all-to-all-start.4) | async-done | bytes 131104 | tf_op jit(solution)/shard_map/all_to_all | solution.py:550
  (72 shorter events, 32.9 us)
Async XLA Ops:
  0.6 24.1 %collective-permute-start = (bf16[512,2048]{1,0:T(8,128)(2,1)}, bf16[512,2048]{1,0:T(8,128)(2,1)}, u32[]{:S(2)}, u32[]{:S(2)}) collective-permute-start(bf16[512,2048]{1,0:T(8,128)(2,1)} %bitcast.27), channel_id=1, source_target_pairs={{0,1},{1,0},{2,3},{3,2},{4,5},{5,4},{6,7},{7,6},{8,9},{9,8},{10,11... | collective-permute-start | bytes 6291464 | tf_op jit(solution)/shard_map/ppermute | solution.py:482
  6.7 18.1 %all-to-all-start = ((bf16[32,32,128]{2,1,0:T(8,128)(2,1)}), bf16[32,32,128]{2,1,0:T(8,128)(2,1)S(1)}, u32[]{:S(2)}, u32[]{:S(2)}) async-start(bf16[32,32,128]{2,1,0:T(8,128)(2,1)} %bitcast.6), calls=%async_computation | async-start | bytes 524288 | tf_op jit(solution)/shard_map/all_to_all | solution.py:513
  12.4 9.5 %collective-permute-start.3 = (bf16[32,2048]{1,0:T(8,128)(2,1)S(1)}, bf16[32,2048]{1,0:T(8,128)(2,1)}, u32[]{:S(2)}, u32[]{:S(2)}) collective-permute-start(bf16[32,2048]{1,0:T(8,128)(2,1)S(1)} %copy-done.8), channel_id=1, source_target_pairs={{0,4},{2,6},{4,0},{6,2},{1,5},{3,7},{5,1},{7,3},{8,12},{10,14},{12... | collective-permute-start | bytes 393224 | tf_op jit(solution)/shard_map/ppermute | solution.py:486
  15.4 9.4 %collective-permute-start.2 = (bf16[32,2048]{1,0:T(8,128)(2,1)S(1)}, bf16[32,2048]{1,0:T(8,128)(2,1)}, u32[]{:S(2)}, u32[]{:S(2)}) collective-permute-start(bf16[32,2048]{1,0:T(8,128)(2,1)S(1)} %copy-done.8), channel_id=1, source_target_pairs={{0,2},{2,4},{4,6},{6,0},{1,3},{3,5},{5,7},{7,1},{8,10},{10,12},{12... | collective-permute-start | bytes 393224 | tf_op jit(solution)/shard_map/ppermute | solution.py:486
  15.7 9.1 %collective-permute-start.1 = (bf16[32,2048]{1,0:T(8,128)(2,1)S(1)}, bf16[32,2048]{1,0:T(8,128)(2,1)}, u32[]{:S(2)}, u32[]{:S(2)}) collective-permute-start(bf16[32,2048]{1,0:T(8,128)(2,1)S(1)} %copy-done.8), channel_id=1, source_target_pairs={{0,16},{8,24},{16,0},{24,8},{1,17},{9,25},{17,1},{25,9},{2,18},{10... | collective-permute-start | bytes 393224 | tf_op jit(solution)/shard_map/ppermute | solution.py:486
  18.4 6.4 %collective-permute-start.4 = (bf16[32,2048]{1,0:T(8,128)(2,1)S(1)}, bf16[32,2048]{1,0:T(8,128)(2,1)}, u32[]{:S(2)}, u32[]{:S(2)}) collective-permute-start(bf16[32,2048]{1,0:T(8,128)(2,1)S(1)} %copy-done.8), channel_id=1, source_target_pairs={{0,6},{2,0},{4,2},{6,4},{1,7},{3,1},{5,3},{7,5},{8,14},{10,8},{12,... | collective-permute-start | bytes 393224 | tf_op jit(solution)/shard_map/ppermute | solution.py:486
  27.4 24.3 %collective-permute-start.10 = (bf16[4,32,2048]{2,1,0:T(8,128)(2,1)}, bf16[4,32,2048]{2,1,0:T(8,128)(2,1)}, u32[]{:S(2)}, u32[]{:S(2)}) collective-permute-start(bf16[4,32,2048]{2,1,0:T(8,128)(2,1)} %join_row.2.refs_0_), channel_id=1, source_target_pairs={{0,1},{1,0},{2,3},{3,2},{4,5},{5,4},{6,7},{7,6},{8,9},{9,8},{10,11... | collective-permute-start | bytes 1572872 | tf_op jit(solution)/shard_map/ppermute | solution.py:482
  28.0 23.7 %collective-permute-start.6 = (bf16[4,32,2048]{2,1,0:T(8,128)(2,1)}, bf16[4,32,2048]{2,1,0:T(8,128)(2,1)}, u32[]{:S(2)}, u32[]{:S(2)}) collective-permute-start(bf16[4,32,2048]{2,1,0:T(8,128)(2,1)} %join_row.2.refs_0_), channel_id=1, source_target_pairs={{0,24},{8,0},{16,8},{24,16},{1,25},{9,1},{17,9},{25,17},{2,26},{10... | collective-permute-start | bytes 1572872 | tf_op jit(solution)/shard_map/ppermute | solution.py:486
  30.5 21.3 %collective-permute-start.5 = (bf16[4,32,2048]{2,1,0:T(8,128)(2,1)}, bf16[4,32,2048]{2,1,0:T(8,128)(2,1)}, u32[]{:S(2)}, u32[]{:S(2)}) collective-permute-start(bf16[4,32,2048]{2,1,0:T(8,128)(2,1)} %join_row.2.refs_0_), channel_id=1, source_target_pairs={{0,8},{8,16},{16,24},{24,0},{1,9},{9,17},{17,25},{25,1},{2,10},{10... | collective-permute-start | bytes 1572872 | tf_op jit(solution)/shard_map/ppermute | solution.py:486
  30.5 10.1 %collective-permute-start.9 = (bf16[32,2048]{1,0:T(8,128)(2,1)}, bf16[32,2048]{1,0:T(8,128)(2,1)S(1)}, u32[]{:S(2)}, u32[]{:S(2)}) collective-permute-start(bf16[32,2048]{1,0:T(8,128)(2,1)} %collective-permute-done.1.own_ref), channel_id=1, source_target_pairs={{0,6},{2,0},{4,2},{6,4},{1,7},{3,1},{5,3},{7,5},{8,14},{10,8},{12,... | collective-permute-start | bytes 393224 | tf_op jit(solution)/shard_map/ppermute | solution.py:486
  32.3 19.4 %all-to-all-start.1 = ((bf16[32,32,128]{2,1,0:T(8,128)(2,1)}), bf16[32,32,128]{2,1,0:T(8,128)(2,1)S(1)}, u32[]{:S(2)}, u32[]{:S(2)}) async-start(bf16[32,32,128]{2,1,0:T(8,128)(2,1)} %strict_prefix.1), calls=%async_computation.1 | async-start | bytes 524288 | tf_op jit(solution)/shard_map/all_to_all | solution.py:519
  37.6 9.4 %collective-permute-start.8 = (bf16[32,2048]{1,0:T(8,128)(2,1)}, bf16[32,2048]{1,0:T(8,128)(2,1)S(1)}, u32[]{:S(2)}, u32[]{:S(2)}) collective-permute-start(bf16[32,2048]{1,0:T(8,128)(2,1)} %collective-permute-done.1.own_ref), channel_id=1, source_target_pairs={{0,4},{2,6},{4,0},{6,2},{1,5},{3,7},{5,1},{7,3},{8,12},{10,14},{12... | collective-permute-start | bytes 393224 | tf_op jit(solution)/shard_map/ppermute | solution.py:486
  40.6 9.4 %collective-permute-start.7 = (bf16[32,2048]{1,0:T(8,128)(2,1)}, bf16[32,2048]{1,0:T(8,128)(2,1)S(1)}, u32[]{:S(2)}, u32[]{:S(2)}) collective-permute-start(bf16[32,2048]{1,0:T(8,128)(2,1)} %collective-permute-done.1.own_ref), channel_id=1, source_target_pairs={{0,2},{2,4},{4,6},{6,0},{1,3},{3,5},{5,7},{7,1},{8,10},{10,12},{12... | collective-permute-start | bytes 393224 | tf_op jit(solution)/shard_map/ppermute | solution.py:486
  54.3 3.1 %collective-permute-start.11 = (bf16[512,1024]{1,0:T(8,128)(2,1)S(1)}, bf16[512,1024]{1,0:T(8,128)(2,1)S(1)}, u32[]{:S(2)}, u32[]{:S(2)}) collective-permute-start(bf16[512,1024]{1,0:T(8,128)(2,1)S(1)} %attended.1.a_ref), channel_id=1, source_target_pairs={{0,1},{1,0},{2,3},{3,2},{4,5},{5,4},{6,7},{7,6},{8,9},{9,8},{10,11... | collective-permute-start | bytes 3145736 | tf_op jit(solution)/shard_map/ppermute | solution.py:482
  62.4 37.2 %all-to-all-start.2 = ((bf16[16,64,1024]{2,1,0:T(8,128)(2,1)}), bf16[16,64,1024]{2,1,0:T(8,128)(2,1)}, u32[]{:S(2)}, u32[]{:S(2)}) async-start(bf16[16,64,1024]{2,1,0:T(8,128)(2,1)} %bitcast.33), calls=%async_computation.2 | async-start | bytes 4194304 | tf_op jit(solution)/shard_map/all_to_all | solution.py:527
  67.7 3.1 %collective-permute-start.14 = (bf16[4,32,2048]{2,1,0:T(8,128)(2,1)}, bf16[4,32,2048]{2,1,0:T(8,128)(2,1)S(1)}, u32[]{:S(2)}, u32[]{:S(2)}) collective-permute-start(bf16[4,32,2048]{2,1,0:T(8,128)(2,1)} %collective-permute-done.6.refs_3_), channel_id=1, source_target_pairs={{0,1},{1,0},{2,3},{3,2},{4,5},{5,4},{6,7},{7,6},{8,9},{9,8},{10,11... | collective-permute-start | bytes 1572872 | tf_op jit(solution)/shard_map/ppermute | solution.py:482
  83.4 18.6 %collective-permute-start.18 = (bf16[512,128]{1,0:T(8,128)(2,1)S(1)}, bf16[512,128]{1,0:T(8,128)(2,1)S(1)}, u32[]{:S(2)}, u32[]{:S(2)}) collective-permute-start(bf16[512,128]{1,0:T(8,128)(2,1)S(1)} %chip_states.1.chip_ref), channel_id=1, source_target_pairs={{0,2},{2,4},{4,6},{6,0},{1,3},{3,5},{5,7},{7,1},{8,10},{10,12},{12... | collective-permute-start | bytes 393224 | tf_op jit(solution)/shard_map/ppermute | solution.py:486
  85.1 18.7 %collective-permute-start.17 = (bf16[512,128]{1,0:T(8,128)(2,1)S(1)}, bf16[512,128]{1,0:T(8,128)(2,1)S(1)}, u32[]{:S(2)}, u32[]{:S(2)}) collective-permute-start(bf16[512,128]{1,0:T(8,128)(2,1)S(1)} %chip_states.1.chip_ref), channel_id=1, source_target_pairs={{0,4},{2,6},{4,0},{6,2},{1,5},{3,7},{5,1},{7,3},{8,12},{10,14},{12... | collective-permute-start | bytes 393224 | tf_op jit(solution)/shard_map/ppermute | solution.py:486
  87.5 16.3 %collective-permute-start.16 = (bf16[512,128]{1,0:T(8,128)(2,1)S(1)}, bf16[512,128]{1,0:T(8,128)(2,1)S(1)}, u32[]{:S(2)}, u32[]{:S(2)}) collective-permute-start(bf16[512,128]{1,0:T(8,128)(2,1)S(1)} %chip_states.1.chip_ref), channel_id=1, source_target_pairs={{0,6},{2,0},{4,2},{6,4},{1,7},{3,1},{5,3},{7,5},{8,14},{10,8},{12,... | collective-permute-start | bytes 393224 | tf_op jit(solution)/shard_map/ppermute | solution.py:486
  104.5 19.1 %all-to-all-start.3 = ((bf16[16,32,128]{2,1,0:T(8,128)(2,1)}), bf16[16,32,128]{2,1,0:T(8,128)(2,1)S(1)}, u32[]{:S(2)}, u32[]{:S(2)}) async-start(bf16[16,32,128]{2,1,0:T(8,128)(2,1)} %bitcast.34), calls=%async_computation.3 | async-start | bytes 262144 | tf_op jit(solution)/shard_map/all_to_all | solution.py:545
  114.4 13.2 %collective-permute-start.21 = (bf16[512,128]{1,0:T(8,128)(2,1)S(1)}, bf16[512,128]{1,0:T(8,128)(2,1)S(1)}, u32[]{:S(2)}, u32[]{:S(2)}) collective-permute-start(bf16[512,128]{1,0:T(8,128)(2,1)S(1)} %get-tuple-element.55), channel_id=1, source_target_pairs={{0,8},{8,16},{16,24},{24,0},{1,9},{9,17},{17,25},{25,1},{2,10},{10... | collective-permute-start | bytes 393224 | tf_op jit(solution)/shard_map/ppermute | solution.py:486
  114.5 13.1 %collective-permute-start.20 = (bf16[512,128]{1,0:T(8,128)(2,1)S(1)}, bf16[512,128]{1,0:T(8,128)(2,1)S(1)}, u32[]{:S(2)}, u32[]{:S(2)}) collective-permute-start(bf16[512,128]{1,0:T(8,128)(2,1)S(1)} %get-tuple-element.55), channel_id=1, source_target_pairs={{0,16},{8,24},{16,0},{24,8},{1,17},{9,25},{17,1},{25,9},{2,18},{10... | collective-permute-start | bytes 393224 | tf_op jit(solution)/shard_map/ppermute | solution.py:486
  117.1 10.5 %collective-permute-start.19 = (bf16[512,128]{1,0:T(8,128)(2,1)S(1)}, bf16[512,128]{1,0:T(8,128)(2,1)S(1)}, u32[]{:S(2)}, u32[]{:S(2)}) collective-permute-start(bf16[512,128]{1,0:T(8,128)(2,1)S(1)} %get-tuple-element.55), channel_id=1, source_target_pairs={{0,24},{8,0},{16,8},{24,16},{1,25},{9,1},{17,9},{25,17},{2,26},{10... | collective-permute-start | bytes 393224 | tf_op jit(solution)/shard_map/ppermute | solution.py:486
  124.2 12.2 %all-to-all-start.4 = ((bf16[8,2,32,128]{3,2,1,0:T(8,128)(2,1)}), bf16[8,2,32,128]{3,2,1,0:T(8,128)(2,1)S(1)}, u32[]{:S(2)}, u32[]{:S(2)}) async-start(bf16[8,2,32,128]{3,2,1,0:T(8,128)(2,1)} %sum_groups.1), calls=%async_computation.4 | async-start | bytes 262144 | tf_op jit(solution)/shard_map/all_to_all | solution.py:550
  (16 other events, 203.4 us)
